TPU v7x, 256 devices: a whole 4x4x8 slice. The times are simulated.
256 devices in a mesh: ctx: 64 (over y, x, z_hi), ch: 2 (over core), fsdp: 2 (over z_lo).
Axes of the slice: x: 4, y: 4, z: 8 (z_hi: 4, z_lo: 2; z = z_hi * 2 + z_lo), core: 2. Of those that a mesh axis runs over, the one named last changes fastest.
Arguments:
- query_rows: bfloat16 [16384, 8192], P(('ctx', 'fsdp'), 'ch'), may hold values from -6 to 6
- key_rows: bfloat16 [16384, 8192], P(('ctx', 'fsdp'), 'ch'), may hold values from -6 to 6
- value_rows: bfloat16 [16384, 8192], P(('ctx', 'fsdp'), 'ch'), may hold values from -6 to 6
- upstream: bfloat16 [16384, 8192], P(('ctx', 'fsdp'), 'ch'), may hold values from -6 to 6
- decay_rate: float32 [8, 512], P(None, 'fsdp'), may hold values from 0.1 to 341
- residue: float32 [8, 512], P(None, 'fsdp'), may hold values from -4 to 4
Outputs:
- grad_query: bfloat16 [16384, 8192], P(('ctx', 'fsdp'), 'ch')
- grad_key: bfloat16 [16384, 8192], P(('ctx', 'fsdp'), 'ch')
- grad_value: bfloat16 [16384, 8192], P(('ctx', 'fsdp'), 'ch')
- residue_grad: float32 [8, 512], P(None, 'fsdp')
All inputs are finite; a program needn't handle non-finite values.
Results may differ from a plain program's by a relative error of at most 0.0017.
Values sent between devices are 32-bit elements; how exact they have to be, the bound alone decides.
No kernel may reach another device: no remote copies, remote signals or barrier semaphores. Data moves between devices by JAX's collectives and lax.ppermute only.
A program may use at most 128 MiB of HBM per device.

v0:
```python
import math

import jax
import jax.numpy as jnp
from jax import lax
from jax.sharding import PartitionSpec as P


def carried_in(part, axis, combine, identity, reverse):
    count = lax.axis_size(axis)
    place = lax.axis_index(axis)
    ahead = count - 1 - place if reverse else place
    gathered = jax.tree.map(lambda a: lax.all_gather(a, axis), part)
    state = jax.tree.map(lambda a, e: jnp.zeros_like(a) + jnp.asarray(e, a.dtype), part, identity)

    def one(lap, state):
        source = count - 1 - lap if reverse else lap
        return combine(
            state, jax.tree.map(lambda a: lax.dynamic_index_in_dim(a, source, 0, False), gathered)
        )

    return lax.fori_loop(0, ahead, one, state)


def to_blocks(matrix, block_count, width):
    return matrix.reshape(matrix.shape[0], block_count, width).transpose(1, 0, 2)


def from_blocks(blocked):
    return blocked.transpose(1, 0, 2).reshape(blocked.shape[1], -1)


def local(query_rows, key_rows, value_rows, upstream, decay_rate, residue):
    rates, residues = (
        lax.all_gather(decay_rate, "fsdp", axis=1, tiled=True),
        lax.all_gather(residue, "fsdp", axis=1, tiled=True),
    )
    row_count = query_rows.shape[0]
    local_width = query_rows.shape[1]
    width = rates.shape[1]
    modes = rates.shape[0]
    block_count = local_width // width
    tokens = row_count * lax.axis_size("ctx") * lax.axis_size("fsdp")
    log_decay = rates / tokens
    mode_gain = jnp.sqrt((1.0 + rates) / tokens)
    weight = residues * mode_gain
    positions = jnp.arange(row_count, dtype=jnp.float32)[:, None, None]
    blocks = tuple(
        (
            to_blocks(matrix, block_count, width)
            for matrix in (query_rows, key_rows, value_rows, upstream)
        )
    )
    span = min(row_count, 128)
    steps_in = jnp.arange(span, dtype=jnp.float32)[:, None, None]
    rising = jnp.exp(log_decay * steps_in)
    falling = jnp.exp(-log_decay * steps_in)
    index_row = jnp.arange(span)[:, None]
    index_col = jnp.arange(span)[None, :]
    lower_ones = (index_row >= index_col).astype(jnp.float32)
    upper_ones = (index_row <= index_col).astype(jnp.float32)
    enter_next = jnp.exp(-log_decay * (steps_in + 1.0))
    enter_prior = jnp.exp(-log_decay * (span - steps_in))

    def summarize(block):
        query_part, key_part, value_part, grad_part = block
        product = key_part.astype(jnp.float32) * value_part.astype(jnp.float32)
        gated = grad_part.astype(jnp.float32) * query_part.astype(jnp.float32)
        tail = jnp.exp(-log_decay * (row_count - 1.0 - positions))
        head = jnp.exp(-log_decay * positions)
        return (
            jnp.sum(tail * product[:, None, :], axis=0),
            jnp.sum(head * gated[:, None, :], axis=0),
        )

    ahead, behind = lax.map(summarize, blocks)

    def combine(earlier, later):
        return (earlier[0] + later[0], later[1] + jnp.exp(-log_decay * later[0][0]) * earlier[1])

    identity = (jnp.zeros((1,), jnp.float32), jnp.zeros_like(ahead))
    single = jnp.full((1,), float(row_count), jnp.float32)
    carry_ahead = carried_in((single, ahead), ("ctx", "fsdp"), combine, identity, False)[1]
    carry_behind = carried_in((single, behind), ("ctx", "fsdp"), combine, identity, True)[1]

    def running(ones, scaled):
        flat = scaled.reshape(span, -1)
        summed = jnp.dot(
            ones, flat, precision=lax.Precision.HIGHEST, preferred_element_type=jnp.float32
        )
        return summed.reshape(span, modes, width)

    def finish(block):
        query_part, key_part, value_part, grad_part, enter_ahead, enter_behind = block
        product = key_part.astype(jnp.float32) * value_part.astype(jnp.float32)
        gated = grad_part.astype(jnp.float32) * query_part.astype(jnp.float32)
        state = enter_ahead
        terms = jnp.zeros((modes, width), jnp.float32)
        states = falling * running(lower_ones, rising * product[:, None, :]) + enter_next * state
        conv_parts = [jnp.sum(weight * states, axis=1)]
        terms = terms + jnp.sum(gated[:, None, :] * states, axis=0)
        state = enter_behind
        flow_parts = []
        states = rising * running(upper_ones, falling * gated[:, None, :]) + enter_prior * state
        flow_parts.insert(0, jnp.sum(weight * states, axis=1))
        conv = jnp.concatenate(conv_parts, axis=0)
        flowing = jnp.concatenate(flow_parts, axis=0)
        grad_q = (grad_part.astype(jnp.float32) * conv).astype(jnp.bfloat16)
        grad_k = (flowing * value_part.astype(jnp.float32)).astype(jnp.bfloat16)
        grad_v = (flowing * key_part.astype(jnp.float32)).astype(jnp.bfloat16)
        return (grad_q, grad_k, grad_v, terms)

    query_grads, key_grads, value_grads, all_terms = lax.map(
        finish, blocks + (carry_ahead, carry_behind)
    )
    partial_grad = mode_gain * jnp.sum(all_terms, axis=0) / math.sqrt(tokens)
    summed = lax.psum(partial_grad, ("ctx", "ch"))
    residue_grad = lax.psum_scatter(summed, "fsdp", scatter_dimension=1, tiled=True)
    return (
        from_blocks(query_grads),
        from_blocks(key_grads),
        from_blocks(value_grads),
        residue_grad,
    )


def solution(mesh):
    placed = (
        P(("ctx", "fsdp"), "ch"),
        P(("ctx", "fsdp"), "ch"),
        P(("ctx", "fsdp"), "ch"),
        P(("ctx", "fsdp"), "ch"),
        P(None, "fsdp"),
        P(None, "fsdp"),
    )
    return jax.shard_map(
        local,
        mesh=mesh,
        in_specs=placed,
        out_specs=(
            P(("ctx", "fsdp"), "ch"),
            P(("ctx", "fsdp"), "ch"),
            P(("ctx", "fsdp"), "ch"),
            P(None, "fsdp"),
        ),
        check_vma=False,
    )
```

profile of v0, /device:TPU:1, one launch (start us, length us, event | category | flops | bytes accessed | tf_op | source)
XLA Modules:
  0.0 1254.4 jit_solution(2737631735284426398)
XLA Ops:
  7.2 4.6 all_gather.23
  11.8 3.4 all_gather.22
  22.5 36.9 %while.64 = (s32[]{:T(128)}, f32[8,8,512]{2,1,0:T(8,128)}, f32[8,8,512]{2,1,0:T(8,128)}, f32[1,8,512]{2,1,0:T(8,128)}, bf16[8,128,512]{1,2,0:T(8,128)(2,1)S(1)},...) while((s32[]{:T(128)}, f32[8,8,512]{2,1,0:T(8,128)}, ...), condition=%wide.region_3.4_spmd.clone.clone, body=%wide.region_0.3_spmd.clone.clone.sunk | while | flops 3530882 | bytes 3786349 | solution.py:76
  62.2 301.8 %all-reduce = f32[128]{0:T(128)S(1)} all-reduce(f32[128]{0:T(128)S(1)} %dynamic-update-slice), channel_id=1, replica_groups=mesh['ctx'=64,'ch'=2,'fsdp'=2] {'ctx','fsdp'}, use_global_device_ids=true, to_apply=%add | all-reduce | flops 128 | bytes 1024
  364.1 375.5 %while.63 = (s32[]{:T(128)}, f32[8,8,512]{2,1,0:T(8,128)S(1)}, s32[]{:T(128)}, f32[128,8,8,512]{3,2,1,0:T(8,128)}, f32[128,1]{0,1:T(1,128)S(1)}, /*index=5*/f32[...) while((s32[]{:T(128)}, f32[8,8,512]{2,1,0:T(8,128)S(1)}, s32[]{:T(128)}, ...), condition=%wide.region_7.8_spmd, body=%wide.region_6.7_spmd.sunk | while | flops 69638 | bytes 442535 | solution.py:22
  740.4 94.5 %while.65 = (s32[]{:T(128)}, bf16[8,128,512]{1,2,0:T(8,128)(2,1)}, bf16[8,128,512]{1,2,0:T(8,128)(2,1)}, bf16[8,128,512]{1,2,0:T(8,128)(2,1)}, f32[8,8,512]{2,1,...) while((s32[]{:T(128)}, bf16[8,128,512]{1,2,0:T(8,128)(2,1)}, ...), condition=%wide.region_12.13_spmd.clone.clone, body=%wide.region_8.12_spmd.clone.clone.sunk | while | flops 1624109056 | bytes 28904616 | solution.py:113
  742.6 2.3 fusion.58
  744.9 1.8 fusion.59
  746.7 3.4 fusion.60
  754.4 2.3 fusion.58
  756.7 1.8 fusion.59
  758.5 3.4 fusion.60
  766.2 2.3 fusion.58
  768.5 1.8 fusion.59
  770.3 3.4 fusion.60
  778.0 2.2 fusion.58
  780.3 1.8 fusion.59
  782.1 3.4 fusion.60
  789.8 2.2 fusion.58
  792.1 1.8 fusion.59
  793.9 3.4 fusion.60
  801.6 2.2 fusion.58
  805.7 3.4 fusion.60
  813.4 2.3 fusion.58
  815.7 1.8 fusion.59
  817.5 3.4 fusion.60
  825.2 2.3 fusion.58
  827.5 1.8 fusion.59
  829.3 3.4 fusion.60
  836.5 2.4 copy.43
  841.5 58.0 %reduce-scatter.2.cloned.1.call-done = f32[8,256]{1,0:T(8,128)} async-done(((f32[8,512]{1,0:T(8,128)}), f32[8,256]{1,0:T(8,128)}) %reduce-scatter.2.cloned.1.call-update) | async-done | bytes 8208 | tf_op jit(solution)/shard_map/reduce_scatter | solution.py:118
  899.4 348.4 %psum.8 = f32[8,256]{1,0:T(8,128)} all-reduce(f32[8,256]{1,0:T(8,128)} %reduce-scatter.2.cloned.1.call-done), channel_id=1, replica_groups=mesh['ctx'=64,'ch'=2,'fsdp'=2] {'ctx','ch'}, use_global_device_ids=true, to_apply=%region_14.15 | all-reduce | flops 2048 | bytes 16384 | tf_op jit(solution)/shard_map/psum | solution.py:117
  (612 shorter events, 459.3 us)
Async XLA Ops:
  7.2 9.8 copy-start.1
  7.2 356.9 %all-gather.7.cloned.1.call-start = ((), (), s32[]{:S(2)}) async-start(), calls=%async_computation.2 | async-start | bytes 16908288 | tf_op jit(solution)/shard_map/all_gather | solution.py:13
  11.8 8.7 copy-start.6
  15.2 3.0 copy-start.2
  59.5 680.2 %all-gather.5.cloned.1.call-start = ((), (), s32[]{:S(2)}) async-start(), calls=%async_computation.1 | async-start | bytes 16908288 | tf_op jit(solution)/shard_map/all_gather | solution.py:13
  60.2 839.2 %reduce-scatter.2.cloned.1.call-start = ((), (), s32[]{:S(2)}) async-start(), calls=%async_computation.3 | async-start | bytes 24576 | tf_op jit(solution)/shard_map/reduce_scatter | solution.py:118
  364.1 376.3 %copy-start = (f32[8,512]{1,0:T(8,128)S(1)}, f32[8,512]{1,0:T(8,128)}, u32[]{:S(2)}) copy-start(f32[8,512]{1,0:T(8,128)} %get-tuple-element.1009) | copy-start | bytes 49156
  364.1 376.3 %copy-start.5 = (f32[8,512]{1,0:T(8,128)S(1)}, f32[8,512]{1,0:T(8,128)}, u32[]{:S(2)}) copy-start(f32[8,512]{1,0:T(8,128)} %get-tuple-element.1003) | copy-start | bytes 49156
  740.4 95.5 %copy-start.7 = (f32[8,512]{1,0:T(8,128)S(1)}, f32[8,512]{1,0:T(8,128)}, u32[]{:S(2)}) copy-start(f32[8,512]{1,0:T(8,128)} %copy-done.6) | copy-start | bytes 49156
  834.8 4.0 copy-start.3
  836.5 3.7 copy-start.4
Sparse Core Ops, SparseCore 0:
  59.6 155.9 all-gather.6
  219.2 147.7 all-gather.4
  836.6 62.7 reduce-scatter.1
where the time goes:
time: 1270 us; the launch traced here: 1250 us
  blocking collectives  658 us (52%)
  other arithmetic  373 us (29%)
  local copies, waits for them, and re-layouts  113 us (9%)
  waiting for transfers between devices  58.7 us (5%)
  matrix products  32.5 us (3%)
  between operations  13.9 us (1%)
    psum x1, blocking collectives, local(): summed = lax.psum(partial_grad, ('ctx', 'ch'))  348 us
    unnamed x1, blocking collectives  302 us
    exp x127, other arithmetic, combine(): jnp.exp(-log_decay * later[0][0]) * earlier[1]  173 us
    add x127, other arithmetic, combine(): later[1] + jnp.exp(-log_decay * later[0][0]) * earlier[1]  122 us
    dynamic_slice x127, local copies, waits for them, and re-layouts, one(): lax.dynamic_index_in_dim(a, source, 0, False)  77.7 us
    reduce_scatter x1, waiting for transfers between devices, local(): lax.psum_scatter(summed, 'fsdp', scatter_dimension=1, tiled=True)  58 us
    dot_general x16, matrix products, running(): jnp.dot(ones, flat, precision=lax.Precision.HIGHEST, preferred_element_ty...  32.5 us
    reduce_sum x8, other arithmetic, finish(): flow_parts.insert(0, jnp.sum(weight * states, axis=1))  27.3 us
  transfers between devices with their start and end apart: 3, of which 1 were waited for; matrix products, arithmetic and copies ran while one was open for 30% of the time, Pallas kernels for 0%

commit v1 on v0

v1 whole, which is shorter than its diff:
```python
import functools
import math

import jax
import jax.numpy as jnp
from jax import lax
from jax.experimental import pallas as pl
from jax.experimental.pallas import tpu as pltpu
from jax.sharding import PartitionSpec as P

TOKENS = 16384
ROWS = 128
MODES = 8
FILTERS = 512
BLOCKS = 8
SUB = 8
RUN = ROWS // SUB
LANES = 128
STRIPS = FILTERS // LANES
PAIRS = BLOCKS // 2
WIDTH = BLOCKS * FILTERS
SHARDS = TOKENS // ROWS
ALL = ("ctx", "fsdp")
f32 = jnp.float32


def sublane():
    return lax.broadcasted_iota(jnp.int32, (SUB, LANES), 0)


def rows_of(ref, j):
    return ref[pl.ds(j, SUB, stride=RUN), :]


def owner(n, pair, strip):
    return (n * PAIRS + pair) * STRIPS + strip


def summarize_kernel(rate_ref, q_ref, k_ref, v_ref, u_ref, send_ref, cf_ref, cb_ref, tab, ps, gs):
    blk = pl.program_id(0)
    s = sublane()

    @pl.when(blk == 0)
    def _():
        def make(i, _):
            strip, n = i // MODES, i % MODES
            log_decay = jnp.broadcast_to(rate_ref[pl.ds(n * STRIPS + strip, 1), :], (SUB, LANES)) / TOKENS
            tab[0, i] = jnp.exp(-log_decay)
            for step in range(3):
                hop = 1 << step
                factor = jnp.exp(-log_decay * (RUN * hop))
                tab[1 + step, i] = jnp.where(s >= hop, factor, 0.0)
                tab[4 + step, i] = jnp.where(s < SUB - hop, factor, 0.0)
            return 0

        lax.fori_loop(0, STRIPS * MODES, make, 0)

    pair, odd = blk // 2, blk % 2

    def strip_body(strip, _):
        cols = pl.ds(pl.multiple_of(strip * LANES, LANES), LANES)
        ps[...] = k_ref[:, cols].astype(f32) * v_ref[:, cols].astype(f32)
        gs[...] = u_ref[:, cols].astype(f32) * q_ref[:, cols].astype(f32)
        base = strip * MODES
        decay = [tab[0, base + n] for n in range(MODES)]
        behind = [None] * MODES
        for j in reversed(range(RUN)):
            gated = rows_of(gs, j)
            for n in range(MODES):
                behind[n] = gated if j == RUN - 1 else decay[n] * behind[n] + gated
        ahead, terms = [None] * MODES, [None] * MODES
        for j in range(RUN):
            product, gated = rows_of(ps, j), rows_of(gs, j)
            for n in range(MODES):
                if j == 0:
                    ahead[n] = product
                    terms[n] = gated * product
                else:
                    ahead[n] = decay[n] * ahead[n] + product
                    terms[n] = terms[n] + gated * ahead[n]
        for n in range(MODES):
            place = owner(n, pair, strip)
            total = ahead[n]
            for step in range(3):
                total = total + tab[1 + step, base + n] * pltpu.roll(total, 1 << step, 0)
            send_ref[place, pl.ds(odd, 1), :] = total[SUB - 1 :, :]
            enter = jnp.where(s >= 1, pltpu.roll(total, 1, 0), 0.0)
            cf_ref[n, :, cols] = enter
            term = jnp.sum(terms[n] + decay[n] * behind[n] * enter, axis=0, keepdims=True)
            total = behind[n]
            for step in range(3):
                total = total + tab[4 + step, base + n] * pltpu.roll(total, SUB - (1 << step), 0)
            send_ref[place, pl.ds(2 + odd, 1), :] = total[:1, :]
            cb_ref[n, :, cols] = jnp.where(s < SUB - 1, pltpu.roll(total, SUB - 1, 0), 0.0)

            @pl.when(odd == 0)
            def _():
                send_ref[place, 4:5, :] = term
                send_ref[place, 5:8, :] = jnp.zeros((3, LANES), f32)

            @pl.when(odd == 1)
            def _():
                send_ref[place, 4:5, :] = send_ref[place, 4:5, :] + term

        return 0

    lax.fori_loop(0, STRIPS, strip_body, 0)


def carry_kernel(where_ref, rate_ref, x_ref, y_ref, cross_ref):
    place = where_ref[0]
    n, strip = place // (PAIRS * STRIPS), place % STRIPS
    log_decay = jnp.broadcast_to(rate_ref[pl.ds(n * STRIPS + strip, 1), :], (SUB, LANES)) / TOKENS
    across = jnp.exp(-log_decay * ROWS)
    s = sublane()
    zero = jnp.zeros((SUB, LANES), f32)

    def up(i, state_cross):
        state, cross, terms = state_cross
        x = x_ref[i]
        y_ref[i] = state
        cross = cross + pltpu.roll(x, SUB - 2, 0) * state
        return across * state + x, cross, terms + x

    _, cross, terms = lax.fori_loop(0, SHARDS, up, (zero, zero, zero), unroll=8)
    cross_row = cross[0:1, :] + cross[1:2, :]
    row = jnp.exp(-log_decay[0:1, :]) * cross_row + terms[4:5, :]
    row = jnp.broadcast_to(row, (SUB, LANES))

    def down(i, state):
        at = SHARDS - 1 - i
        y_ref[at] = jnp.where(s < 2, y_ref[at], jnp.where(s < 4, state, row))
        return across * state + x_ref[at]

    lax.fori_loop(0, SHARDS, down, zero, unroll=8)


def finish_kernel(
    rate_ref, residue_ref, q_ref, k_ref, v_ref, u_ref, cf_ref, cb_ref, in_ref,
    gq_ref, gk_ref, gv_ref, tab, ps, gs, cs, fs,
):
    blk = pl.program_id(0)
    s = sublane()

    @pl.when(blk == 0)
    def _():
        def make(i, _):
            strip, n = i // MODES, i % MODES
            at = pl.ds(n * STRIPS + strip, 1)
            rate = jnp.broadcast_to(rate_ref[at, :], (SUB, LANES))
            log_decay = rate / TOKENS
            gain = jnp.sqrt((1.0 + rate) / TOKENS)
            tab[0, i] = jnp.exp(-log_decay)
            tab[1, i] = jnp.broadcast_to(residue_ref[at, :], (SUB, LANES)) * gain
            tab[2, i] = jnp.exp(-log_decay * (RUN * s).astype(f32))
            tab[3, i] = jnp.exp(-log_decay * (RUN * (SUB - 1 - s)).astype(f32))
            return 0

        lax.fori_loop(0, STRIPS * MODES, make, 0)

    pair, odd = blk // 2, blk % 2

    def strip_body(strip, _):
        cols = pl.ds(pl.multiple_of(strip * LANES, LANES), LANES)
        key, value = k_ref[:, cols].astype(f32), v_ref[:, cols].astype(f32)
        grad = u_ref[:, cols].astype(f32)
        ps[...] = key * value
        gs[...] = grad * q_ref[:, cols].astype(f32)
        base = strip * MODES
        decay = [tab[0, base + n] for n in range(MODES)]
        weight = [tab[1, base + n] for n in range(MODES)]

        def weighted(states):
            parts = [weight[n] * states[n] for n in range(MODES)]
            while len(parts) > 1:
                parts = [a + b for a, b in zip(parts[::2], parts[1::2])]
            return parts[0]

        state = []
        for n in range(MODES):
            carry = in_ref[owner(n, pair, strip), pl.ds(odd, 1), :]
            state.append(cf_ref[n, :, cols] + tab[2, base + n] * carry)
        for j in range(RUN):
            product = rows_of(ps, j)
            state = [decay[n] * state[n] + product for n in range(MODES)]
            cs[pl.ds(j, SUB, stride=RUN), :] = weighted(state)
        state = []
        for n in range(MODES):
            carry = in_ref[owner(n, pair, strip), pl.ds(2 + odd, 1), :]
            state.append(cb_ref[n, :, cols] + tab[3, base + n] * carry)
        for j in reversed(range(RUN)):
            gated = rows_of(gs, j)
            state = [decay[n] * state[n] + gated for n in range(MODES)]
            fs[pl.ds(j, SUB, stride=RUN), :] = weighted(state)
        flowing = fs[...]
        gq_ref[:, cols] = (grad * cs[...]).astype(jnp.bfloat16)
        gk_ref[:, cols] = (flowing * value).astype(jnp.bfloat16)
        gv_ref[:, cols] = (flowing * key).astype(jnp.bfloat16)
        return 0

    lax.fori_loop(0, STRIPS, strip_body, 0)


def whole(shape):
    return pl.BlockSpec(shape, lambda *_: (0,) * len(shape))


def local(query_rows, key_rows, value_rows, upstream, decay_rate, residue):
    half = lax.axis_index("fsdp")
    mine = jnp.concatenate([decay_rate, residue], axis=0)
    other = lax.ppermute(mine, "fsdp", [(0, 1), (1, 0)])
    both = jnp.where(
        half == 0, jnp.concatenate([mine, other], 1), jnp.concatenate([other, mine], 1)
    )
    rates, residues = both.reshape(2, MODES * STRIPS, LANES)
    bf16 = jnp.bfloat16
    wide = pl.BlockSpec((ROWS, FILTERS), lambda b: (0, b))
    states = pl.BlockSpec((MODES, SUB, FILTERS), lambda b: (0, 0, b))
    params = whole((MODES * STRIPS, LANES))
    packet = (SHARDS, SUB, LANES)
    packet_shape = jax.ShapeDtypeStruct(packet, f32)
    state_shape = jax.ShapeDtypeStruct((MODES, SUB, WIDTH), f32)
    table = (STRIPS * MODES, SUB, LANES)
    send, enter_ahead, enter_behind = pl.pallas_call(
        summarize_kernel,
        grid=(BLOCKS,),
        in_specs=[params] + [wide] * 4,
        out_specs=[whole(packet), states, states],
        out_shape=[packet_shape, state_shape, state_shape],
        scratch_shapes=[pltpu.VMEM((7,) + table, f32)] + [pltpu.VMEM((ROWS, LANES), f32)] * 2,
        name="summarize",
    )(rates, query_rows, key_rows, value_rows, upstream)
    arrived = lax.all_to_all(send, ALL, 0, 0, tiled=True)
    place = lax.axis_index(ALL).astype(jnp.int32).reshape(1)
    carries = pl.pallas_call(
        carry_kernel,
        in_specs=[pl.BlockSpec(memory_space=pltpu.SMEM)] + [pl.BlockSpec(memory_space=pltpu.VMEM)] * 2,
        out_specs=pl.BlockSpec(memory_space=pltpu.VMEM),
        out_shape=packet_shape,
        scratch_shapes=[pltpu.VMEM((SUB, LANES), f32)],
        name="carry",
    )(place, rates, arrived)
    back = lax.all_to_all(carries, ALL, 0, 0, tiled=True)
    rows = back[:, 4, :].reshape(MODES, PAIRS, FILTERS).sum(axis=1)
    width = FILTERS // 2
    rows = lax.dynamic_slice_in_dim(rows, half * width, width, 1)
    rows = rows + lax.ppermute(rows, "ch", [(0, 1), (1, 0)])
    gain = jnp.sqrt((1.0 + decay_rate) / TOKENS)
    residue_grad = gain * rows / math.sqrt(TOKENS)
    out = jax.ShapeDtypeStruct((ROWS, WIDTH), bf16)
    grads = pl.pallas_call(
        finish_kernel,
        grid=(BLOCKS,),
        in_specs=[params] * 2 + [wide] * 4 + [states] * 2 + [whole(packet)],
        out_specs=[wide] * 3,
        out_shape=[out] * 3,
        scratch_shapes=[pltpu.VMEM((4,) + table, f32)] + [pltpu.VMEM((ROWS, LANES), f32)] * 4,
        name="finish",
    )(rates, residues, query_rows, key_rows, value_rows, upstream, enter_ahead, enter_behind, back)
    return (*grads, residue_grad)


def solution(mesh):
    rows = P(ALL, "ch")
    params = P(None, "fsdp")
    return jax.shard_map(
        local,
        mesh=mesh,
        in_specs=(rows, rows, rows, rows, params, params),
        out_specs=(rows, rows, rows, params),
        check_vma=False,
    )
```

time: 1270 us -> 96.3 us (0.08); the launches traced: 1250 us -> 95.7 us
  blocking collectives: 658 us -> 0 us
  other arithmetic: 373 us -> 0.66 us
  local copies, waits for them, and re-layouts: 113 us -> 2.93 us
  matrix products: 32.5 us -> 0 us
  starting transfers between devices: 0.12 us -> 29.1 us
  Pallas kernels: 0 us -> 26.1 us
  waiting for transfers between devices: 58.7 us -> 36.2 us
  between operations: 13.9 us -> 0.71 us
    psum x1 -> x0, blocking collectives: 348 us -> none  [local(): summed = lax.psum(partial_grad, ('ctx', 'ch'))]
    unnamed x1 -> x0, blocking collectives: 302 us -> none
    exp x135 -> x0, other arithmetic: 177 us -> none  [the longest x127 173 us: combine(): jnp.exp(-log_decay * later[0][0]) * earlier[1]]
    add x127 -> x0, other arithmetic: 122 us -> none  [combine(): later[1] + jnp.exp(-log_decay * later[0][0]) * earlier[1]]
    dynamic_slice x191 -> x1, local copies, waits for them, and re-layouts: 89 us -> 0.01 us  [local(): rows = lax.dynamic_slice_in_dim(rows, half * width, width, 1)]
    reduce_scatter x1 -> x0, waiting for transfers between devices: 58 us -> none  [local(): lax.psum_scatter(summed, 'fsdp', scatter_dimension=1, tiled=True)]
    reduce_sum x17 -> x1, other arithmetic: 42.3 us -> 0.04 us  [local(): rows = back[:, 4, :].reshape(MODES, PAIRS, FILTERS).sum(axis=1)]
    all_to_all x0 -> x2, waiting for transfers between devices: none -> 35.1 us  [the longest x1 18.3 us: local(): arrived = lax.all_to_all(send, ALL, 0, 0, tiled=True)]
  transfers between devices with their start and end apart: 3 -> 4, of which waited for: 1 -> 3; matrix products, arithmetic and copies ran while one was open for 30% -> 1% of each run, Pallas kernels for 0% -> 12%
where the time goes in v1:
time: 96.3 us; the launch traced here: 95.7 us
  waiting for transfers between devices  36.2 us (38%)
  starting transfers between devices  29.1 us (30%)
  Pallas kernels  26.1 us (27%)
  local copies, waits for them, and re-layouts  2.93 us (3%)
    all_to_all x1, waiting for transfers between devices, local(): arrived = lax.all_to_all(send, ALL, 0, 0, tiled=True)  18.3 us
    all_to_all x1, waiting for transfers between devices, local(): back = lax.all_to_all(carries, ALL, 0, 0, tiled=True)  16.8 us
    all_to_all x1, starting transfers between devices, local(): arrived = lax.all_to_all(send, ALL, 0, 0, tiled=True)  15.3 us
    pallas_call x1, Pallas kernels, local(): pl.pallas_call(summarize_kernel, grid=(BLOCKS,), in_specs=[params] + [wid...  12.4 us
    pallas_call x1, Pallas kernels, local(): pl.pallas_call(finish_kernel, grid=(BLOCKS,), in_specs=[params] * 2 + [wi...  11.2 us
    all_to_all x1, starting transfers between devices, local(): back = lax.all_to_all(carries, ALL, 0, 0, tiled=True)  6.39 us
    ppermute x1, starting transfers between devices, local(): rows = rows + lax.ppermute(rows, 'ch', [(0, 1), (1, 0)])  4.89 us
    pallas_call x1, Pallas kernels, local(): pl.pallas_call(carry_kernel, in_specs=[pl.BlockSpec(memory_space=pltpu.SM...  2.54 us
  transfers between devices with their start and end apart: 4, of which 3 were waited for; matrix products, arithmetic and copies ran while one was open for 1% of the time, Pallas kernels for 12%

profile of v1, /device:TPU:1, one launch (start us, length us, event | category | flops | bytes accessed | tf_op | source)
XLA Modules:
  0.0 95.7 jit_solution(10704017997720890798)
XLA Ops:
  0.6 0.0 copy-start.3
  0.6 0.7 constant_dynamic-update-slice_fusion.1
  1.3 0.0 copy-done.3
  1.3 2.5 %collective-permute-start = (f32[16,256]{1,0:T(8,128)S(1)}, f32[16,256]{1,0:T(8,128)S(1)}, u32[]{:S(2)}, u32[]{:S(2)}) collective-permute-start(f32[16,256]{1,0:T(8,128)S(1)} %constant_dynamic-update-slice_fusion), channel_id=1, source_target_pairs={{0,1},{1,0},{2,3},{3,2},{4,5},{5,4},{6,7},{7,6},{8,9},{9,8},{10,11... | collective-permute-start | bytes 49160 | tf_op jit(solution)/shard_map/ppermute | solution.py:211
  3.8 1.1 %collective-permute-done = f32[16,256]{1,0:T(8,128)S(1)} collective-permute-done((f32[16,256]{1,0:T(8,128)S(1)}, f32[16,256]{1,0:T(8,128)S(1)}, u32[]{:S(2)}, u32[]{:S(2)}) %collective-permute-start) | collective-permute-done | bytes 16416 | tf_op jit(solution)/shard_map/ppermute | solution.py:211
  4.9 0.6 unstack.13.rate_ref
  5.6 12.4 %summarize.1 = (f32[128,8,128]{2,1,0:T(8,128)}, f32[8,8,4096]{2,1,0:T(8,128)}, f32[8,8,4096]{2,1,0:T(8,128)}) custom-call(f32[32,128]{1,0:T(8,128)} %unstack.13.rate_ref, bf16[128,4096]{1,0:T(8,128)(2,1)} %q_ref.3, bf16[128,4096]{1,0:T(8,128)(2,1)} %k_ref.3, bf16[128,4096]{1,0:T(8,128)(2,1)} %v_ref.3, bf16[128,4096]{1,0:T(8,128)(2,1)} %u_ref.3), custom_call_target="tpu_custom_call" | custom-call | tf_op jit(solution)/shard_map/summarize/pallas_call | solution.py:224
  17.9 15.3 %all-to-all-start = ((f32[128,8,128]{2,1,0:T(8,128)}), f32[128,8,128]{2,1,0:T(8,128)S(1)}, u32[]{:S(2)}, u32[]{:S(2)}) async-start(f32[128,8,128]{2,1,0:T(8,128)} %get-tuple-element.12), calls=%async_computation | async-start | bytes 1048576 | tf_op jit(solution)/shard_map/all_to_all | solution.py:233
  33.3 18.3 %all-to-all-done.x_ref = f32[128,8,128]{2,1,0:T(8,128)S(1)} async-done(((f32[128,8,128]{2,1,0:T(8,128)}), f32[128,8,128]{2,1,0:T(8,128)S(1)}, u32[]{:S(2)}, u32[]{:S(2)}) %all-to-all-start) | async-done | bytes 524320 | tf_op jit(solution)/shard_map/all_to_all | solution.py:233
  51.5 0.0 copy-start.1
  51.6 0.8 copy-done.1
  52.3 2.5 %carry.1 = f32[128,8,128]{2,1,0:T(8,128)} custom-call(s32[1]{0:T(128)} %bitcast.where_ref, f32[32,128]{1,0:T(8,128)} %unstack.13.rate_ref, f32[128,8,128]{2,1,0:T(8,128)} %copy-done.1), custom_call_target="tpu_custom_call" | custom-call | tf_op jit(solution)/shard_map/carry/pallas_call | solution.py:235
  54.9 6.4 %all-to-all-start.1 = ((f32[128,8,128]{2,1,0:T(8,128)}), f32[128,8,128]{2,1,0:T(8,128)S(1)}, u32[]{:S(2)}, u32[]{:S(2)}) async-start(f32[128,8,128]{2,1,0:T(8,128)} %carry.1), calls=%async_computation.1 | async-start | bytes 1048576 | tf_op jit(solution)/shard_map/all_to_all | solution.py:243
  61.3 16.8 %all-to-all-done.1.in_ref = f32[128,8,128]{2,1,0:T(8,128)S(1)} async-done(((f32[128,8,128]{2,1,0:T(8,128)}), f32[128,8,128]{2,1,0:T(8,128)S(1)}, u32[]{:S(2)}, u32[]{:S(2)}) %all-to-all-start.1) | async-done | bytes 524320 | tf_op jit(solution)/shard_map/all_to_all | solution.py:243
  78.1 0.0 copy-start
  78.1 0.2 slice_reduce_fusion
  78.4 4.9 %collective-permute-start.1 = (f32[8,256]{1,0:T(8,128)S(1)}, f32[8,256]{1,0:T(8,128)S(1)}, u32[]{:S(2)}, u32[]{:S(2)}) collective-permute-start(f32[8,256]{1,0:T(8,128)S(1)} %constant_dynamic-slice_fusion), channel_id=1, source_target_pairs={{0,2},{2,0},{1,3},{3,1},{4,6},{6,4},{5,7},{7,5},{8,10},{10,8},{9,1... | collective-permute-start | bytes 24584 | tf_op jit(solution)/shard_map/ppermute | solution.py:247
  83.3 0.6 unstack.15.residue_ref
  83.9 0.0 copy-done
  83.9 0.0 copy-start.2
  83.9 11.2 %finish.1 = (bf16[128,4096]{1,0:T(8,128)(2,1)}, bf16[128,4096]{1,0:T(8,128)(2,1)}, bf16[128,4096]{1,0:T(8,128)(2,1)}) custom-call(f32[32,128]{1,0:T(8,128)} %unstack.13.rate_ref, f32[32,128]{1,0:T(8,128)} %unstack.15.residue_ref, bf16[128,4096]{1,0:T(8,128)(2,1)} %q_ref.3, bf16[128,4096]{1,0:T(8,128)(2,1)} %k_ref.3, bf16[128,4096]{1,0:T(8,128)(2,1)} %v_ref.3, ...), custom_call_target="tpu_custom_call" | custom-call | tf_op jit(solution)/shard_map/finish/pallas_call | solution.py:251
  95.1 0.0 collective-permute-done.1
  95.1 0.0 copy-done.2
  95.1 0.6 multiply_multiply_fusion
  (6 shorter events, 0.1 us)
Async XLA Ops:
  0.6 0.7 copy-start.3
  1.3 3.6 %collective-permute-start = (f32[16,256]{1,0:T(8,128)S(1)}, f32[16,256]{1,0:T(8,128)S(1)}, u32[]{:S(2)}, u32[]{:S(2)}) collective-permute-start(f32[16,256]{1,0:T(8,128)S(1)} %constant_dynamic-update-slice_fusion), channel_id=1, source_target_pairs={{0,1},{1,0},{2,3},{3,2},{4,5},{5,4},{6,7},{7,6},{8,9},{9,8},{10,11... | collective-permute-start | bytes 49160 | tf_op jit(solution)/shard_map/ppermute | solution.py:211
  17.9 33.6 %all-to-all-start = ((f32[128,8,128]{2,1,0:T(8,128)}), f32[128,8,128]{2,1,0:T(8,128)S(1)}, u32[]{:S(2)}, u32[]{:S(2)}) async-start(f32[128,8,128]{2,1,0:T(8,128)} %get-tuple-element.12), calls=%async_computation | async-start | bytes 1048576 | tf_op jit(solution)/shard_map/all_to_all | solution.py:233
  51.5 0.8 copy-start.1
  54.9 23.2 %all-to-all-start.1 = ((f32[128,8,128]{2,1,0:T(8,128)}), f32[128,8,128]{2,1,0:T(8,128)S(1)}, u32[]{:S(2)}, u32[]{:S(2)}) async-start(f32[128,8,128]{2,1,0:T(8,128)} %carry.1), calls=%async_computation.1 | async-start | bytes 1048576 | tf_op jit(solution)/shard_map/all_to_all | solution.py:243
  78.1 5.8 %copy-start = (f32[128,8,128]{2,1,0:T(8,128)}, f32[128,8,128]{2,1,0:T(8,128)S(1)}, u32[]{:S(2)}) copy-start(f32[128,8,128]{2,1,0:T(8,128)S(1)} %all-to-all-done.1.in_ref) | copy-start | bytes 1572868
  78.4 16.7 %collective-permute-start.1 = (f32[8,256]{1,0:T(8,128)S(1)}, f32[8,256]{1,0:T(8,128)S(1)}, u32[]{:S(2)}, u32[]{:S(2)}) collective-permute-start(f32[8,256]{1,0:T(8,128)S(1)} %constant_dynamic-slice_fusion), channel_id=1, source_target_pairs={{0,2},{2,0},{1,3},{3,1},{4,6},{6,4},{5,7},{7,5},{8,10},{10,8},{9,1... | collective-permute-start | bytes 24584 | tf_op jit(solution)/shard_map/ppermute | solution.py:247
  83.9 11.2 %copy-start.2 = (f32[8,256]{1,0:T(8,128)S(1)}, f32[8,256]{1,0:T(8,128)}, u32[]{:S(2)}) copy-start(f32[8,256]{1,0:T(8,128)} %param.10) | copy-start | bytes 24580

commit v2 on v0

v2 whole, which is shorter than its diff:
```python
import functools
import math

import jax
import jax.numpy as jnp
from jax import lax
from jax.experimental import pallas as pl
from jax.experimental.pallas import tpu as pltpu
from jax.sharding import PartitionSpec as P

TOKENS = 16384
ROWS = 128
MODES = 8
FILTERS = 512
BLOCKS = 8
SUB = 8
RUN = ROWS // SUB
LANES = 128
STRIPS = FILTERS // LANES
PAIRS = BLOCKS // 2
WIDTH = BLOCKS * FILTERS
SHARDS = TOKENS // ROWS
PACKET = 5 * LANES
ALL = ("ctx", "fsdp")
f32 = jnp.float32
bf16 = jnp.bfloat16


def sublane():
    return lax.broadcasted_iota(jnp.int32, (SUB, LANES), 0)


def owner(strip, pair, n):
    return (strip * PAIRS + pair) * MODES + n


def lanes_of(at):
    return pl.ds(pl.multiple_of(at * LANES, LANES), LANES)


def piece(r):
    return pl.ds(r * LANES, LANES)


def spread(ref, at, natural):
    half = RUN // SUB
    for r in range(ROWS // SUB):
        start = (r % half) * SUB * SUB + r // half
        ref[at, pl.ds(start, SUB, stride=SUB), :] = natural[SUB * r : SUB * (r + 1), :]


def run_rows(ref, at, j):
    return ref[at, SUB * j : SUB * (j + 1), :]


def for_filters(make):
    def body(i, _):
        make(i)
        return 0

    lax.fori_loop(0, STRIPS * MODES, body, 0)


def row_of(ref, i):
    return jnp.broadcast_to(ref[pl.ds(i, 1), :], (SUB, LANES))


def total(parts):
    while len(parts) > 1:
        parts = [a + b for a, b in zip(parts[::2], parts[1::2])]
    return parts[0]


def prepare_kernel(q_hbm, k_hbm, v_hbm, u_hbm, ps, gs, q_ref, k_ref, v_ref, u_ref, sems):
    def copies(blk):
        cols = pl.ds(blk * FILTERS, FILTERS)
        return [
            pltpu.make_async_copy(src.at[:, cols], dst.at[:, cols], sems.at[blk, i])
            for i, (src, dst) in enumerate(
                ((k_hbm, k_ref), (v_hbm, v_ref), (u_hbm, u_ref), (q_hbm, q_ref))
            )
        ]

    for blk in range(BLOCKS):
        for copy in copies(blk):
            copy.start()
    for blk in range(BLOCKS):
        for copy in copies(blk):
            copy.wait()

        def strip_body(strip, _):
            at = blk * STRIPS + strip
            cols = lanes_of(at)
            spread(ps, at, k_ref[:, cols].astype(f32) * v_ref[:, cols].astype(f32))
            spread(gs, at, u_ref[:, cols].astype(f32) * q_ref[:, cols].astype(f32))
            return 0

        lax.fori_loop(0, STRIPS, strip_body, 0)


def summarize_kernel(
    half_ref, rate_ref, other_rate_ref, residue_ref, other_residue_ref, ps, gs,
    send_hbm, cf_hbm, cb_hbm, rates_hbm, residues_hbm,
    tab, send_ref, cf_ref, cb_ref, rates_ref, residues_ref, sems, param_sems,
):
    s = sublane()
    lower = jnp.broadcast_to(half_ref[0], (MODES, LANES)) == 0
    for strip in range(STRIPS):
        cols = pl.ds((strip % 2) * LANES, LANES)
        at = pl.ds(strip * MODES, MODES)
        for mine, other, out in (
            (rate_ref, other_rate_ref, rates_ref),
            (residue_ref, other_residue_ref, residues_ref),
        ):
            here, there = mine[:, cols], other[:, cols]
            if strip < STRIPS // 2:
                out[at, :] = jnp.where(lower, here, there)
            else:
                out[at, :] = jnp.where(lower, there, here)

    stored = [
        pltpu.make_async_copy(rates_ref, rates_hbm, param_sems.at[0]),
        pltpu.make_async_copy(residues_ref, residues_hbm, param_sems.at[1]),
    ]
    for copy in stored:
        copy.start()

    def make(i):
        log_decay = row_of(rates_ref, i) / TOKENS
        tab[0, i] = jnp.exp(-log_decay)
        for step in range(3):
            hop = 1 << step
            factor = jnp.exp(-log_decay * (RUN * hop))
            tab[1 + step, i] = jnp.where(s >= hop, factor, 0.0)
            tab[4 + step, i] = jnp.where(s < SUB - hop, factor, 0.0)

    for_filters(make)

    def sent(strip):
        at = pl.ds(strip * PAIRS * MODES, PAIRS * MODES)
        return [
            pltpu.make_async_copy(send_ref.at[at], send_hbm.at[at], sems.at[strip, 0]),
            pltpu.make_async_copy(cf_ref.at[strip], cf_hbm.at[strip], sems.at[strip, 1]),
            pltpu.make_async_copy(cb_ref.at[strip], cb_hbm.at[strip], sems.at[strip, 2]),
        ]

    def strip_body(strip, _):
        base = strip * MODES

        def pair_body(pair, _):
            gathered = [None] * MODES
            for odd in range(2):
                at = (2 * pair + odd) * STRIPS + strip
                decay = [tab[0, base + n] for n in range(MODES)]
                behind = [None] * MODES
                for j in reversed(range(RUN)):
                    gated = run_rows(gs, at, j)
                    for n in range(MODES):
                        behind[n] = gated if j == RUN - 1 else decay[n] * behind[n] + gated
                ahead, terms = [None] * MODES, [None] * MODES
                for j in range(RUN):
                    product, gated = run_rows(ps, at, j), run_rows(gs, at, j)
                    for n in range(MODES):
                        if j == 0:
                            ahead[n] = product
                            terms[n] = gated * product
                        else:
                            ahead[n] = decay[n] * ahead[n] + product
                            terms[n] = terms[n] + gated * ahead[n]
                first = list(behind)
                for step in range(3):
                    for n in range(MODES):
                        moved = pltpu.roll(ahead[n], 1 << step, 0)
                        ahead[n] = ahead[n] + tab[1 + step, base + n] * moved
                        moved = pltpu.roll(behind[n], SUB - (1 << step), 0)
                        behind[n] = behind[n] + tab[4 + step, base + n] * moved
                for n in range(MODES):
                    place = owner(strip, pair, n)
                    send_ref[place, :, piece(odd)] = ahead[n][SUB - 1 :, :]
                    send_ref[place, :, piece(2 + odd)] = behind[n][:1, :]
                    enter = jnp.where(s >= 1, pltpu.roll(ahead[n], 1, 0), 0.0)
                    leave = jnp.where(s < SUB - 1, pltpu.roll(behind[n], SUB - 1, 0), 0.0)
                    cf_ref[strip, 2 * pair + odd, n] = enter
                    cb_ref[strip, 2 * pair + odd, n] = leave
                    term = terms[n] + decay[n] * first[n] * enter
                    if odd == 0:
                        gathered[n] = term
                    else:
                        term = jnp.sum(gathered[n] + term, axis=0, keepdims=True)
                        send_ref[place, :, piece(4)] = term
            return 0

        lax.fori_loop(0, PAIRS, pair_body, 0)
        for copy in sent(strip):
            copy.start()
        return 0

    lax.fori_loop(0, STRIPS, strip_body, 0)
    for strip in range(STRIPS):
        for copy in sent(strip):
            copy.wait()
    for copy in stored:
        copy.wait()


def inner_kernel(reverse, rates_ref, residues_ref, one_ref, two_ref, enter_ref, out_ref, tab, xs):
    @pl.when(pl.program_id(0) == 0)
    def _():
        def make(i):
            rate = row_of(rates_ref, i)
            tab[0, i] = jnp.exp(-rate / TOKENS)
            tab[1, i] = row_of(residues_ref, i) * jnp.sqrt((1.0 + rate) / TOKENS)

        for_filters(make)

    def body(strip, _):
        base = strip * MODES
        cols = lanes_of(strip)
        spread(xs, 0, one_ref[:, cols].astype(f32) * two_ref[:, cols].astype(f32))
        decay = [tab[0, base + n] for n in range(MODES)]
        weight = [tab[1, base + n] for n in range(MODES)]
        state = [enter_ref[strip, 0, n] for n in range(MODES)]
        for j in reversed(range(RUN)) if reverse else range(RUN):
            x = run_rows(xs, 0, j)
            state = [decay[n] * state[n] + x for n in range(MODES)]
            mixed = total([weight[n] * state[n] for n in range(MODES)])
            out_ref[strip, pl.ds(j, SUB, stride=RUN), :] = mixed
        return 0

    lax.fori_loop(0, STRIPS, body, 0)


def carry_kernel(where_ref, rates_ref, x_ref, y_hbm, y_ref, sem):
    place = where_ref[0]
    at = (place // (PAIRS * MODES)) * MODES + place % MODES
    log_decay = rates_ref[pl.ds(at, 1), :] / TOKENS
    across = jnp.exp(-log_decay * ROWS)
    zero = jnp.zeros((1, LANES), f32)

    def step(i, carried):
        a0, a1, b0, b1, cross, terms = carried
        y_ref[i, :, piece(0)] = a0
        y_ref[i, :, piece(1)] = a1
        cross = cross + (a0 * x_ref[i, :, piece(2)] + a1 * x_ref[i, :, piece(3)])
        terms = terms + x_ref[i, :, piece(4)]
        back = SHARDS - 1 - i
        y_ref[back, :, piece(2)] = b0
        y_ref[back, :, piece(3)] = b1
        return (
            across * a0 + x_ref[i, :, piece(0)],
            across * a1 + x_ref[i, :, piece(1)],
            across * b0 + x_ref[back, :, piece(2)],
            across * b1 + x_ref[back, :, piece(3)],
            cross,
            terms,
        )

    carried = lax.fori_loop(0, SHARDS, step, (zero,) * 6, unroll=8)
    row = jnp.exp(-log_decay) * carried[4] + carried[5]

    def fill(i, _):
        y_ref[i, :, piece(4)] = row
        return 0

    lax.fori_loop(0, SHARDS, fill, 0, unroll=16)
    copy = pltpu.make_async_copy(y_ref, y_hbm, sem)
    copy.start()
    copy.wait()


def finish_kernel(
    rates_ref, residues_ref, k_hbm, v_hbm, u_hbm, conv_hbm, flow_hbm, in_ref,
    gq_hbm, gk_hbm, gv_hbm,
    tab, k_ref, v_ref, u_ref, conv_ref, flow_ref, gq_ref, gk_ref, gv_ref, arrive_sems, sems,
):
    s = sublane()

    def arrivals(blk):
        cols = pl.ds(blk * FILTERS, FILTERS)
        if not isinstance(blk, int):
            cols = pl.ds(pl.multiple_of(blk * FILTERS, FILTERS), FILTERS)
        deep = pl.ds(blk * STRIPS, STRIPS)
        pairs = [(a.at[deep], b.at[deep]) for a, b in ((conv_hbm, conv_ref), (flow_hbm, flow_ref))]
        for a, b in ((u_hbm, u_ref), (v_hbm, v_ref), (k_hbm, k_ref)):
            pairs.append((a.at[:, cols], b.at[:, cols]))
        return [
            pltpu.make_async_copy(a, b, arrive_sems.at[blk, i]) for i, (a, b) in enumerate(pairs)
        ]

    for blk in range(BLOCKS):
        for copy in arrivals(blk):
            copy.start()

    def make(i):
        rate = row_of(rates_ref, i)
        log_decay = rate / TOKENS
        weight = row_of(residues_ref, i) * jnp.sqrt((1.0 + rate) / TOKENS)
        tab[0, i] = jnp.exp(-log_decay * SUB)
        tab[1, i] = weight * jnp.exp(-log_decay * (s + 1).astype(f32))
        tab[2, i] = weight * jnp.exp(-log_decay * (SUB - s).astype(f32))

    for_filters(make)

    def copies(blk):
        cols = pl.ds(pl.multiple_of(blk * FILTERS, FILTERS), FILTERS)
        return [
            pltpu.make_async_copy(src.at[:, cols], dst.at[:, cols], sems.at[blk, i])
            for i, (src, dst) in enumerate(((gq_ref, gq_hbm), (gk_ref, gk_hbm), (gv_ref, gv_hbm)))
        ]

    def pair_body(pair, _):
        for odd in range(2):
            blk = 2 * pair + odd
            for copy in arrivals(blk):
                copy.wait()

            def strip_body(strip, _):
                base = strip * MODES
                col = blk * STRIPS + strip
                cols = lanes_of(col)
                leap = [tab[0, base + n] for n in range(MODES)]
                places = [owner(strip, pair, n) for n in range(MODES)]
                state = [
                    tab[1, base + n] * in_ref[places[n], :, piece(odd)] for n in range(MODES)
                ]
                for i in range(ROWS // 16):
                    parts = []
                    for _ in range(2):
                        parts.append(total(state))
                        state = [leap[n] * state[n] for n in range(MODES)]
                    at = pl.ds(16 * i, 16)
                    conv = conv_ref[col, at, :] + jnp.concatenate(parts, axis=0)
                    gq_ref[at, cols] = (u_ref[at, cols].astype(f32) * conv).astype(bf16)
                state = [
                    tab[2, base + n] * in_ref[places[n], :, piece(2 + odd)] for n in range(MODES)
                ]
                for i in reversed(range(ROWS // 16)):
                    parts = []
                    for _ in range(2):
                        parts.insert(0, total(state))
                        state = [leap[n] * state[n] for n in range(MODES)]
                    at = pl.ds(16 * i, 16)
                    flow = flow_ref[col, at, :] + jnp.concatenate(parts, axis=0)
                    gk_ref[at, cols] = (flow * v_ref[at, cols].astype(f32)).astype(bf16)
                    gv_ref[at, cols] = (flow * k_ref[at, cols].astype(f32)).astype(bf16)
                return 0

            lax.fori_loop(0, STRIPS, strip_body, 0)
            for copy in copies(blk):
                copy.start()
        return 0

    lax.fori_loop(0, PAIRS, pair_body, 0)
    for blk in range(BLOCKS):
        for copy in copies(blk):
            copy.wait()


def in_hbm(*arrays):
    return [pltpu.with_memory_space_constraint(a, pltpu.HBM) for a in arrays]


def local(query_rows, key_rows, value_rows, upstream, decay_rate, residue):
    half = lax.axis_index("fsdp")
    swap = [(0, 1), (1, 0)]
    other_rate = lax.ppermute(decay_rate, "fsdp", swap)
    other_residue = lax.ppermute(residue, "fsdp", swap)
    vmem = pl.BlockSpec(memory_space=pltpu.VMEM)
    smem = pl.BlockSpec(memory_space=pltpu.SMEM)
    hbm = pl.BlockSpec(memory_space=pltpu.HBM)
    limit = pltpu.CompilerParams(vmem_limit_bytes=16 << 20)
    packet = (SHARDS, 1, PACKET)
    packets = pltpu.HBM(packet, f32)
    tiles = (BLOCKS * STRIPS, ROWS, LANES)
    state = (STRIPS, BLOCKS, MODES, SUB, LANES)
    params = (STRIPS * MODES, LANES)
    table = (STRIPS * MODES, SUB, LANES)
    whole = pltpu.VMEM((ROWS, WIDTH), bf16)
    query_rows, key_rows, value_rows, upstream = in_hbm(
        query_rows, key_rows, value_rows, upstream
    )
    ps, gs = pl.pallas_call(
        prepare_kernel,
        in_specs=[hbm] * 4,
        out_specs=[vmem] * 2,
        out_shape=[jax.ShapeDtypeStruct(tiles, f32)] * 2,
        scratch_shapes=[whole] * 4 + [pltpu.SemaphoreType.DMA((BLOCKS, 4))],
        compiler_params=limit,
        cost_estimate=pl.CostEstimate(flops=1 << 22, bytes_accessed=12 << 20, transcendentals=0),
        name="prepare",
    )(query_rows, key_rows, value_rows, upstream)
    send, enter_ahead, enter_behind, rates, residues = pl.pallas_call(
        summarize_kernel,
        in_specs=[smem] + [vmem] * 6,
        out_specs=[hbm] * 5,
        out_shape=[packets] + [pltpu.HBM(state, f32)] * 2 + [pltpu.HBM(params, f32)] * 2,
        scratch_shapes=[
            pltpu.VMEM((7,) + table, f32),
            pltpu.VMEM(packet, f32),
            pltpu.VMEM(state, f32),
            pltpu.VMEM(state, f32),
            pltpu.VMEM(params, f32),
            pltpu.VMEM(params, f32),
            pltpu.SemaphoreType.DMA((STRIPS, 3)),
            pltpu.SemaphoreType.DMA((2,)),
        ],
        compiler_params=limit,
        name="summarize",
    )(half.astype(jnp.int32).reshape(1), decay_rate, other_rate, residue, other_residue, ps, gs)
    arrived = lax.all_to_all(send, ALL, 0, 0, tiled=True)

    def inner(one, two, enter, reverse):
        wide = pl.BlockSpec((ROWS, FILTERS), lambda b: (0, b))
        param = pl.BlockSpec((STRIPS * MODES, LANES), lambda b: (0, 0))
        return pl.pallas_call(
            functools.partial(inner_kernel, reverse),
            grid=(BLOCKS,),
            in_specs=[param] * 2
            + [wide] * 2
            + [pl.BlockSpec((STRIPS, 1, MODES, SUB, LANES), lambda b: (0, b, 0, 0, 0))],
            out_specs=pl.BlockSpec((STRIPS, ROWS, LANES), lambda b: (b, 0, 0)),
            out_shape=pltpu.HBM(tiles, f32),
            scratch_shapes=[pltpu.VMEM((2,) + table, f32), pltpu.VMEM((1, ROWS, LANES), f32)],
            cost_estimate=pl.CostEstimate(
                flops=1 << 24, bytes_accessed=16 << 20, transcendentals=0
            ),
            name="behind" if reverse else "ahead",
        )(rates, residues, one, two, enter)

    conv = inner(key_rows, value_rows, enter_ahead, False)
    arrived, conv = lax.optimization_barrier((arrived, conv))
    place = lax.axis_index(ALL).astype(jnp.int32).reshape(1)
    carries = pl.pallas_call(
        carry_kernel,
        in_specs=[smem] + [vmem] * 2,
        out_specs=hbm,
        out_shape=packets,
        scratch_shapes=[pltpu.VMEM(packet, f32), pltpu.SemaphoreType.DMA],
        compiler_params=limit,
        name="carry",
    )(place, rates, arrived)
    back = lax.all_to_all(carries, ALL, 0, 0, tiled=True)
    flowing = inner(upstream, query_rows, enter_behind, True)
    back, flowing = lax.optimization_barrier((back, flowing))
    rows = back[:, 0, 4 * LANES :].reshape(STRIPS, PAIRS, MODES, LANES)
    count = STRIPS // 2
    rows = lax.dynamic_slice_in_dim(rows, half * count, count, 0).sum(axis=1)
    rows = rows + lax.ppermute(rows, "ch", swap)
    rows = rows.transpose(1, 0, 2).reshape(MODES, count * LANES)
    gain = jnp.sqrt((1.0 + decay_rate) / TOKENS)
    residue_grad = gain * rows / math.sqrt(TOKENS)
    conv, flowing = in_hbm(conv, flowing)
    grads_out = pl.pallas_call(
        finish_kernel,
        in_specs=[vmem] * 2 + [hbm] * 5 + [vmem],
        out_specs=[hbm] * 3,
        out_shape=[pltpu.HBM((ROWS, WIDTH), bf16)] * 3,
        scratch_shapes=[
            pltpu.VMEM((3,) + table, f32),
            whole,
            whole,
            whole,
            pltpu.VMEM(tiles, f32),
            pltpu.VMEM(tiles, f32),
            whole,
            whole,
            whole,
            pltpu.SemaphoreType.DMA((BLOCKS, 5)),
            pltpu.SemaphoreType.DMA((BLOCKS, 3)),
        ],
        compiler_params=limit,
        name="finish",
    )(rates, residues, key_rows, value_rows, upstream, conv, flowing, back)
    return (*grads_out, residue_grad)


def solution(mesh):
    rows = P(ALL, "ch")
    params = P(None, "fsdp")
    return jax.shard_map(
        local,
        mesh=mesh,
        in_specs=(rows, rows, rows, rows, params, params),
        out_specs=(rows, rows, rows, params),
        check_vma=False,
    )
```

time: 1270 us -> 74.3 us (0.06); the launches traced: 1250 us -> 73.8 us
  blocking collectives: 658 us -> 0 us
  other arithmetic: 373 us -> 0.63 us
  local copies, waits for them, and re-layouts: 113 us -> 0.07 us
  waiting for transfers between devices: 58.7 us -> 12.6 us
  matrix products: 32.5 us -> 0 us
  Pallas kernels: 0 us -> 31.1 us
  starting transfers between devices: 0.12 us -> 28.6 us
  between operations: 13.9 us -> 0.77 us
    psum x1 -> x0, blocking collectives: 348 us -> none  [local(): summed = lax.psum(partial_grad, ('ctx', 'ch'))]
    unnamed x1 -> x0, blocking collectives: 302 us -> none
    exp x135 -> x0, other arithmetic: 177 us -> none  [the longest x127 173 us: combine(): jnp.exp(-log_decay * later[0][0]) * earlier[1]]
    add x127 -> x0, other arithmetic: 122 us -> none  [combine(): later[1] + jnp.exp(-log_decay * later[0][0]) * earlier[1]]
    dynamic_slice x191 -> x0, local copies, waits for them, and re-layouts: 89 us -> none  [the longest x127 77.7 us: one(): lax.dynamic_index_in_dim(a, source, 0, False)]
    reduce_scatter x1 -> x0, waiting for transfers between devices: 58 us -> none  [local(): lax.psum_scatter(summed, 'fsdp', scatter_dimension=1, tiled=True)]
    reduce_sum x17 -> x1, other arithmetic: 42.3 us -> 0.01 us  [local(): rows = lax.dynamic_slice_in_dim(rows, half * count, count, 0).sum(axis=1)]
    dot_general x16 -> x0, matrix products: 32.5 us -> none  [running(): jnp.dot(ones, flat, precision=lax.Precision.HIGHEST, preferred_element_ty...]
  transfers between devices with their start and end apart: 3 -> 5, of which waited for: 1 -> 2; matrix products, arithmetic and copies ran while one was open for 30% -> 0% of each run, Pallas kernels for 0% -> 32%
where the time goes in v2:
time: 74.3 us; the launch traced here: 73.8 us
  Pallas kernels  31.1 us (42%)
  starting transfers between devices  28.6 us (38%)
  waiting for transfers between devices  12.6 us (17%)
  between operations  0.77 us (1%)
    pallas_call x2, Pallas kernels, inner(): pl.pallas_call(functools.partial(inner_kernel, reverse), grid=(BLOCKS,),...  15.5 us
    all_to_all x1, starting transfers between devices, local(): arrived = lax.all_to_all(send, ALL, 0, 0, tiled=True)  15.2 us
    all_to_all x1, starting transfers between devices, local(): back = lax.all_to_all(carries, ALL, 0, 0, tiled=True)  7.12 us
    all_to_all x1, waiting for transfers between devices, local(): arrived = lax.all_to_all(send, ALL, 0, 0, tiled=True)  6.43 us
    pallas_call x1, Pallas kernels, local(): pl.pallas_call(summarize_kernel, in_specs=[smem] + [vmem] * 6, out_specs=...  6.15 us
    all_to_all x1, waiting for transfers between devices, local(): back = lax.all_to_all(carries, ALL, 0, 0, tiled=True)  6.12 us
    pallas_call x1, Pallas kernels, local(): pl.pallas_call(finish_kernel, in_specs=[vmem] * 2 + [hbm] * 5 + [vmem], o...  5.59 us
    ppermute x1, starting transfers between devices, local(): rows = rows + lax.ppermute(rows, 'ch', swap)  3.64 us
  transfers between devices with their start and end apart: 5, of which 2 were waited for; matrix products, arithmetic and copies ran while one was open for 0% of the time, Pallas kernels for 32%

profile of v2, /device:TPU:1, one launch (start us, length us, event | category | flops | bytes accessed | tf_op | source)
XLA Modules:
  0.0 73.8 jit_solution(6386123405742849908)
XLA Ops:
  0.6 2.5 %collective-permute-start.1 = (f32[8,256]{1,0:T(8,128)}, f32[8,256]{1,0:T(8,128)S(1)}, u32[]{:S(2)}, u32[]{:S(2)}) collective-permute-start(f32[8,256]{1,0:T(8,128)} %residue_ref.1), channel_id=1, source_target_pairs={{0,1},{1,0},{2,3},{3,2},{4,5},{5,4},{6,7},{7,6},{8,9},{9,8},{10,11... | collective-permute-start | bytes 24584 | tf_op jit(solution)/shard_map/ppermute | solution.py:367
  3.2 0.1 collective-permute-start
  3.3 0.0 copy-start.3
  3.3 0.0 copy-start.4
  3.3 2.7 %prepare.1 = (f32[32,128,128]{2,1,0:T(8,128)S(1)}, f32[32,128,128]{2,1,0:T(8,128)S(1)}) custom-call(bf16[128,4096]{1,0:T(8,128)(2,1)} %two_ref.3, bf16[128,4096]{1,0:T(8,128)(2,1)} %k_hbm.3, bf16[128,4096]{1,0:T(8,128)(2,1)} %v_hbm.3, bf16[128,4096]{1,0:T(8,128)(2,1)} %u_hbm.3), custom_call_target="tpu_custom_call" | custom-call | flops 4194304 | bytes 12582912 | tf_op jit(solution)/shard_map/prepare/pallas_call | solution.py:382
  6.0 0.0 collective-permute-done.1.other_residue_ref
  6.0 0.0 collective-permute-done.other_rate_ref
  6.0 0.0 copy-done.3
  6.0 0.0 copy-done.4
  6.0 6.2 %summarize.1 = (f32[128,1,640]{2,1,0:T(1,128)}, f32[4,8,8,8,128]{4,3,2,1,0:T(8,128)}, f32[4,8,8,8,128]{4,3,2,1,0:T(8,128)}, f32[32,128]{1,0:T(8,128)}, f32[32,128]{1,0:T(8,128)}) custom-call(s32[1]{0:T(128)} %bitcast.half_ref, f32[8,256]{1,0:T(8,128)S(1)} %copy-done.3, f32[8,256]{1,0:T(8,128)S(1)} %collective-permute-done.other_rate_ref, ...), custom_call_target="tpu_custom_call" | custom-call | tf_op jit(solution)/shard_map/summarize/pallas_call | solution.py:392
  12.2 15.2 %all-to-all-start = ((f32[128,1,640]{2,1,0:T(1,128)}), f32[128,1,640]{2,1,0:T(1,128)S(1)}, u32[]{:S(2)}, u32[]{:S(2)}) async-start(f32[128,1,640]{2,1,0:T(1,128)} %get-tuple-element.22), calls=%async_computation | async-start | bytes 655360 | tf_op jit(solution)/shard_map/all_to_all | solution.py:410
  27.5 0.0 copy-start
  27.5 7.8 %ahead.1.conv_hbm = f32[32,128,128]{2,1,0:T(8,128)} custom-call(f32[32,128]{1,0:T(8,128)} %get-tuple-element.20.rates_ref, f32[32,128]{1,0:T(8,128)} %get-tuple-element.21.residues_ref, bf16[128,4096]{1,0:T(8,128)(2,1)} %k_hbm.3, bf16[128,4096]{1,0:T(8,128)(2,1)} %v_hbm.3, f32[4,8,8,8,128]{4,3,2,1,0:T(8,128)} %get-tuple-element.23.enter_ref), custom_call_target="tpu_custom_call" | custom-call | flops 16777216 | bytes 16777216 | tf_op jit(solution)/shard_map/ahead/pallas_call | solution.py:415
  35.2 6.4 %all-to-all-done.x_ref = f32[128,1,640]{2,1,0:T(1,128)S(1)} async-done(((f32[128,1,640]{2,1,0:T(1,128)}), f32[128,1,640]{2,1,0:T(1,128)S(1)}, u32[]{:S(2)}, u32[]{:S(2)}) %all-to-all-start) | async-done | bytes 327712 | tf_op jit(solution)/shard_map/all_to_all | solution.py:410
  41.7 0.0 copy-done
  41.7 1.2 %carry.1 = f32[128,1,640]{2,1,0:T(1,128)} custom-call(s32[1]{0:T(128)} %bitcast.1.where_ref, f32[32,128]{1,0:T(8,128)S(1)} %copy-done, f32[128,1,640]{2,1,0:T(1,128)S(1)} %all-to-all-done.x_ref), custom_call_target="tpu_custom_call" | custom-call | tf_op jit(solution)/shard_map/carry/pallas_call | solution.py:433
  42.9 7.1 %all-to-all-start.1 = ((f32[128,1,640]{2,1,0:T(1,128)}), f32[128,1,640]{2,1,0:T(1,128)S(1)}, u32[]{:S(2)}, u32[]{:S(2)}) async-start(f32[128,1,640]{2,1,0:T(1,128)} %carry.1), calls=%async_computation.1 | async-start | bytes 655360 | tf_op jit(solution)/shard_map/all_to_all | solution.py:442
  50.0 0.0 copy-start.1
  50.0 0.0 copy-start.2
  50.0 7.7 %behind.1.flow_hbm = f32[32,128,128]{2,1,0:T(8,128)} custom-call(f32[32,128]{1,0:T(8,128)} %get-tuple-element.20.rates_ref, f32[32,128]{1,0:T(8,128)} %get-tuple-element.21.residues_ref, bf16[128,4096]{1,0:T(8,128)(2,1)} %u_hbm.3, bf16[128,4096]{1,0:T(8,128)(2,1)} %two_ref.3, f32[4,8,8,8,128]{4,3,2,1,0:T(8,128)} %get-tuple-element.26.enter_ref), custom_call_target="tpu_custom_call" | custom-call | flops 16777216 | bytes 16777216 | tf_op jit(solution)/shard_map/behind/pallas_call | solution.py:415
  57.8 6.1 %all-to-all-done.1.in_ref = f32[128,1,640]{2,1,0:T(1,128)S(1)} async-done(((f32[128,1,640]{2,1,0:T(1,128)}), f32[128,1,640]{2,1,0:T(1,128)S(1)}, u32[]{:S(2)}, u32[]{:S(2)}) %all-to-all-start.1) | async-done | bytes 327712 | tf_op jit(solution)/shard_map/all_to_all | solution.py:442
  64.0 3.6 %collective-permute-start.2 = (f32[2,8,128]{2,1,0:T(8,128)S(1)}, f32[2,8,128]{2,1,0:T(8,128)S(1)}, u32[]{:S(2)}, u32[]{:S(2)}) collective-permute-start(f32[2,8,128]{2,1,0:T(8,128)S(1)} %dynamic-slice_reduce_fusion), channel_id=1, source_target_pairs={{0,2},{2,0},{1,3},{3,1},{4,6},{6,4},{5,7},{7,5},{8,10},{10,8},{9,1... | collective-permute-start | bytes 24584 | tf_op jit(solution)/shard_map/ppermute | solution.py:448
  67.6 0.0 copy-done.1
  67.6 0.0 copy-done.2
  67.6 5.6 %finish.1 = (bf16[128,4096]{1,0:T(8,128)(2,1)}, bf16[128,4096]{1,0:T(8,128)(2,1)}, bf16[128,4096]{1,0:T(8,128)(2,1)}) custom-call(f32[32,128]{1,0:T(8,128)S(1)} %copy-done.1, f32[32,128]{1,0:T(8,128)S(1)} %copy-done.2, bf16[128,4096]{1,0:T(8,128)(2,1)} %k_hbm.3, bf16[128,4096]{1,0:T(8,128)(2,1)} %v_hbm.3, bf16[128,4096]{1,0:T(8,128)(2,1)} %u_hbm.3, ...), custom_call_target="tpu_custom_call" | custom-call | tf_op jit(solution)/shard_map/finish/pallas_call | solution.py:453
  73.2 0.0 collective-permute-done.2
  73.2 0.6 fusion
  (2 shorter events, 0.1 us)
Async XLA Ops:
  0.6 5.4 %collective-permute-start.1 = (f32[8,256]{1,0:T(8,128)}, f32[8,256]{1,0:T(8,128)S(1)}, u32[]{:S(2)}, u32[]{:S(2)}) collective-permute-start(f32[8,256]{1,0:T(8,128)} %residue_ref.1), channel_id=1, source_target_pairs={{0,1},{1,0},{2,3},{3,2},{4,5},{5,4},{6,7},{7,6},{8,9},{9,8},{10,11... | collective-permute-start | bytes 24584 | tf_op jit(solution)/shard_map/ppermute | solution.py:367
  3.2 2.8 %collective-permute-start = (f32[8,256]{1,0:T(8,128)}, f32[8,256]{1,0:T(8,128)S(1)}, u32[]{:S(2)}, u32[]{:S(2)}) collective-permute-start(f32[8,256]{1,0:T(8,128)} %rate_ref.1), channel_id=1, source_target_pairs={{0,1},{1,0},{2,3},{3,2},{4,5},{5,4},{6,7},{7,6},{8,9},{9,8},{10,11... | collective-permute-start | bytes 24584 | tf_op jit(solution)/shard_map/ppermute | solution.py:366
  3.3 2.7 %copy-start.3 = (f32[8,256]{1,0:T(8,128)S(1)}, f32[8,256]{1,0:T(8,128)}, u32[]{:S(2)}) copy-start(f32[8,256]{1,0:T(8,128)} %rate_ref.1) | copy-start | bytes 24580
  3.3 2.8 %copy-start.4 = (f32[8,256]{1,0:T(8,128)S(1)}, f32[8,256]{1,0:T(8,128)}, u32[]{:S(2)}) copy-start(f32[8,256]{1,0:T(8,128)} %residue_ref.1) | copy-start | bytes 24580
  12.2 29.5 %all-to-all-start = ((f32[128,1,640]{2,1,0:T(1,128)}), f32[128,1,640]{2,1,0:T(1,128)S(1)}, u32[]{:S(2)}, u32[]{:S(2)}) async-start(f32[128,1,640]{2,1,0:T(1,128)} %get-tuple-element.22), calls=%async_computation | async-start | bytes 655360 | tf_op jit(solution)/shard_map/all_to_all | solution.py:410
  27.5 14.2 %copy-start = (f32[32,128]{1,0:T(8,128)S(1)}, f32[32,128]{1,0:T(8,128)}, u32[]{:S(2)}) copy-start(f32[32,128]{1,0:T(8,128)} %get-tuple-element.20.rates_ref) | copy-start | bytes 49156
  42.9 21.0 %all-to-all-start.1 = ((f32[128,1,640]{2,1,0:T(1,128)}), f32[128,1,640]{2,1,0:T(1,128)S(1)}, u32[]{:S(2)}, u32[]{:S(2)}) async-start(f32[128,1,640]{2,1,0:T(1,128)} %carry.1), calls=%async_computation.1 | async-start | bytes 655360 | tf_op jit(solution)/shard_map/all_to_all | solution.py:442
  50.0 17.6 %copy-start.1 = (f32[32,128]{1,0:T(8,128)S(1)}, f32[32,128]{1,0:T(8,128)}, u32[]{:S(2)}) copy-start(f32[32,128]{1,0:T(8,128)} %get-tuple-element.20.rates_ref) | copy-start | bytes 49156
  50.0 17.6 %copy-start.2 = (f32[32,128]{1,0:T(8,128)S(1)}, f32[32,128]{1,0:T(8,128)}, u32[]{:S(2)}) copy-start(f32[32,128]{1,0:T(8,128)} %get-tuple-element.21.residues_ref) | copy-start | bytes 49156
  64.0 9.2 %collective-permute-start.2 = (f32[2,8,128]{2,1,0:T(8,128)S(1)}, f32[2,8,128]{2,1,0:T(8,128)S(1)}, u32[]{:S(2)}, u32[]{:S(2)}) collective-permute-start(f32[2,8,128]{2,1,0:T(8,128)S(1)} %dynamic-slice_reduce_fusion), channel_id=1, source_target_pairs={{0,2},{2,0},{1,3},{3,1},{4,6},{6,4},{5,7},{7,5},{8,10},{10,8},{9,1... | collective-permute-start | bytes 24584 | tf_op jit(solution)/shard_map/ppermute | solution.py:448

commit v3 on v2

--- a/solution.py
+++ b/solution.py
@@ -15,6 +15,7 @@
 BLOCKS = 8
 SUB = 8
 RUN = ROWS // SUB
+HALF = RUN // 2
 LANES = 128
 STRIPS = FILTERS // LANES
 PAIRS = BLOCKS // 2
@@ -46,11 +47,11 @@
     half = RUN // SUB
     for r in range(ROWS // SUB):
         start = (r % half) * SUB * SUB + r // half
-        ref[at, pl.ds(start, SUB, stride=SUB), :] = natural[SUB * r : SUB * (r + 1), :]
+        ref[(*at, pl.ds(start, SUB, stride=SUB))] = natural[SUB * r : SUB * (r + 1), :]
 
 
 def run_rows(ref, at, j):
-    return ref[at, SUB * j : SUB * (j + 1), :]
+    return ref[(*at, pl.ds(SUB * j, SUB))]
 
 
 def for_filters(make):
@@ -89,8 +90,8 @@
             copy.wait()
 
         def strip_body(strip, _):
-            at = blk * STRIPS + strip
-            cols = lanes_of(at)
+            at = (strip, blk)
+            cols = lanes_of(blk * STRIPS + strip)
             spread(ps, at, k_ref[:, cols].astype(f32) * v_ref[:, cols].astype(f32))
             spread(gs, at, u_ref[:, cols].astype(f32) * q_ref[:, cols].astype(f32))
             return 0
@@ -99,28 +100,28 @@
 
 
 def summarize_kernel(
-    half_ref, rate_ref, other_rate_ref, residue_ref, other_residue_ref, ps, gs,
-    send_hbm, cf_hbm, cb_hbm, rates_hbm, residues_hbm,
-    tab, send_ref, cf_ref, cb_ref, rates_ref, residues_ref, sems, param_sems,
+    half_ref, mine_ref, other_ref, ps, gs,
+    send_hbm, cf_hbm, cb_hbm, rates_hbm, residues_hbm, ps_hbm, gs_hbm,
+    tab, lags, joins, send_ref, cf_ref, cb_ref, rates_ref, residues_ref, sems, early_sems,
 ):
     s = sublane()
     lower = jnp.broadcast_to(half_ref[0], (MODES, LANES)) == 0
     for strip in range(STRIPS):
         cols = pl.ds((strip % 2) * LANES, LANES)
         at = pl.ds(strip * MODES, MODES)
-        for mine, other, out in (
-            (rate_ref, other_rate_ref, rates_ref),
-            (residue_ref, other_residue_ref, residues_ref),
-        ):
-            here, there = mine[:, cols], other[:, cols]
+        for part, out in enumerate((rates_ref, residues_ref)):
+            rows = pl.ds(part * MODES, MODES)
+            here, there = mine_ref[rows, cols], other_ref[rows, cols]
             if strip < STRIPS // 2:
                 out[at, :] = jnp.where(lower, here, there)
             else:
                 out[at, :] = jnp.where(lower, there, here)
 
     stored = [
-        pltpu.make_async_copy(rates_ref, rates_hbm, param_sems.at[0]),
-        pltpu.make_async_copy(residues_ref, residues_hbm, param_sems.at[1]),
+        pltpu.make_async_copy(a, b, early_sems.at[i])
+        for i, (a, b) in enumerate(
+            ((rates_ref, rates_hbm), (residues_ref, residues_hbm), (ps, ps_hbm), (gs, gs_hbm))
+        )
     ]
     for copy in stored:
         copy.start()
@@ -132,7 +133,7 @@
             hop = 1 << step
             factor = jnp.exp(-log_decay * (RUN * hop))
             tab[1 + step, i] = jnp.where(s >= hop, factor, 0.0)
-            tab[4 + step, i] = jnp.where(s < SUB - hop, factor, 0.0)
+        tab[4, i] = jnp.exp(-log_decay * (RUN * s).astype(f32))
 
     for_filters(make)
 
@@ -147,50 +148,61 @@
     def strip_body(strip, _):
         base = strip * MODES
 
+        for lag in range(HALF):
+            lags[lag] = jnp.zeros((SUB, LANES), f32)
+        for n in range(MODES):
+            joins[n] = jnp.zeros((SUB, LANES), f32)
+
         def pair_body(pair, _):
-            gathered = [None] * MODES
             for odd in range(2):
-                at = (2 * pair + odd) * STRIPS + strip
+                at = (strip, 2 * pair + odd)
                 decay = [tab[0, base + n] for n in range(MODES)]
-                behind = [None] * MODES
+                behind, middle = [None] * MODES, [None] * MODES
                 for j in reversed(range(RUN)):
                     gated = run_rows(gs, at, j)
                     for n in range(MODES):
                         behind[n] = gated if j == RUN - 1 else decay[n] * behind[n] + gated
-                ahead, terms = [None] * MODES, [None] * MODES
+                    if j == HALF:
+                        middle = list(behind)
+                ahead, joint = [None] * MODES, [None] * MODES
                 for j in range(RUN):
-                    product, gated = run_rows(ps, at, j), run_rows(gs, at, j)
+                    product = run_rows(ps, at, j)
                     for n in range(MODES):
-                        if j == 0:
-                            ahead[n] = product
-                            terms[n] = gated * product
-                        else:
-                            ahead[n] = decay[n] * ahead[n] + product
-                            terms[n] = terms[n] + gated * ahead[n]
-                first = list(behind)
+                        ahead[n] = product if j == 0 else decay[n] * ahead[n] + product
+                        if j == HALF - 1:
+                            joint[n] = ahead[n] * middle[n]
+                for lag in range(HALF):
+                    starts = [j for j in range(RUN) if j // HALF == (j + lag) // HALF]
+                    pairs = [run_rows(gs, at, j + lag) * run_rows(ps, at, j) for j in starts]
+                    while len(pairs) > 1:
+                        odd_one = pairs[-1:] if len(pairs) % 2 else []
+                        pairs = [a + b for a, b in zip(pairs[::2], pairs[1::2])] + odd_one
+                    lags[lag] = lags[lag] + pairs[0]
                 for step in range(3):
                     for n in range(MODES):
                         moved = pltpu.roll(ahead[n], 1 << step, 0)
                         ahead[n] = ahead[n] + tab[1 + step, base + n] * moved
-                        moved = pltpu.roll(behind[n], SUB - (1 << step), 0)
-                        behind[n] = behind[n] + tab[4 + step, base + n] * moved
                 for n in range(MODES):
                     place = owner(strip, pair, n)
                     send_ref[place, :, piece(odd)] = ahead[n][SUB - 1 :, :]
-                    send_ref[place, :, piece(2 + odd)] = behind[n][:1, :]
+                    first = jnp.sum(tab[4, base + n] * behind[n], axis=0, keepdims=True)
+                    send_ref[place, :, piece(2 + odd)] = first
                     enter = jnp.where(s >= 1, pltpu.roll(ahead[n], 1, 0), 0.0)
-                    leave = jnp.where(s < SUB - 1, pltpu.roll(behind[n], SUB - 1, 0), 0.0)
                     cf_ref[strip, 2 * pair + odd, n] = enter
-                    cb_ref[strip, 2 * pair + odd, n] = leave
-                    term = terms[n] + decay[n] * first[n] * enter
-                    if odd == 0:
-                        gathered[n] = term
-                    else:
-                        term = jnp.sum(gathered[n] + term, axis=0, keepdims=True)
-                        send_ref[place, :, piece(4)] = term
+                    cb_ref[strip, 2 * pair + odd, n] = behind[n]
+                    joins[n] = joins[n] + (joint[n] + behind[n] * enter)
             return 0
 
         lax.fori_loop(0, PAIRS, pair_body, 0)
+        for n in range(MODES):
+            decay = tab[0, base + n]
+            term = lags[HALF - 1]
+            for lag in reversed(range(HALF - 1)):
+                term = decay * term + lags[lag]
+            term = jnp.sum(term + decay * joins[n], axis=0, keepdims=True)
+            for pair in range(PAIRS):
+                row = term if pair == 0 else jnp.zeros((1, LANES), f32)
+                send_ref[owner(strip, pair, n), :, piece(4)] = row
         for copy in sent(strip):
             copy.start()
         return 0
@@ -203,31 +215,73 @@
         copy.wait()
 
 
-def inner_kernel(reverse, rates_ref, residues_ref, one_ref, two_ref, enter_ref, out_ref, tab, xs):
-    @pl.when(pl.program_id(0) == 0)
-    def _():
-        def make(i):
-            rate = row_of(rates_ref, i)
-            tab[0, i] = jnp.exp(-rate / TOKENS)
-            tab[1, i] = row_of(residues_ref, i) * jnp.sqrt((1.0 + rate) / TOKENS)
-
-        for_filters(make)
-
-    def body(strip, _):
+def inner_kernel(
+    reverse, rates_hbm, residues_hbm, xs_hbm, enter_hbm, out_hbm,
+    tab, rates_ref, residues_ref, xs, enter_ref, out_ref, param_sems, sems,
+):
+    params = [
+        pltpu.make_async_copy(rates_hbm, rates_ref, param_sems.at[0]),
+        pltpu.make_async_copy(residues_hbm, residues_ref, param_sems.at[1]),
+    ]
+
+    def arrivals(strip):
+        return [
+            pltpu.make_async_copy(enter_hbm.at[strip], enter_ref.at[strip], sems.at[strip, 0]),
+            pltpu.make_async_copy(xs_hbm.at[strip], xs.at[strip], sems.at[strip, 1]),
+        ]
+
+    def leaving(strip):
+        return pltpu.make_async_copy(out_ref.at[strip], out_hbm.at[strip], sems.at[strip, 2])
+
+    s = sublane()
+    for copy in params:
+        copy.start()
+    for strip in range(STRIPS):
+        for copy in arrivals(strip):
+            copy.start()
+    for copy in params:
+        copy.wait()
+
+    def make(i):
+        rate = row_of(rates_ref, i)
+        tab[0, i] = jnp.exp(-rate / TOKENS)
+        tab[1, i] = row_of(residues_ref, i) * jnp.sqrt((1.0 + rate) / TOKENS)
+        for step in range(3 if reverse else 0):
+            factor = jnp.exp(-rate / TOKENS * (RUN << step))
+            tab[2 + step, i] = jnp.where(s < SUB - (1 << step), factor, 0.0)
+
+    for_filters(make)
+
+    def strip_body(strip, _):
+        for copy in arrivals(strip):
+            copy.wait()
         base = strip * MODES
-        cols = lanes_of(strip)
-        spread(xs, 0, one_ref[:, cols].astype(f32) * two_ref[:, cols].astype(f32))
-        decay = [tab[0, base + n] for n in range(MODES)]
-        weight = [tab[1, base + n] for n in range(MODES)]
-        state = [enter_ref[strip, 0, n] for n in range(MODES)]
-        for j in reversed(range(RUN)) if reverse else range(RUN):
-            x = run_rows(xs, 0, j)
-            state = [decay[n] * state[n] + x for n in range(MODES)]
-            mixed = total([weight[n] * state[n] for n in range(MODES)])
-            out_ref[strip, pl.ds(j, SUB, stride=RUN), :] = mixed
+
+        def body(blk, _):
+            at = (strip, blk)
+            decay = [tab[0, base + n] for n in range(MODES)]
+            weight = [tab[1, base + n] for n in range(MODES)]
+            state = [enter_ref[strip, blk, n] for n in range(MODES)]
+            if reverse:
+                for step in range(3):
+                    for n in range(MODES):
+                        moved = pltpu.roll(state[n], SUB - (1 << step), 0)
+                        state[n] = state[n] + tab[2 + step, base + n] * moved
+                state = [jnp.where(s < SUB - 1, pltpu.roll(a, SUB - 1, 0), 0.0) for a in state]
+            for j in reversed(range(RUN)) if reverse else range(RUN):
+                x = run_rows(xs, at, j)
+                state = [decay[n] * state[n] + x for n in range(MODES)]
+                mixed = total([weight[n] * state[n] for n in range(MODES)])
+                out_ref[strip, blk, pl.ds(j, SUB, stride=RUN), :] = mixed
+            return 0
+
+        lax.fori_loop(0, BLOCKS, body, 0)
+        leaving(strip).start()
         return 0
 
-    lax.fori_loop(0, STRIPS, body, 0)
+    lax.fori_loop(0, STRIPS, strip_body, 0)
+    for strip in range(STRIPS):
+        leaving(strip).wait()
 
 
 def carry_kernel(where_ref, rates_ref, x_ref, y_hbm, y_ref, sem):
@@ -279,8 +333,9 @@
         cols = pl.ds(blk * FILTERS, FILTERS)
         if not isinstance(blk, int):
             cols = pl.ds(pl.multiple_of(blk * FILTERS, FILTERS), FILTERS)
-        deep = pl.ds(blk * STRIPS, STRIPS)
-        pairs = [(a.at[deep], b.at[deep]) for a, b in ((conv_hbm, conv_ref), (flow_hbm, flow_ref))]
+        pairs = [
+            (a.at[:, blk], b.at[:, blk]) for a, b in ((conv_hbm, conv_ref), (flow_hbm, flow_ref))
+        ]
         for a, b in ((u_hbm, u_ref), (v_hbm, v_ref), (k_hbm, k_ref)):
             pairs.append((a.at[:, cols], b.at[:, cols]))
         return [
@@ -316,8 +371,7 @@
 
             def strip_body(strip, _):
                 base = strip * MODES
-                col = blk * STRIPS + strip
-                cols = lanes_of(col)
+                cols = lanes_of(blk * STRIPS + strip)
                 leap = [tab[0, base + n] for n in range(MODES)]
                 places = [owner(strip, pair, n) for n in range(MODES)]
                 state = [
@@ -329,7 +383,7 @@
                         parts.append(total(state))
                         state = [leap[n] * state[n] for n in range(MODES)]
                     at = pl.ds(16 * i, 16)
-                    conv = conv_ref[col, at, :] + jnp.concatenate(parts, axis=0)
+                    conv = conv_ref[strip, blk, at, :] + jnp.concatenate(parts, axis=0)
                     gq_ref[at, cols] = (u_ref[at, cols].astype(f32) * conv).astype(bf16)
                 state = [
                     tab[2, base + n] * in_ref[places[n], :, piece(2 + odd)] for n in range(MODES)
@@ -340,7 +394,7 @@
                         parts.insert(0, total(state))
                         state = [leap[n] * state[n] for n in range(MODES)]
                     at = pl.ds(16 * i, 16)
-                    flow = flow_ref[col, at, :] + jnp.concatenate(parts, axis=0)
+                    flow = flow_ref[strip, blk, at, :] + jnp.concatenate(parts, axis=0)
                     gk_ref[at, cols] = (flow * v_ref[at, cols].astype(f32)).astype(bf16)
                     gv_ref[at, cols] = (flow * k_ref[at, cols].astype(f32)).astype(bf16)
                 return 0
@@ -363,15 +417,18 @@
 def local(query_rows, key_rows, value_rows, upstream, decay_rate, residue):
     half = lax.axis_index("fsdp")
     swap = [(0, 1), (1, 0)]
-    other_rate = lax.ppermute(decay_rate, "fsdp", swap)
-    other_residue = lax.ppermute(residue, "fsdp", swap)
+    first = lax.broadcasted_iota(jnp.int32, (2 * MODES, FILTERS // 2), 0) < MODES
+    below, above = ((0, MODES, 0), (0, 0, 0)), ((MODES, 0, 0), (0, 0, 0))
+    zero = jnp.zeros((), f32)
+    mine = jnp.where(first, lax.pad(decay_rate, zero, below), lax.pad(residue, zero, above))
+    other = lax.ppermute(mine, "fsdp", swap)
     vmem = pl.BlockSpec(memory_space=pltpu.VMEM)
     smem = pl.BlockSpec(memory_space=pltpu.SMEM)
     hbm = pl.BlockSpec(memory_space=pltpu.HBM)
     limit = pltpu.CompilerParams(vmem_limit_bytes=16 << 20)
     packet = (SHARDS, 1, PACKET)
     packets = pltpu.HBM(packet, f32)
-    tiles = (BLOCKS * STRIPS, ROWS, LANES)
+    tiles = (STRIPS, BLOCKS, ROWS, LANES)
     state = (STRIPS, BLOCKS, MODES, SUB, LANES)
     params = (STRIPS * MODES, LANES)
     table = (STRIPS * MODES, SUB, LANES)
@@ -389,45 +446,54 @@
         cost_estimate=pl.CostEstimate(flops=1 << 22, bytes_accessed=12 << 20, transcendentals=0),
         name="prepare",
     )(query_rows, key_rows, value_rows, upstream)
-    send, enter_ahead, enter_behind, rates, residues = pl.pallas_call(
+    send, enter_ahead, enter_behind, rates, residues, product, gated = pl.pallas_call(
         summarize_kernel,
-        in_specs=[smem] + [vmem] * 6,
-        out_specs=[hbm] * 5,
-        out_shape=[packets] + [pltpu.HBM(state, f32)] * 2 + [pltpu.HBM(params, f32)] * 2,
+        in_specs=[smem] + [vmem] * 4,
+        out_specs=[hbm] * 7,
+        out_shape=[packets]
+        + [pltpu.HBM(state, f32)] * 2
+        + [pltpu.HBM(params, f32)] * 2
+        + [pltpu.HBM(tiles, f32)] * 2,
         scratch_shapes=[
-            pltpu.VMEM((7,) + table, f32),
+            pltpu.VMEM((5,) + table, f32),
+            pltpu.VMEM((HALF, SUB, LANES), f32),
+            pltpu.VMEM((MODES, SUB, LANES), f32),
             pltpu.VMEM(packet, f32),
             pltpu.VMEM(state, f32),
             pltpu.VMEM(state, f32),
             pltpu.VMEM(params, f32),
             pltpu.VMEM(params, f32),
             pltpu.SemaphoreType.DMA((STRIPS, 3)),
-            pltpu.SemaphoreType.DMA((2,)),
+            pltpu.SemaphoreType.DMA((4,)),
         ],
         compiler_params=limit,
         name="summarize",
-    )(half.astype(jnp.int32).reshape(1), decay_rate, other_rate, residue, other_residue, ps, gs)
+    )(half.astype(jnp.int32).reshape(1), mine, other, ps, gs)
     arrived = lax.all_to_all(send, ALL, 0, 0, tiled=True)
 
-    def inner(one, two, enter, reverse):
-        wide = pl.BlockSpec((ROWS, FILTERS), lambda b: (0, b))
-        param = pl.BlockSpec((STRIPS * MODES, LANES), lambda b: (0, 0))
+    def inner(xs, enter, reverse):
         return pl.pallas_call(
             functools.partial(inner_kernel, reverse),
-            grid=(BLOCKS,),
-            in_specs=[param] * 2
-            + [wide] * 2
-            + [pl.BlockSpec((STRIPS, 1, MODES, SUB, LANES), lambda b: (0, b, 0, 0, 0))],
-            out_specs=pl.BlockSpec((STRIPS, ROWS, LANES), lambda b: (b, 0, 0)),
+            in_specs=[hbm] * 4,
+            out_specs=hbm,
             out_shape=pltpu.HBM(tiles, f32),
-            scratch_shapes=[pltpu.VMEM((2,) + table, f32), pltpu.VMEM((1, ROWS, LANES), f32)],
+            scratch_shapes=[
+                pltpu.VMEM((5 if reverse else 2,) + table, f32),
+                pltpu.VMEM(params, f32),
+                pltpu.VMEM(params, f32),
+                pltpu.VMEM(tiles, f32),
+                pltpu.VMEM(state, f32),
+                pltpu.VMEM(tiles, f32),
+                pltpu.SemaphoreType.DMA((2,)),
+                pltpu.SemaphoreType.DMA((STRIPS, 3)),
+            ],
             cost_estimate=pl.CostEstimate(
                 flops=1 << 24, bytes_accessed=16 << 20, transcendentals=0
             ),
             name="behind" if reverse else "ahead",
-        )(rates, residues, one, two, enter)
-
-    conv = inner(key_rows, value_rows, enter_ahead, False)
+        )(rates, residues, xs, enter)
+
+    conv = inner(product, enter_ahead, False)
     arrived, conv = lax.optimization_barrier((arrived, conv))
     place = lax.axis_index(ALL).astype(jnp.int32).reshape(1)
     carries = pl.pallas_call(
@@ -440,7 +506,7 @@
         name="carry",
     )(place, rates, arrived)
     back = lax.all_to_all(carries, ALL, 0, 0, tiled=True)
-    flowing = inner(upstream, query_rows, enter_behind, True)
+    flowing = inner(gated, enter_behind, True)
     back, flowing = lax.optimization_barrier((back, flowing))
     rows = back[:, 0, 4 * LANES :].reshape(STRIPS, PAIRS, MODES, LANES)
     count = STRIPS // 2

time: 74.3 us -> 73.4 us (0.988)
  Pallas kernels: 31.1 us -> 26 us
  waiting for transfers between devices: 12.6 us -> 17.5 us
  starting transfers between devices: 28.6 us -> 27.3 us
  other arithmetic: 0.63 us -> 1.42 us
    pallas_call x3, Pallas kernels: 21.7 us -> 16.5 us  [the longest x2 11.3 us: inner(): pl.pallas_call(functools.partial(inner_kernel, reverse), in_specs=[hbm] *...]
    all_to_all x1, waiting for transfers between devices: 6.43 us -> 9.47 us  [local(): arrived = lax.all_to_all(send, ALL, 0, 0, tiled=True)]
    all_to_all x1, waiting for transfers between devices: 6.12 us -> 8.01 us  [local(): back = lax.all_to_all(carries, ALL, 0, 0, tiled=True)]
    select_n x0 -> x1, other arithmetic: none -> 0.79 us  [local(): jnp.where(first, lax.pad(decay_rate, zero, below), lax.pad(residue, zero,...]
    ppermute x2 -> x1, starting transfers between devices: 2.64 us -> 2.46 us  [local(): other = lax.ppermute(mine, 'fsdp', swap)]
  transfers between devices with their start and end apart: 5 -> 4, of which waited for: 2 -> 2; matrix products, arithmetic and copies ran while one was open for 0% -> 0% of each run, Pallas kernels for 32% -> 27%
where the time goes in v3:
time: 73.4 us; the launch traced here: 73 us
  starting transfers between devices  27.3 us (37%)
  Pallas kernels  26 us (35%)
  waiting for transfers between devices  17.5 us (24%)
  other arithmetic  1.42 us (2%)
  between operations  0.78 us (1%)
    all_to_all x1, starting transfers between devices, local(): arrived = lax.all_to_all(send, ALL, 0, 0, tiled=True)  14.6 us
    pallas_call x2, Pallas kernels, inner(): pl.pallas_call(functools.partial(inner_kernel, reverse), in_specs=[hbm] *...  11.3 us
    all_to_all x1, waiting for transfers between devices, local(): arrived = lax.all_to_all(send, ALL, 0, 0, tiled=True)  9.47 us
    all_to_all x1, waiting for transfers between devices, local(): back = lax.all_to_all(carries, ALL, 0, 0, tiled=True)  8.01 us
    all_to_all x1, starting transfers between devices, local(): back = lax.all_to_all(carries, ALL, 0, 0, tiled=True)  6.61 us
    pallas_call x1, Pallas kernels, local(): pl.pallas_call(finish_kernel, in_specs=[vmem] * 2 + [hbm] * 5 + [vmem], o...  5.59 us
    pallas_call x1, Pallas kernels, local(): pl.pallas_call(summarize_kernel, in_specs=[smem] + [vmem] * 4, out_specs=...  5.22 us
    ppermute x1, starting transfers between devices, local(): rows = rows + lax.ppermute(rows, 'ch', swap)  3.63 us
  transfers between devices with their start and end apart: 4, of which 2 were waited for; matrix products, arithmetic and copies ran while one was open for 0% of the time, Pallas kernels for 27%

profile of v3, /device:TPU:1, one launch (start us, length us, event | category | flops | bytes accessed | tf_op | source)
XLA Modules:
  0.0 73.0 jit_solution(17939688221838771967)
XLA Ops:
  0.6 0.8 %pad_select_fusion.mine_ref = f32[16,256]{1,0:T(8,128)S(1)} fusion(f32[8,256]{1,0:T(8,128)} %param.11, f32[8,256]{1,0:T(8,128)} %param.10, pred[16]{0:T(512)(128)(4,1)S(1)} %iota_compare_fusion), kind=kLoop, calls=%fused_computation.1 | loop fusion | flops 4096 | bytes 32784 | tf_op jit(solution)/shard_map/jit(_where)/select_n | solution.py:423
  1.4 2.5 %collective-permute-start = (f32[16,256]{1,0:T(8,128)S(1)}, f32[16,256]{1,0:T(8,128)S(1)}, u32[]{:S(2)}, u32[]{:S(2)}) collective-permute-start(f32[16,256]{1,0:T(8,128)S(1)} %pad_select_fusion.mine_ref), channel_id=1, source_target_pairs={{0,1},{1,0},{2,3},{3,2},{4,5},{5,4},{6,7},{7,6},{8,9},{9,8},{10,11... | collective-permute-start | bytes 49160 | tf_op jit(solution)/shard_map/ppermute | solution.py:424
  3.9 2.7 %prepare.1 = (f32[4,8,128,128]{3,2,1,0:T(8,128)S(1)}, f32[4,8,128,128]{3,2,1,0:T(8,128)S(1)}) custom-call(bf16[128,4096]{1,0:T(8,128)(2,1)} %q_hbm.1, bf16[128,4096]{1,0:T(8,128)(2,1)} %k_hbm.3, bf16[128,4096]{1,0:T(8,128)(2,1)} %v_hbm.3, bf16[128,4096]{1,0:T(8,128)(2,1)} %u_hbm.3), custom_call_target="tpu_custom_call" | custom-call | flops 4194304 | bytes 12582912 | tf_op jit(solution)/shard_map/prepare/pallas_call | solution.py:439
  6.6 0.0 collective-permute-done.other_ref
  6.6 5.2 %summarize.1 = (f32[128,1,640]{2,1,0:T(1,128)}, f32[4,8,8,8,128]{4,3,2,1,0:T(8,128)}, f32[4,8,8,8,128]{4,3,2,1,0:T(8,128)}, f32[32,128]{1,0:T(8,128)}, f32[32,12...) custom-call(s32[1]{0:T(128)} %bitcast.half_ref, f32[16,256]{1,0:T(8,128)S(1)} %pad_select_fusion.mine_ref, ...), custom_call_target="tpu_custom_call" | custom-call | tf_op jit(solution)/shard_map/summarize/pallas_call | solution.py:449
  11.8 14.6 %all-to-all-start = ((f32[128,1,640]{2,1,0:T(1,128)}), f32[128,1,640]{2,1,0:T(1,128)S(1)}, u32[]{:S(2)}, u32[]{:S(2)}) async-start(f32[128,1,640]{2,1,0:T(1,128)} %get-tuple-element.24), calls=%async_computation | async-start | bytes 655360 | tf_op jit(solution)/shard_map/all_to_all | solution.py:472
  26.5 0.0 copy-start
  26.5 5.4 %ahead.1.conv_hbm = f32[4,8,128,128]{3,2,1,0:T(8,128)} custom-call(f32[32,128]{1,0:T(8,128)} %get-tuple-element.22.rates_hbm.rates_ref, f32[32,128]{1,0:T(8,128)} %get-tuple-element.23.residues_hbm.residues_ref, f32[4,8,128,128]{3,2,1,0:T(8,128)} %get-tuple-element.25.xs_hbm, f32[4,8,8,8,128]{4,3,2,1,0:T(8,128)} %get-tuple-element.26.enter_hbm), custom_call_target="tpu_custom_call" | custom-call | flops 16777216 | bytes 16777216 | tf_op jit(solution)/shard_map/ahead/pallas_call | solution.py:475
  31.9 9.5 %all-to-all-done.x_ref = f32[128,1,640]{2,1,0:T(1,128)S(1)} async-done(((f32[128,1,640]{2,1,0:T(1,128)}), f32[128,1,640]{2,1,0:T(1,128)S(1)}, u32[]{:S(2)}, u32[]{:S(2)}) %all-to-all-start) | async-done | bytes 327712 | tf_op jit(solution)/shard_map/all_to_all | solution.py:472
  41.4 0.0 copy-done
  41.4 1.2 %carry.1 = f32[128,1,640]{2,1,0:T(1,128)} custom-call(s32[1]{0:T(128)} %bitcast.1.where_ref, f32[32,128]{1,0:T(8,128)S(1)} %copy-done, f32[128,1,640]{2,1,0:T(1,128)S(1)} %all-to-all-done.x_ref), custom_call_target="tpu_custom_call" | custom-call | tf_op jit(solution)/shard_map/carry/pallas_call | solution.py:499
  42.6 6.6 %all-to-all-start.1 = ((f32[128,1,640]{2,1,0:T(1,128)}), f32[128,1,640]{2,1,0:T(1,128)S(1)}, u32[]{:S(2)}, u32[]{:S(2)}) async-start(f32[128,1,640]{2,1,0:T(1,128)} %carry.1), calls=%async_computation.1 | async-start | bytes 655360 | tf_op jit(solution)/shard_map/all_to_all | solution.py:508
  49.2 0.0 copy-start.1
  49.2 0.0 copy-start.2
  49.2 5.8 %behind.1.flow_hbm = f32[4,8,128,128]{3,2,1,0:T(8,128)} custom-call(f32[32,128]{1,0:T(8,128)} %get-tuple-element.22.rates_hbm.rates_ref, f32[32,128]{1,0:T(8,128)} %get-tuple-element.23.residues_hbm.residues_ref, f32[4,8,128,128]{3,2,1,0:T(8,128)} %get-tuple-element.29.xs_hbm, f32[4,8,8,8,128]{4,3,2,1,0:T(8,128)} %get-tuple-element.30.enter_hbm), custom_call_target="tpu_custom_call" | custom-call | flops 16777216 | bytes 16777216 | tf_op jit(solution)/shard_map/behind/pallas_call | solution.py:475
  55.1 8.0 %all-to-all-done.1.in_ref = f32[128,1,640]{2,1,0:T(1,128)S(1)} async-done(((f32[128,1,640]{2,1,0:T(1,128)}), f32[128,1,640]{2,1,0:T(1,128)S(1)}, u32[]{:S(2)}, u32[]{:S(2)}) %all-to-all-start.1) | async-done | bytes 327712 | tf_op jit(solution)/shard_map/all_to_all | solution.py:508
  63.2 0.0 copy-start.3
  63.2 3.6 %collective-permute-start.1 = (f32[2,8,128]{2,1,0:T(8,128)S(1)}, f32[2,8,128]{2,1,0:T(8,128)S(1)}, u32[]{:S(2)}, u32[]{:S(2)}) collective-permute-start(f32[2,8,128]{2,1,0:T(8,128)S(1)} %dynamic-slice_reduce_fusion), channel_id=1, source_target_pairs={{0,2},{2,0},{1,3},{3,1},{4,6},{6,4},{5,7},{7,5},{8,10},{10,8},{9,1... | collective-permute-start | bytes 24584 | tf_op jit(solution)/shard_map/ppermute | solution.py:514
  66.8 0.0 copy-done.1
  66.8 0.0 copy-done.2
  66.8 5.6 %finish.1 = (bf16[128,4096]{1,0:T(8,128)(2,1)}, bf16[128,4096]{1,0:T(8,128)(2,1)}, bf16[128,4096]{1,0:T(8,128)(2,1)}) custom-call(f32[32,128]{1,0:T(8,128)S(1)} %copy-done.1, f32[32,128]{1,0:T(8,128)S(1)} %copy-done.2, bf16[128,4096]{1,0:T(8,128)(2,1)} %k_hbm.3, bf16[128,4096]{1,0:T(8,128)(2,1)} %v_hbm.3, bf16[128,4096]{1,0:T(8,128)(2,1)} %u_hbm.3, ...), custom_call_target="tpu_custom_call" | custom-call | tf_op jit(solution)/shard_map/finish/pallas_call | solution.py:519
  72.4 0.0 collective-permute-done.1
  72.4 0.0 copy-done.3
  72.4 0.6 fusion
  (3 shorter events, 0.1 us)
Async XLA Ops:
  1.4 5.2 %collective-permute-start = (f32[16,256]{1,0:T(8,128)S(1)}, f32[16,256]{1,0:T(8,128)S(1)}, u32[]{:S(2)}, u32[]{:S(2)}) collective-permute-start(f32[16,256]{1,0:T(8,128)S(1)} %pad_select_fusion.mine_ref), channel_id=1, source_target_pairs={{0,1},{1,0},{2,3},{3,2},{4,5},{5,4},{6,7},{7,6},{8,9},{9,8},{10,11... | collective-permute-start | bytes 49160 | tf_op jit(solution)/shard_map/ppermute | solution.py:424
  11.8 29.6 %all-to-all-start = ((f32[128,1,640]{2,1,0:T(1,128)}), f32[128,1,640]{2,1,0:T(1,128)S(1)}, u32[]{:S(2)}, u32[]{:S(2)}) async-start(f32[128,1,640]{2,1,0:T(1,128)} %get-tuple-element.24), calls=%async_computation | async-start | bytes 655360 | tf_op jit(solution)/shard_map/all_to_all | solution.py:472
  26.5 14.9 %copy-start = (f32[32,128]{1,0:T(8,128)S(1)}, f32[32,128]{1,0:T(8,128)}, u32[]{:S(2)}) copy-start(f32[32,128]{1,0:T(8,128)} %get-tuple-element.22.rates_hbm.rates_ref) | copy-start | bytes 49156
  42.6 20.5 %all-to-all-start.1 = ((f32[128,1,640]{2,1,0:T(1,128)}), f32[128,1,640]{2,1,0:T(1,128)S(1)}, u32[]{:S(2)}, u32[]{:S(2)}) async-start(f32[128,1,640]{2,1,0:T(1,128)} %carry.1), calls=%async_computation.1 | async-start | bytes 655360 | tf_op jit(solution)/shard_map/all_to_all | solution.py:508
  49.2 17.6 %copy-start.1 = (f32[32,128]{1,0:T(8,128)S(1)}, f32[32,128]{1,0:T(8,128)}, u32[]{:S(2)}) copy-start(f32[32,128]{1,0:T(8,128)} %get-tuple-element.22.rates_hbm.rates_ref) | copy-start | bytes 49156
  49.2 17.6 %copy-start.2 = (f32[32,128]{1,0:T(8,128)S(1)}, f32[32,128]{1,0:T(8,128)}, u32[]{:S(2)}) copy-start(f32[32,128]{1,0:T(8,128)} %get-tuple-element.23.residues_hbm.residues_ref) | copy-start | bytes 49156
  63.2 9.3 %copy-start.3 = (f32[8,256]{1,0:T(8,128)S(1)}, f32[8,256]{1,0:T(8,128)}, u32[]{:S(2)}) copy-start(f32[8,256]{1,0:T(8,128)} %param.10) | copy-start | bytes 24580
  63.2 9.2 %collective-permute-start.1 = (f32[2,8,128]{2,1,0:T(8,128)S(1)}, f32[2,8,128]{2,1,0:T(8,128)S(1)}, u32[]{:S(2)}, u32[]{:S(2)}) collective-permute-start(f32[2,8,128]{2,1,0:T(8,128)S(1)} %dynamic-slice_reduce_fusion), channel_id=1, source_target_pairs={{0,2},{2,0},{1,3},{3,1},{4,6},{6,4},{5,7},{7,5},{8,10},{10,8},{9,1... | collective-permute-start | bytes 24584 | tf_op jit(solution)/shard_map/ppermute | solution.py:514

commit v4 on v3

--- a/solution.py
+++ b/solution.py
@@ -6,6 +6,7 @@
 from jax import lax
 from jax.experimental import pallas as pl
 from jax.experimental.pallas import tpu as pltpu
+from jax.sharding import Mesh
 from jax.sharding import PartitionSpec as P
 
 TOKENS = 16384
@@ -21,8 +22,13 @@
 PAIRS = BLOCKS // 2
 WIDTH = BLOCKS * FILTERS
 SHARDS = TOKENS // ROWS
-PACKET = 5 * LANES
-ALL = ("ctx", "fsdp")
+LINE = MODES
+LINES = SHARDS // LINE
+BACK = STRIPS * BLOCKS
+TERMS = 2 * BACK
+DEPTH = TERMS + SUB
+ALONG = ("zh", "fsdp")
+ALL = ("yx",) + ALONG
 f32 = jnp.float32
 bf16 = jnp.bfloat16
 
@@ -31,16 +37,8 @@
     return lax.broadcasted_iota(jnp.int32, (SUB, LANES), 0)
 
 
-def owner(strip, pair, n):
-    return (strip * PAIRS + pair) * MODES + n
-
-
 def lanes_of(at):
     return pl.ds(pl.multiple_of(at * LANES, LANES), LANES)
-
-
-def piece(r):
-    return pl.ds(r * LANES, LANES)
 
 
 def spread(ref, at, natural):
@@ -138,12 +136,18 @@
     for_filters(make)
 
     def sent(strip):
-        at = pl.ds(strip * PAIRS * MODES, PAIRS * MODES)
-        return [
-            pltpu.make_async_copy(send_ref.at[at], send_hbm.at[at], sems.at[strip, 0]),
-            pltpu.make_async_copy(cf_ref.at[strip], cf_hbm.at[strip], sems.at[strip, 1]),
-            pltpu.make_async_copy(cb_ref.at[strip], cb_hbm.at[strip], sems.at[strip, 2]),
-        ]
+        ahead_at = pl.ds(pl.multiple_of(strip * BLOCKS, BLOCKS), BLOCKS)
+        behind_at = pl.ds(pl.multiple_of(BACK + strip * BLOCKS, BLOCKS), BLOCKS)
+        pairs = (
+            (send_ref.at[:, ahead_at], send_hbm.at[:, ahead_at]),
+            (send_ref.at[:, behind_at], send_hbm.at[:, behind_at]),
+            (cf_ref.at[strip], cf_hbm.at[strip]),
+            (cb_ref.at[strip], cb_hbm.at[strip]),
+        )
+        return [pltpu.make_async_copy(a, b, sems.at[strip, i]) for i, (a, b) in enumerate(pairs)]
+
+    for n in range(MODES):
+        send_ref[n, TERMS:, :] = jnp.zeros((SUB, LANES), f32)
 
     def strip_body(strip, _):
         base = strip * MODES
@@ -183,10 +187,10 @@
                         moved = pltpu.roll(ahead[n], 1 << step, 0)
                         ahead[n] = ahead[n] + tab[1 + step, base + n] * moved
                 for n in range(MODES):
-                    place = owner(strip, pair, n)
-                    send_ref[place, :, piece(odd)] = ahead[n][SUB - 1 :, :]
+                    row = strip * BLOCKS + 2 * pair + odd
+                    send_ref[n, pl.ds(row, 1), :] = ahead[n][SUB - 1 :, :]
                     first = jnp.sum(tab[4, base + n] * behind[n], axis=0, keepdims=True)
-                    send_ref[place, :, piece(2 + odd)] = first
+                    send_ref[n, pl.ds(BACK + row, 1), :] = first
                     enter = jnp.where(s >= 1, pltpu.roll(ahead[n], 1, 0), 0.0)
                     cf_ref[strip, 2 * pair + odd, n] = enter
                     cb_ref[strip, 2 * pair + odd, n] = behind[n]
@@ -200,18 +204,19 @@
             for lag in reversed(range(HALF - 1)):
                 term = decay * term + lags[lag]
             term = jnp.sum(term + decay * joins[n], axis=0, keepdims=True)
-            for pair in range(PAIRS):
-                row = term if pair == 0 else jnp.zeros((1, LANES), f32)
-                send_ref[owner(strip, pair, n), :, piece(4)] = row
+            send_ref[n, pl.ds(TERMS + strip, 1), :] = term
         for copy in sent(strip):
             copy.start()
         return 0
 
     lax.fori_loop(0, STRIPS, strip_body, 0)
+    tail = pl.ds(TERMS, SUB)
+    last = pltpu.make_async_copy(send_ref.at[:, tail], send_hbm.at[:, tail], early_sems.at[4])
+    last.start()
     for strip in range(STRIPS):
         for copy in sent(strip):
             copy.wait()
-    for copy in stored:
+    for copy in [last] + stored:
         copy.wait()
 
 
@@ -284,40 +289,70 @@
         leaving(strip).wait()
 
 
-def carry_kernel(where_ref, rates_ref, x_ref, y_hbm, y_ref, sem):
-    place = where_ref[0]
-    at = (place // (PAIRS * MODES)) * MODES + place % MODES
-    log_decay = rates_ref[pl.ds(at, 1), :] / TOKENS
-    across = jnp.exp(-log_decay * ROWS)
-    zero = jnp.zeros((1, LANES), f32)
-
-    def step(i, carried):
-        a0, a1, b0, b1, cross, terms = carried
-        y_ref[i, :, piece(0)] = a0
-        y_ref[i, :, piece(1)] = a1
-        cross = cross + (a0 * x_ref[i, :, piece(2)] + a1 * x_ref[i, :, piece(3)])
-        terms = terms + x_ref[i, :, piece(4)]
-        back = SHARDS - 1 - i
-        y_ref[back, :, piece(2)] = b0
-        y_ref[back, :, piece(3)] = b1
-        return (
-            across * a0 + x_ref[i, :, piece(0)],
-            across * a1 + x_ref[i, :, piece(1)],
-            across * b0 + x_ref[back, :, piece(2)],
-            across * b1 + x_ref[back, :, piece(3)],
-            cross,
-            terms,
-        )
-
-    carried = lax.fori_loop(0, SHARDS, step, (zero,) * 6, unroll=8)
-    row = jnp.exp(-log_decay) * carried[4] + carried[5]
-
-    def fill(i, _):
-        y_ref[i, :, piece(4)] = row
-        return 0
-
-    lax.fori_loop(0, SHARDS, fill, 0, unroll=16)
-    copy = pltpu.make_async_copy(y_ref, y_hbm, sem)
+def tile_rows(first):
+    return pl.ds(first, SUB)
+
+
+def line_kernel(where_ref, rates_ref, x_ref, y_hbm, y_ref, sems):
+    n = where_ref[0]
+    y_ref[TERMS:, :] = jnp.zeros((SUB, LANES), f32)
+    for strip in range(STRIPS):
+        log_decay = row_of(rates_ref, strip * MODES + n) / TOKENS
+        across = jnp.exp(-log_decay * ROWS)
+        forth, back = tile_rows(strip * BLOCKS), tile_rows(BACK + strip * BLOCKS)
+        state, cross, terms = x_ref[0, forth, :], None, None
+        for z in range(1, LINE):
+            product = state * x_ref[z, back, :]
+            cross = product if cross is None else cross + product
+            state = across * state + x_ref[z, forth, :]
+        y_ref[forth, :] = state
+        state = x_ref[LINE - 1, back, :]
+        for z in reversed(range(LINE - 1)):
+            state = across * state + x_ref[z, back, :]
+        y_ref[back, :] = state
+        row = pl.ds(TERMS + strip, 1)
+        terms = total([x_ref[z, row, :] for z in range(LINE)])
+        cross = jnp.sum(jnp.exp(-log_decay) * cross, axis=0, keepdims=True)
+        y_ref[row, :] = terms + cross
+    copies = [pltpu.make_async_copy(y_ref, y_hbm.at[g], sems.at[g]) for g in range(LINES)]
+    for copy in copies:
+        copy.start()
+    for copy in copies:
+        copy.wait()
+
+
+def join_kernel(where_ref, rates_ref, x_ref, y_ref, out_hbm, out_ref, sem):
+    n = where_ref[0]
+    line = jnp.broadcast_to(where_ref[1], (SUB, LANES))
+    for z in range(LINE):
+        out_ref[z, TERMS:, :] = jnp.zeros((SUB, LANES), f32)
+    for strip in range(STRIPS):
+        log_decay = row_of(rates_ref, strip * MODES + n) / TOKENS
+        across = jnp.exp(-log_decay * ROWS)
+        leap = jnp.exp(-log_decay * (ROWS * LINE))
+        forth, back = tile_rows(strip * BLOCKS), tile_rows(BACK + strip * BLOCKS)
+        zero = jnp.zeros((SUB, LANES), f32)
+        state, enter, cross = zero, zero, zero
+        for g in range(LINES):
+            enter = jnp.where(line == g, state, enter)
+            cross = cross + state * y_ref[g, back, :]
+            state = leap * state + y_ref[g, forth, :]
+        for z in range(LINE):
+            out_ref[z, forth, :] = enter
+            enter = across * enter + x_ref[z, forth, :]
+        state, enter = zero, zero
+        for g in reversed(range(LINES)):
+            enter = jnp.where(line == g, state, enter)
+            state = leap * state + y_ref[g, back, :]
+        for z in reversed(range(LINE)):
+            out_ref[z, back, :] = enter
+            enter = across * enter + x_ref[z, back, :]
+        row = pl.ds(TERMS + strip, 1)
+        terms = total([y_ref[g, row, :] for g in range(LINES)])
+        cross = jnp.sum(jnp.exp(-log_decay) * cross, axis=0, keepdims=True)
+        for z in range(LINE):
+            out_ref[z, row, :] = terms + cross
+    copy = pltpu.make_async_copy(out_ref, out_hbm, sem)
     copy.start()
     copy.wait()
 
@@ -373,9 +408,9 @@
                 base = strip * MODES
                 cols = lanes_of(blk * STRIPS + strip)
                 leap = [tab[0, base + n] for n in range(MODES)]
-                places = [owner(strip, pair, n) for n in range(MODES)]
+                row = strip * BLOCKS + blk
                 state = [
-                    tab[1, base + n] * in_ref[places[n], :, piece(odd)] for n in range(MODES)
+                    tab[1, base + n] * in_ref[n, pl.ds(row, 1), :] for n in range(MODES)
                 ]
                 for i in range(ROWS // 16):
                     parts = []
@@ -386,7 +421,7 @@
                     conv = conv_ref[strip, blk, at, :] + jnp.concatenate(parts, axis=0)
                     gq_ref[at, cols] = (u_ref[at, cols].astype(f32) * conv).astype(bf16)
                 state = [
-                    tab[2, base + n] * in_ref[places[n], :, piece(2 + odd)] for n in range(MODES)
+                    tab[2, base + n] * in_ref[n, pl.ds(BACK + row, 1), :] for n in range(MODES)
                 ]
                 for i in reversed(range(ROWS // 16)):
                     parts = []
@@ -426,7 +461,7 @@
     smem = pl.BlockSpec(memory_space=pltpu.SMEM)
     hbm = pl.BlockSpec(memory_space=pltpu.HBM)
     limit = pltpu.CompilerParams(vmem_limit_bytes=16 << 20)
-    packet = (SHARDS, 1, PACKET)
+    packet = (LINE, DEPTH, LANES)
     packets = pltpu.HBM(packet, f32)
     tiles = (STRIPS, BLOCKS, ROWS, LANES)
     state = (STRIPS, BLOCKS, MODES, SUB, LANES)
@@ -463,13 +498,13 @@
             pltpu.VMEM(state, f32),
             pltpu.VMEM(params, f32),
             pltpu.VMEM(params, f32),
-            pltpu.SemaphoreType.DMA((STRIPS, 3)),
-            pltpu.SemaphoreType.DMA((4,)),
+            pltpu.SemaphoreType.DMA((STRIPS, 4)),
+            pltpu.SemaphoreType.DMA((5,)),
         ],
         compiler_params=limit,
         name="summarize",
     )(half.astype(jnp.int32).reshape(1), mine, other, ps, gs)
-    arrived = lax.all_to_all(send, ALL, 0, 0, tiled=True)
+    arrived = lax.all_to_all(send, ALONG, 0, 0, tiled=True)
 
     def inner(xs, enter, reverse):
         return pl.pallas_call(
@@ -495,24 +530,33 @@
 
     conv = inner(product, enter_ahead, False)
     arrived, conv = lax.optimization_barrier((arrived, conv))
-    place = lax.axis_index(ALL).astype(jnp.int32).reshape(1)
+    where = jnp.stack([lax.axis_index(ALONG), lax.axis_index("yx")]).astype(jnp.int32)
+    lines = pl.pallas_call(
+        line_kernel,
+        in_specs=[smem] + [vmem] * 2,
+        out_specs=hbm,
+        out_shape=pltpu.HBM((LINES, DEPTH, LANES), f32),
+        scratch_shapes=[pltpu.VMEM((DEPTH, LANES), f32), pltpu.SemaphoreType.DMA((LINES,))],
+        compiler_params=limit,
+        name="line",
+    )(where, rates, arrived)
+    totals = lax.all_to_all(lines, "yx", 0, 0, tiled=True)
+    flowing = inner(gated, enter_behind, True)
+    totals, flowing = lax.optimization_barrier((totals, flowing))
     carries = pl.pallas_call(
-        carry_kernel,
-        in_specs=[smem] + [vmem] * 2,
+        join_kernel,
+        in_specs=[smem] + [vmem] * 3,
         out_specs=hbm,
         out_shape=packets,
         scratch_shapes=[pltpu.VMEM(packet, f32), pltpu.SemaphoreType.DMA],
         compiler_params=limit,
-        name="carry",
-    )(place, rates, arrived)
-    back = lax.all_to_all(carries, ALL, 0, 0, tiled=True)
-    flowing = inner(gated, enter_behind, True)
-    back, flowing = lax.optimization_barrier((back, flowing))
-    rows = back[:, 0, 4 * LANES :].reshape(STRIPS, PAIRS, MODES, LANES)
+        name="join",
+    )(where, rates, arrived, totals)
+    back = lax.all_to_all(carries, ALONG, 0, 0, tiled=True)
     count = STRIPS // 2
-    rows = lax.dynamic_slice_in_dim(rows, half * count, count, 0).sum(axis=1)
+    rows = lax.dynamic_slice_in_dim(back, TERMS + half * count, count, 1)
+    rows = rows.reshape(MODES, count * LANES)
     rows = rows + lax.ppermute(rows, "ch", swap)
-    rows = rows.transpose(1, 0, 2).reshape(MODES, count * LANES)
     gain = jnp.sqrt((1.0 + decay_rate) / TOKENS)
     residue_grad = gain * rows / math.sqrt(TOKENS)
     conv, flowing = in_hbm(conv, flowing)
@@ -545,7 +589,7 @@
     params = P(None, "fsdp")
     return jax.shard_map(
         local,
-        mesh=mesh,
+        mesh=Mesh(mesh.devices.reshape(LINES, LINE // 2, 2, 2), ("yx", "zh", "ch", "fsdp")),
         in_specs=(rows, rows, rows, rows, params, params),
         out_specs=(rows, rows, rows, params),
         check_vma=False,

time: 73.4 us -> 74 us (level)
  starting transfers between devices: 27.3 us -> 25.1 us
  Pallas kernels: 26 us -> 27.6 us
  waiting for transfers between devices: 17.5 us -> 18.5 us
    all_to_all x2 -> x3, starting transfers between devices: 21.2 us -> 18.6 us  [the longest x1 7.3 us: local(): arrived = lax.all_to_all(send, ALONG, 0, 0, tiled=True)]
    pallas_call x1 -> x2, Pallas kernels: 1.19 us -> 2.92 us  [the longest x1 1.53 us: local(): pl.pallas_call(line_kernel, in_specs=[smem] + [vmem] * 2, out_specs=hbm,...]
    all_to_all x2 -> x3, waiting for transfers between devices: 17.5 us -> 18.5 us  [the longest x1 9.76 us: local(): back = lax.all_to_all(carries, ALONG, 0, 0, tiled=True)]
  transfers between devices with their start and end apart: 4 -> 5, of which waited for: 2 -> 3; matrix products, arithmetic and copies ran while one was open for 0% -> 0% of each run, Pallas kernels for 27% -> 27%
where the time goes in v4:
time: 74 us; the launch traced here: 73.5 us
  Pallas kernels  27.6 us (37%)
  starting transfers between devices  25.1 us (34%)
  waiting for transfers between devices  18.5 us (25%)
  other arithmetic  1.48 us (2%)
  between operations  0.75 us (1%)
    pallas_call x2, Pallas kernels, inner(): pl.pallas_call(functools.partial(inner_kernel, reverse), in_specs=[hbm] *...  11.3 us
    all_to_all x1, waiting for transfers between devices, local(): back = lax.all_to_all(carries, ALONG, 0, 0, tiled=True)  9.76 us
    all_to_all x1, starting transfers between devices, local(): arrived = lax.all_to_all(send, ALONG, 0, 0, tiled=True)  7.3 us
    all_to_all x1, starting transfers between devices, local(): totals = lax.all_to_all(lines, 'yx', 0, 0, tiled=True)  6.77 us
    pallas_call x1, Pallas kernels, local(): pl.pallas_call(finish_kernel, in_specs=[vmem] * 2 + [hbm] * 5 + [vmem], o...  5.6 us
    all_to_all x1, waiting for transfers between devices, local(): arrived = lax.all_to_all(send, ALONG, 0, 0, tiled=True)  5.25 us
    pallas_call x1, Pallas kernels, local(): pl.pallas_call(summarize_kernel, in_specs=[smem] + [vmem] * 4, out_specs=...  5.07 us
    all_to_all x1, starting transfers between devices, local(): back = lax.all_to_all(carries, ALONG, 0, 0, tiled=True)  4.55 us
  transfers between devices with their start and end apart: 5, of which 3 were waited for; matrix products, arithmetic and copies ran while one was open for 0% of the time, Pallas kernels for 27%

profile of v4, /device:TPU:1, one launch (start us, length us, event | category | flops | bytes accessed | tf_op | source)
XLA Modules:
  0.0 73.5 jit_solution(12287123808862521488)
XLA Ops:
  0.6 0.8 %pad_select_fusion.mine_ref = f32[16,256]{1,0:T(8,128)S(1)} fusion(f32[8,256]{1,0:T(8,128)} %param.11, f32[8,256]{1,0:T(8,128)} %param.10, pred[16]{0:T(512)(128)(4,1)S(1)} %iota_compare_fusion), kind=kLoop, calls=%fused_computation | loop fusion | flops 4096 | bytes 32784 | tf_op jit(solution)/shard_map/jit(_where)/select_n | solution.py:458
  1.4 2.5 %collective-permute-start = (f32[16,256]{1,0:T(8,128)S(1)}, f32[16,256]{1,0:T(8,128)S(1)}, u32[]{:S(2)}, u32[]{:S(2)}) collective-permute-start(f32[16,256]{1,0:T(8,128)S(1)} %pad_select_fusion.mine_ref), channel_id=1, source_target_pairs={{0,1},{1,0},{2,3},{3,2},{4,5},{5,4},{6,7},{7,6},{8,9},{9,8},{10,11... | collective-permute-start | bytes 49160 | tf_op jit(solution)/shard_map/ppermute | solution.py:459
  3.9 2.7 %prepare.1 = (f32[4,8,128,128]{3,2,1,0:T(8,128)S(1)}, f32[4,8,128,128]{3,2,1,0:T(8,128)S(1)}) custom-call(bf16[128,4096]{1,0:T(8,128)(2,1)} %q_hbm.1, bf16[128,4096]{1,0:T(8,128)(2,1)} %k_hbm.3, bf16[128,4096]{1,0:T(8,128)(2,1)} %v_hbm.3, bf16[128,4096]{1,0:T(8,128)(2,1)} %u_hbm.3), custom_call_target="tpu_custom_call" | custom-call | flops 4194304 | bytes 12582912 | tf_op jit(solution)/shard_map/prepare/pallas_call | solution.py:474
  6.6 0.0 collective-permute-done.other_ref
  6.6 5.1 %summarize.1 = (f32[8,72,128]{2,1,0:T(8,128)}, f32[4,8,8,8,128]{4,3,2,1,0:T(8,128)}, f32[4,8,8,8,128]{4,3,2,1,0:T(8,128)}, f32[32,128]{1,0:T(8,128)}, f32[32,128...) custom-call(s32[1]{0:T(128)} %bitcast.half_ref, f32[16,256]{1,0:T(8,128)S(1)} %pad_select_fusion.mine_ref, ...), custom_call_target="tpu_custom_call" | custom-call | tf_op jit(solution)/shard_map/summarize/pallas_call | solution.py:484
  11.7 7.3 %all-to-all-start = ((f32[8,72,128]{2,1,0:T(8,128)}), f32[8,72,128]{2,1,0:T(8,128)S(1)}, u32[]{:S(2)}, u32[]{:S(2)}) async-start(f32[8,72,128]{2,1,0:T(8,128)} %get-tuple-element.24), calls=%async_computation | async-start | bytes 589824 | tf_op jit(solution)/shard_map/all_to_all | solution.py:507
  19.0 0.1 pad_add_fusion.where_ref
  19.0 0.0 copy-start
  19.0 5.5 %ahead.1.conv_hbm = f32[4,8,128,128]{3,2,1,0:T(8,128)} custom-call(f32[32,128]{1,0:T(8,128)} %get-tuple-element.22.rates_hbm.rates_ref, f32[32,128]{1,0:T(8,128)} %get-tuple-element.23.residues_hbm.residues_ref, f32[4,8,128,128]{3,2,1,0:T(8,128)} %get-tuple-element.25.xs_hbm, f32[4,8,8,8,128]{4,3,2,1,0:T(8,128)} %get-tuple-element.26.enter_hbm), custom_call_target="tpu_custom_call" | custom-call | flops 16777216 | bytes 16777216 | tf_op jit(solution)/shard_map/ahead/pallas_call | solution.py:510
  24.5 5.3 %all-to-all-done.x_ref = f32[8,72,128]{2,1,0:T(8,128)S(1)} async-done(((f32[8,72,128]{2,1,0:T(8,128)}), f32[8,72,128]{2,1,0:T(8,128)S(1)}, u32[]{:S(2)}, u32[]{:S(2)}) %all-to-all-start) | async-done | bytes 294944 | tf_op jit(solution)/shard_map/all_to_all | solution.py:507
  29.8 0.0 copy-done
  29.8 1.5 %line.1 = f32[16,72,128]{2,1,0:T(8,128)} custom-call(s32[2]{0:T(128)S(1)} %pad_add_fusion.where_ref, f32[32,128]{1,0:T(8,128)S(1)} %copy-done, f32[8,72,128]{2,1,0:T(8,128)S(1)} %all-to-all-done.x_ref), custom_call_target="tpu_custom_call" | custom-call | tf_op jit(solution)/shard_map/line/pallas_call | solution.py:534
  31.3 6.8 %all-to-all-start.1 = ((f32[16,72,128]{2,1,0:T(8,128)}), f32[16,72,128]{2,1,0:T(8,128)S(1)}, u32[]{:S(2)}, u32[]{:S(2)}) async-start(f32[16,72,128]{2,1,0:T(8,128)} %line.1), calls=%async_computation.1 | async-start | bytes 1179648 | tf_op jit(solution)/shard_map/all_to_all | solution.py:543
  38.1 0.0 copy-start.1
  38.1 0.0 copy-start.2
  38.1 5.8 %behind.1.flow_hbm = f32[4,8,128,128]{3,2,1,0:T(8,128)} custom-call(f32[32,128]{1,0:T(8,128)} %get-tuple-element.22.rates_hbm.rates_ref, f32[32,128]{1,0:T(8,128)} %get-tuple-element.23.residues_hbm.residues_ref, f32[4,8,128,128]{3,2,1,0:T(8,128)} %get-tuple-element.29.xs_hbm, f32[4,8,8,8,128]{4,3,2,1,0:T(8,128)} %get-tuple-element.30.enter_hbm), custom_call_target="tpu_custom_call" | custom-call | flops 16777216 | bytes 16777216 | tf_op jit(solution)/shard_map/behind/pallas_call | solution.py:510
  43.9 3.5 %all-to-all-done.1.y_ref = f32[16,72,128]{2,1,0:T(8,128)S(1)} async-done(((f32[16,72,128]{2,1,0:T(8,128)}), f32[16,72,128]{2,1,0:T(8,128)S(1)}, u32[]{:S(2)}, u32[]{:S(2)}) %all-to-all-start.1) | async-done | bytes 589856 | tf_op jit(solution)/shard_map/all_to_all | solution.py:543
  47.5 0.0 copy-done.1
  47.5 1.4 %join.1 = f32[8,72,128]{2,1,0:T(8,128)} custom-call(s32[2]{0:T(128)S(1)} %pad_add_fusion.where_ref, f32[32,128]{1,0:T(8,128)S(1)} %copy-done.1, f32[8,72,128]{2,1,0:T(8,128)S(1)} %all-to-all-done.x_ref, f32[16,72,128]{2,1,0:T(8,128)S(1)} %all-to-all-done.1.y_ref), custom_call_target="tpu_custom_call" | custom-call | tf_op jit(solution)/shard_map/join/pallas_call | solution.py:546
  48.9 4.6 %all-to-all-start.2 = ((f32[8,72,128]{2,1,0:T(8,128)}), f32[8,72,128]{2,1,0:T(8,128)S(1)}, u32[]{:S(2)}, u32[]{:S(2)}) async-start(f32[8,72,128]{2,1,0:T(8,128)} %join.1), calls=%async_computation.2 | async-start | bytes 589824 | tf_op jit(solution)/shard_map/all_to_all | solution.py:555
  53.4 9.8 %all-to-all-done.2.in_ref = f32[8,72,128]{2,1,0:T(8,128)S(1)} async-done(((f32[8,72,128]{2,1,0:T(8,128)}), f32[8,72,128]{2,1,0:T(8,128)S(1)}, u32[]{:S(2)}, u32[]{:S(2)}) %all-to-all-start.2) | async-done | bytes 294944 | tf_op jit(solution)/shard_map/all_to_all | solution.py:555
  63.2 0.0 copy-start.3
  63.2 4.1 %collective-permute-start.1 = (f32[8,256]{1,0:T(8,128)S(1)}, f32[8,256]{1,0:T(8,128)S(1)}, u32[]{:S(2)}, u32[]{:S(2)}) collective-permute-start(f32[8,256]{1,0:T(8,128)S(1)} %bitcast.10), channel_id=1, source_target_pairs={{0,2},{2,0},{1,3},{3,1},{4,6},{6,4},{5,7},{7,5},{8,10},{10,8},{9,1... | collective-permute-start | bytes 24584 | tf_op jit(solution)/shard_map/ppermute | solution.py:559
  67.3 0.0 copy-done.2
  67.3 5.6 %finish.1 = (bf16[128,4096]{1,0:T(8,128)(2,1)}, bf16[128,4096]{1,0:T(8,128)(2,1)}, bf16[128,4096]{1,0:T(8,128)(2,1)}) custom-call(f32[32,128]{1,0:T(8,128)S(1)} %copy-done.1, f32[32,128]{1,0:T(8,128)S(1)} %copy-done.2, bf16[128,4096]{1,0:T(8,128)(2,1)} %k_hbm.3, bf16[128,4096]{1,0:T(8,128)(2,1)} %v_hbm.3, bf16[128,4096]{1,0:T(8,128)(2,1)} %u_hbm.3, ...), custom_call_target="tpu_custom_call" | custom-call | tf_op jit(solution)/shard_map/finish/pallas_call | solution.py:563
  72.9 0.0 collective-permute-done.1
  72.9 0.0 copy-done.3
  72.9 0.6 multiply_multiply_fusion
  (3 shorter events, 0.0 us)
Async XLA Ops:
  1.4 5.2 %collective-permute-start = (f32[16,256]{1,0:T(8,128)S(1)}, f32[16,256]{1,0:T(8,128)S(1)}, u32[]{:S(2)}, u32[]{:S(2)}) collective-permute-start(f32[16,256]{1,0:T(8,128)S(1)} %pad_select_fusion.mine_ref), channel_id=1, source_target_pairs={{0,1},{1,0},{2,3},{3,2},{4,5},{5,4},{6,7},{7,6},{8,9},{9,8},{10,11... | collective-permute-start | bytes 49160 | tf_op jit(solution)/shard_map/ppermute | solution.py:459
  11.7 18.1 %all-to-all-start = ((f32[8,72,128]{2,1,0:T(8,128)}), f32[8,72,128]{2,1,0:T(8,128)S(1)}, u32[]{:S(2)}, u32[]{:S(2)}) async-start(f32[8,72,128]{2,1,0:T(8,128)} %get-tuple-element.24), calls=%async_computation | async-start | bytes 589824 | tf_op jit(solution)/shard_map/all_to_all | solution.py:507
  19.0 10.7 %copy-start = (f32[32,128]{1,0:T(8,128)S(1)}, f32[32,128]{1,0:T(8,128)}, u32[]{:S(2)}) copy-start(f32[32,128]{1,0:T(8,128)} %get-tuple-element.22.rates_hbm.rates_ref) | copy-start | bytes 49156
  31.3 16.2 %all-to-all-start.1 = ((f32[16,72,128]{2,1,0:T(8,128)}), f32[16,72,128]{2,1,0:T(8,128)S(1)}, u32[]{:S(2)}, u32[]{:S(2)}) async-start(f32[16,72,128]{2,1,0:T(8,128)} %line.1), calls=%async_computation.1 | async-start | bytes 1179648 | tf_op jit(solution)/shard_map/all_to_all | solution.py:543
  38.1 9.4 %copy-start.1 = (f32[32,128]{1,0:T(8,128)S(1)}, f32[32,128]{1,0:T(8,128)}, u32[]{:S(2)}) copy-start(f32[32,128]{1,0:T(8,128)} %get-tuple-element.22.rates_hbm.rates_ref) | copy-start | bytes 49156
  38.1 29.2 %copy-start.2 = (f32[32,128]{1,0:T(8,128)S(1)}, f32[32,128]{1,0:T(8,128)}, u32[]{:S(2)}) copy-start(f32[32,128]{1,0:T(8,128)} %get-tuple-element.23.residues_hbm.residues_ref) | copy-start | bytes 49156
  48.9 14.3 %all-to-all-start.2 = ((f32[8,72,128]{2,1,0:T(8,128)}), f32[8,72,128]{2,1,0:T(8,128)S(1)}, u32[]{:S(2)}, u32[]{:S(2)}) async-start(f32[8,72,128]{2,1,0:T(8,128)} %join.1), calls=%async_computation.2 | async-start | bytes 589824 | tf_op jit(solution)/shard_map/all_to_all | solution.py:555
  63.2 9.7 %copy-start.3 = (f32[8,256]{1,0:T(8,128)S(1)}, f32[8,256]{1,0:T(8,128)}, u32[]{:S(2)}) copy-start(f32[8,256]{1,0:T(8,128)} %param.10) | copy-start | bytes 24580
  63.2 9.7 %collective-permute-start.1 = (f32[8,256]{1,0:T(8,128)S(1)}, f32[8,256]{1,0:T(8,128)S(1)}, u32[]{:S(2)}, u32[]{:S(2)}) collective-permute-start(f32[8,256]{1,0:T(8,128)S(1)} %bitcast.10), channel_id=1, source_target_pairs={{0,2},{2,0},{1,3},{3,1},{4,6},{6,4},{5,7},{7,5},{8,10},{10,8},{9,1... | collective-permute-start | bytes 24584 | tf_op jit(solution)/shard_map/ppermute | solution.py:559

commit v5 on v3

--- a/solution.py
+++ b/solution.py
@@ -215,10 +215,12 @@
         copy.wait()
 
 
-def inner_kernel(
-    reverse, rates_hbm, residues_hbm, xs_hbm, enter_hbm, out_hbm,
-    tab, rates_ref, residues_ref, xs, enter_ref, out_ref, param_sems, sems,
-):
+def inner_kernel(reverse, rates_hbm, residues_hbm, xs_hbm, enter_hbm, *refs):
+    if reverse:
+        out_hbm, lead_ref = refs[:2]
+    else:
+        k_hbm, v_hbm, u_hbm, out_hbm, lead_ref, lead_k, lead_v, lead_u, late_tab = refs[:9]
+    tab, rates_ref, residues_ref, xs, enter_ref, out_ref, param_sems, sems = refs[-8:]
     params = [
         pltpu.make_async_copy(rates_hbm, rates_ref, param_sems.at[0]),
         pltpu.make_async_copy(residues_hbm, residues_ref, param_sems.at[1]),
@@ -234,11 +236,19 @@
         return pltpu.make_async_copy(out_ref.at[strip], out_hbm.at[strip], sems.at[strip, 2])
 
     s = sublane()
+    leads = []
+    if not reverse:
+        pairs = ((k_hbm, lead_k), (v_hbm, lead_v), (u_hbm, lead_u))
+        for i, (a, b) in enumerate(pairs):
+            source = a.at[:, pl.ds(0, FILTERS)]
+            leads.append(pltpu.make_async_copy(source, b, param_sems.at[2 + i]))
     for copy in params:
         copy.start()
     for strip in range(STRIPS):
         for copy in arrivals(strip):
             copy.start()
+    for copy in leads:
+        copy.start()
     for copy in params:
         copy.wait()
 
@@ -246,6 +256,11 @@
         rate = row_of(rates_ref, i)
         tab[0, i] = jnp.exp(-rate / TOKENS)
         tab[1, i] = row_of(residues_ref, i) * jnp.sqrt((1.0 + rate) / TOKENS)
+        if not reverse:
+            weight = tab[1, i]
+            late_tab[0, i] = jnp.exp(-rate / TOKENS * SUB)
+            late_tab[1, i] = weight * jnp.exp(-rate / TOKENS * (s + 1).astype(f32))
+            late_tab[2, i] = weight * jnp.exp(-rate / TOKENS * (SUB - s).astype(f32))
         for step in range(3 if reverse else 0):
             factor = jnp.exp(-rate / TOKENS * (RUN << step))
             tab[2 + step, i] = jnp.where(s < SUB - (1 << step), factor, 0.0)
@@ -277,11 +292,14 @@
 
         lax.fori_loop(0, BLOCKS, body, 0)
         leaving(strip).start()
+        lead_ref[strip] = out_ref[strip, 0]
         return 0
 
     lax.fori_loop(0, STRIPS, strip_body, 0)
     for strip in range(STRIPS):
         leaving(strip).wait()
+    for copy in leads:
+        copy.wait()
 
 
 def carry_kernel(where_ref, rates_ref, x_ref, y_hbm, y_ref, sem):
@@ -323,12 +341,11 @@
 
 
 def finish_kernel(
-    rates_ref, residues_ref, k_hbm, v_hbm, u_hbm, conv_hbm, flow_hbm, in_ref,
+    tab, k_hbm, v_hbm, u_hbm, conv_hbm, flow_hbm, in_ref,
+    lead_k, lead_v, lead_u, lead_conv, lead_flow,
     gq_hbm, gk_hbm, gv_hbm,
-    tab, k_ref, v_ref, u_ref, conv_ref, flow_ref, gq_ref, gk_ref, gv_ref, arrive_sems, sems,
+    k_ref, v_ref, u_ref, conv_ref, flow_ref, gq_ref, gk_ref, gv_ref, arrive_sems, sems,
 ):
-    s = sublane()
-
     def arrivals(blk):
         cols = pl.ds(blk * FILTERS, FILTERS)
         if not isinstance(blk, int):
@@ -342,19 +359,15 @@
             pltpu.make_async_copy(a, b, arrive_sems.at[blk, i]) for i, (a, b) in enumerate(pairs)
         ]
 
-    for blk in range(BLOCKS):
+    for blk in range(1, BLOCKS):
         for copy in arrivals(blk):
             copy.start()
-
-    def make(i):
-        rate = row_of(rates_ref, i)
-        log_decay = rate / TOKENS
-        weight = row_of(residues_ref, i) * jnp.sqrt((1.0 + rate) / TOKENS)
-        tab[0, i] = jnp.exp(-log_decay * SUB)
-        tab[1, i] = weight * jnp.exp(-log_decay * (s + 1).astype(f32))
-        tab[2, i] = weight * jnp.exp(-log_decay * (SUB - s).astype(f32))
-
-    for_filters(make)
+    lead = pl.ds(0, FILTERS)
+    for a, b in ((lead_k, k_ref), (lead_v, v_ref), (lead_u, u_ref)):
+        b[:, lead] = a[...]
+    for strip in range(STRIPS):
+        conv_ref[strip, 0] = lead_conv[strip]
+        flow_ref[strip, 0] = lead_flow[strip]
 
     def copies(blk):
         cols = pl.ds(pl.multiple_of(blk * FILTERS, FILTERS), FILTERS)
@@ -366,8 +379,11 @@
     def pair_body(pair, _):
         for odd in range(2):
             blk = 2 * pair + odd
-            for copy in arrivals(blk):
-                copy.wait()
+
+            @pl.when(blk > 0)
+            def _():
+                for copy in arrivals(blk):
+                    copy.wait()
 
             def strip_body(strip, _):
                 base = strip * MODES
@@ -471,12 +487,15 @@
     )(half.astype(jnp.int32).reshape(1), mine, other, ps, gs)
     arrived = lax.all_to_all(send, ALL, 0, 0, tiled=True)
 
-    def inner(xs, enter, reverse):
+    lead = jax.ShapeDtypeStruct((STRIPS, ROWS, LANES), f32)
+    lead_rows = jax.ShapeDtypeStruct((ROWS, FILTERS), bf16)
+
+    def inner(xs, enter, reverse, extra=(), more=()):
         return pl.pallas_call(
             functools.partial(inner_kernel, reverse),
-            in_specs=[hbm] * 4,
-            out_specs=hbm,
-            out_shape=pltpu.HBM(tiles, f32),
+            in_specs=[hbm] * (4 + len(extra)),
+            out_specs=[hbm] + [vmem] * (1 + len(more)),
+            out_shape=[pltpu.HBM(tiles, f32), lead, *more],
             scratch_shapes=[
                 pltpu.VMEM((5 if reverse else 2,) + table, f32),
                 pltpu.VMEM(params, f32),
@@ -484,16 +503,24 @@
                 pltpu.VMEM(tiles, f32),
                 pltpu.VMEM(state, f32),
                 pltpu.VMEM(tiles, f32),
-                pltpu.SemaphoreType.DMA((2,)),
+                pltpu.SemaphoreType.DMA((5,)),
                 pltpu.SemaphoreType.DMA((STRIPS, 3)),
             ],
+            compiler_params=limit,
             cost_estimate=pl.CostEstimate(
                 flops=1 << 24, bytes_accessed=16 << 20, transcendentals=0
             ),
             name="behind" if reverse else "ahead",
-        )(rates, residues, xs, enter)
-
-    conv = inner(product, enter_ahead, False)
+        )(*in_hbm(rates, residues, xs, enter), *extra)
+
+    late = jax.ShapeDtypeStruct((3,) + table, f32)
+    conv, lead_conv, lead_k, lead_v, lead_u, late_tab = inner(
+        product,
+        enter_ahead,
+        False,
+        (key_rows, value_rows, upstream),
+        (lead_rows, lead_rows, lead_rows, late),
+    )
     arrived, conv = lax.optimization_barrier((arrived, conv))
     place = lax.axis_index(ALL).astype(jnp.int32).reshape(1)
     carries = pl.pallas_call(
@@ -506,7 +533,7 @@
         name="carry",
     )(place, rates, arrived)
     back = lax.all_to_all(carries, ALL, 0, 0, tiled=True)
-    flowing = inner(gated, enter_behind, True)
+    flowing, lead_flow = inner(gated, enter_behind, True)
     back, flowing = lax.optimization_barrier((back, flowing))
     rows = back[:, 0, 4 * LANES :].reshape(STRIPS, PAIRS, MODES, LANES)
     count = STRIPS // 2
@@ -518,11 +545,10 @@
     conv, flowing = in_hbm(conv, flowing)
     grads_out = pl.pallas_call(
         finish_kernel,
-        in_specs=[vmem] * 2 + [hbm] * 5 + [vmem],
+        in_specs=[vmem] + [hbm] * 5 + [vmem] * 6,
         out_specs=[hbm] * 3,
         out_shape=[pltpu.HBM((ROWS, WIDTH), bf16)] * 3,
         scratch_shapes=[
-            pltpu.VMEM((3,) + table, f32),
             whole,
             whole,
             whole,
@@ -536,7 +562,10 @@
         ],
         compiler_params=limit,
         name="finish",
-    )(rates, residues, key_rows, value_rows, upstream, conv, flowing, back)
+    )(
+        late_tab, key_rows, value_rows, upstream, conv, flowing, back,
+        lead_k, lead_v, lead_u, lead_conv, lead_flow,
+    )
     return (*grads_out, residue_grad)
 
 

time: 73.4 us -> 73 us (level)
  transfers between devices with their start and end apart: 4 -> 4, of which waited for: 2 -> 2; matrix products, arithmetic and copies ran while one was open for 0% -> 0% of each run, Pallas kernels for 27% -> 26%
where the time goes in v5:
time: 73 us; the launch traced here: 72.7 us
  starting transfers between devices  27.3 us (37%)
  Pallas kernels  25.3 us (35%)
  waiting for transfers between devices  17.8 us (24%)
  other arithmetic  1.42 us (2%)
  between operations  0.76 us (1%)
    all_to_all x1, starting transfers between devices, local(): arrived = lax.all_to_all(send, ALL, 0, 0, tiled=True)  14.6 us
    pallas_call x2, Pallas kernels, inner(): pl.pallas_call(functools.partial(inner_kernel, reverse), in_specs=[hbm] *...  11 us
    all_to_all x1, waiting for transfers between devices, local(): arrived = lax.all_to_all(send, ALL, 0, 0, tiled=True)  9.68 us
    all_to_all x1, waiting for transfers between devices, local(): back = lax.all_to_all(carries, ALL, 0, 0, tiled=True)  8.14 us
    all_to_all x1, starting transfers between devices, local(): back = lax.all_to_all(carries, ALL, 0, 0, tiled=True)  6.6 us
    pallas_call x1, Pallas kernels, local(): pl.pallas_call(summarize_kernel, in_specs=[smem] + [vmem] * 4, out_specs=...  5.22 us
    pallas_call x1, Pallas kernels, local(): pl.pallas_call(finish_kernel, in_specs=[vmem] + [hbm] * 5 + [vmem] * 6, o...  5.22 us
    ppermute x1, starting transfers between devices, local(): rows = rows + lax.ppermute(rows, 'ch', swap)  3.63 us
  transfers between devices with their start and end apart: 4, of which 2 were waited for; matrix products, arithmetic and copies ran while one was open for 0% of the time, Pallas kernels for 26%

profile of v5, /device:TPU:1, one launch (start us, length us, event | category | flops | bytes accessed | tf_op | source)
XLA Modules:
  0.0 72.7 jit_solution(7802468581744217609)
XLA Ops:
  0.6 0.8 %pad_select_fusion.mine_ref = f32[16,256]{1,0:T(8,128)S(1)} fusion(f32[8,256]{1,0:T(8,128)} %param.11, f32[8,256]{1,0:T(8,128)} %param.10, pred[16]{0:T(512)(128)(4,1)S(1)} %iota_compare_fusion), kind=kLoop, calls=%fused_computation.1 | loop fusion | flops 4096 | bytes 32784 | tf_op jit(solution)/shard_map/jit(_where)/select_n | solution.py:439
  1.4 2.5 %collective-permute-start = (f32[16,256]{1,0:T(8,128)S(1)}, f32[16,256]{1,0:T(8,128)S(1)}, u32[]{:S(2)}, u32[]{:S(2)}) collective-permute-start(f32[16,256]{1,0:T(8,128)S(1)} %pad_select_fusion.mine_ref), channel_id=1, source_target_pairs={{0,1},{1,0},{2,3},{3,2},{4,5},{5,4},{6,7},{7,6},{8,9},{9,8},{10,11... | collective-permute-start | bytes 49160 | tf_op jit(solution)/shard_map/ppermute | solution.py:440
  3.9 2.7 %prepare.1 = (f32[4,8,128,128]{3,2,1,0:T(8,128)S(1)}, f32[4,8,128,128]{3,2,1,0:T(8,128)S(1)}) custom-call(bf16[128,4096]{1,0:T(8,128)(2,1)} %q_hbm.1, bf16[128,4096]{1,0:T(8,128)(2,1)} %k_hbm.3, bf16[128,4096]{1,0:T(8,128)(2,1)} %v_hbm.3, bf16[128,4096]{1,0:T(8,128)(2,1)} %u_hbm.3), custom_call_target="tpu_custom_call" | custom-call | flops 4194304 | bytes 12582912 | tf_op jit(solution)/shard_map/prepare/pallas_call | solution.py:455
  6.6 0.0 collective-permute-done.other_ref
  6.6 5.2 %summarize.1 = (f32[128,1,640]{2,1,0:T(1,128)}, f32[4,8,8,8,128]{4,3,2,1,0:T(8,128)}, f32[4,8,8,8,128]{4,3,2,1,0:T(8,128)}, f32[32,128]{1,0:T(8,128)}, f32[32,12...) custom-call(s32[1]{0:T(128)} %bitcast.half_ref, f32[16,256]{1,0:T(8,128)S(1)} %pad_select_fusion.mine_ref, ...), custom_call_target="tpu_custom_call" | custom-call | tf_op jit(solution)/shard_map/summarize/pallas_call | solution.py:465
  11.8 14.6 %all-to-all-start = ((f32[128,1,640]{2,1,0:T(1,128)}), f32[128,1,640]{2,1,0:T(1,128)S(1)}, u32[]{:S(2)}, u32[]{:S(2)}) async-start(f32[128,1,640]{2,1,0:T(1,128)} %get-tuple-element.35), calls=%async_computation | async-start | bytes 655360 | tf_op jit(solution)/shard_map/all_to_all | solution.py:488
  26.5 0.0 copy-start
  26.5 5.2 %ahead.1 = (f32[4,8,128,128]{3,2,1,0:T(8,128)}, f32[4,128,128]{2,1,0:T(8,128)S(1)}, bf16[128,512]{1,0:T(8,128)(2,1)S(1)}, bf16[128,512]{1,0:T(8,128)(2,1)S(1)}, ...) custom-call(f32[32,128]{1,0:T(8,128)} %get-tuple-element.30.rates_hbm.rates_ref, ...), custom_call_target="tpu_custom_call" | custom-call | flops 16777216 | bytes 16777216 | tf_op jit(solution)/shard_map/ahead/pallas_call | solution.py:494
  31.7 9.7 %all-to-all-done.x_ref = f32[128,1,640]{2,1,0:T(1,128)S(1)} async-done(((f32[128,1,640]{2,1,0:T(1,128)}), f32[128,1,640]{2,1,0:T(1,128)S(1)}, u32[]{:S(2)}, u32[]{:S(2)}) %all-to-all-start) | async-done | bytes 327712 | tf_op jit(solution)/shard_map/all_to_all | solution.py:488
  41.4 0.0 copy-done
  41.4 1.2 %carry.1 = f32[128,1,640]{2,1,0:T(1,128)} custom-call(s32[1]{0:T(128)} %bitcast.1.where_ref, f32[32,128]{1,0:T(8,128)S(1)} %copy-done, f32[128,1,640]{2,1,0:T(1,128)S(1)} %all-to-all-done.x_ref), custom_call_target="tpu_custom_call" | custom-call | tf_op jit(solution)/shard_map/carry/pallas_call | solution.py:526
  42.6 6.6 %all-to-all-start.1 = ((f32[128,1,640]{2,1,0:T(1,128)}), f32[128,1,640]{2,1,0:T(1,128)S(1)}, u32[]{:S(2)}, u32[]{:S(2)}) async-start(f32[128,1,640]{2,1,0:T(1,128)} %carry.1), calls=%async_computation.1 | async-start | bytes 655360 | tf_op jit(solution)/shard_map/all_to_all | solution.py:535
  49.2 5.7 %behind.1 = (f32[4,8,128,128]{3,2,1,0:T(8,128)}, f32[4,128,128]{2,1,0:T(8,128)S(1)}) custom-call(f32[32,128]{1,0:T(8,128)} %get-tuple-element.30.rates_hbm.rates_ref, f32[32,128]{1,0:T(8,128)} %get-tuple-element.31.residues_hbm, f32[4,8,128,128]{3,2,1,0:T(8,128)} %get-tuple-element.39.xs_hbm, f32[4,8,8,8,128]{4,3,2,1,0:T(8,128)} %get-tuple-element.40.enter_hbm), custom_call_target="tpu_custom_call" | custom-call | flops 16777216 | bytes 16777216 | tf_op jit(solution)/shard_map/behind/pallas_call | solution.py:494
  54.9 8.1 %all-to-all-done.1.in_ref = f32[128,1,640]{2,1,0:T(1,128)S(1)} async-done(((f32[128,1,640]{2,1,0:T(1,128)}), f32[128,1,640]{2,1,0:T(1,128)S(1)}, u32[]{:S(2)}, u32[]{:S(2)}) %all-to-all-start.1) | async-done | bytes 327712 | tf_op jit(solution)/shard_map/all_to_all | solution.py:535
  63.2 3.6 %collective-permute-start.1 = (f32[2,8,128]{2,1,0:T(8,128)S(1)}, f32[2,8,128]{2,1,0:T(8,128)S(1)}, u32[]{:S(2)}, u32[]{:S(2)}) collective-permute-start(f32[2,8,128]{2,1,0:T(8,128)S(1)} %dynamic-slice_reduce_fusion), channel_id=1, source_target_pairs={{0,2},{2,0},{1,3},{3,1},{4,6},{6,4},{5,7},{7,5},{8,10},{10,8},{9,1... | collective-permute-start | bytes 24584 | tf_op jit(solution)/shard_map/ppermute | solution.py:541
  66.8 0.0 copy-start.1
  66.8 5.2 %finish.1 = (bf16[128,4096]{1,0:T(8,128)(2,1)}, bf16[128,4096]{1,0:T(8,128)(2,1)}, bf16[128,4096]{1,0:T(8,128)(2,1)}) custom-call(f32[3,32,8,128]{3,2,1,0:T(8,128)S(1)} %get-tuple-element.34.tab, bf16[128,4096]{1,0:T(8,128)(2,1)} %k_hbm.3, bf16[128,4096]{1,0:T(8,128)(2,1)} %v_hbm.3, bf16[128,4096]{1,0:T(8,128)(2,1)} %u_hbm.3, ...), custom_call_target="tpu_custom_call" | custom-call | tf_op jit(solution)/shard_map/finish/pallas_call | solution.py:546
  72.0 0.0 collective-permute-done.1
  72.0 0.0 copy-done.1
  72.0 0.6 fusion
  (3 shorter events, 0.1 us)
Async XLA Ops:
  1.4 5.2 %collective-permute-start = (f32[16,256]{1,0:T(8,128)S(1)}, f32[16,256]{1,0:T(8,128)S(1)}, u32[]{:S(2)}, u32[]{:S(2)}) collective-permute-start(f32[16,256]{1,0:T(8,128)S(1)} %pad_select_fusion.mine_ref), channel_id=1, source_target_pairs={{0,1},{1,0},{2,3},{3,2},{4,5},{5,4},{6,7},{7,6},{8,9},{9,8},{10,11... | collective-permute-start | bytes 49160 | tf_op jit(solution)/shard_map/ppermute | solution.py:440
  11.8 29.6 %all-to-all-start = ((f32[128,1,640]{2,1,0:T(1,128)}), f32[128,1,640]{2,1,0:T(1,128)S(1)}, u32[]{:S(2)}, u32[]{:S(2)}) async-start(f32[128,1,640]{2,1,0:T(1,128)} %get-tuple-element.35), calls=%async_computation | async-start | bytes 655360 | tf_op jit(solution)/shard_map/all_to_all | solution.py:488
  26.5 14.9 %copy-start = (f32[32,128]{1,0:T(8,128)S(1)}, f32[32,128]{1,0:T(8,128)}, u32[]{:S(2)}) copy-start(f32[32,128]{1,0:T(8,128)} %get-tuple-element.30.rates_hbm.rates_ref) | copy-start | bytes 49156
  42.6 20.5 %all-to-all-start.1 = ((f32[128,1,640]{2,1,0:T(1,128)}), f32[128,1,640]{2,1,0:T(1,128)S(1)}, u32[]{:S(2)}, u32[]{:S(2)}) async-start(f32[128,1,640]{2,1,0:T(1,128)} %carry.1), calls=%async_computation.1 | async-start | bytes 655360 | tf_op jit(solution)/shard_map/all_to_all | solution.py:535
  63.2 8.9 %collective-permute-start.1 = (f32[2,8,128]{2,1,0:T(8,128)S(1)}, f32[2,8,128]{2,1,0:T(8,128)S(1)}, u32[]{:S(2)}, u32[]{:S(2)}) collective-permute-start(f32[2,8,128]{2,1,0:T(8,128)S(1)} %dynamic-slice_reduce_fusion), channel_id=1, source_target_pairs={{0,2},{2,0},{1,3},{3,1},{4,6},{6,4},{5,7},{7,5},{8,10},{10,8},{9,1... | collective-permute-start | bytes 24584 | tf_op jit(solution)/shard_map/ppermute | solution.py:541
  66.8 5.2 %copy-start.1 = (f32[8,256]{1,0:T(8,128)S(1)}, f32[8,256]{1,0:T(8,128)}, u32[]{:S(2)}) copy-start(f32[8,256]{1,0:T(8,128)} %param.10) | copy-start | bytes 24580

commit v6 on v5

--- a/solution.py
+++ b/solution.py
@@ -340,7 +340,13 @@
     copy.wait()
 
 
-def finish_kernel(
+def finish_kernel(turn, core_ref, *refs):
+    @pl.when(core_ref[0] == turn)
+    def _():
+        finish_body(*refs[:12], *refs[-13:])
+
+
+def finish_body(
     tab, k_hbm, v_hbm, u_hbm, conv_hbm, flow_hbm, in_ref,
     lead_k, lead_v, lead_u, lead_conv, lead_flow,
     gq_hbm, gk_hbm, gv_hbm,
@@ -538,34 +544,48 @@
     rows = back[:, 0, 4 * LANES :].reshape(STRIPS, PAIRS, MODES, LANES)
     count = STRIPS // 2
     rows = lax.dynamic_slice_in_dim(rows, half * count, count, 0).sum(axis=1)
-    rows = rows + lax.ppermute(rows, "ch", swap)
+    conv, flowing = in_hbm(conv, flowing)
+    core = lax.axis_index("ch").astype(jnp.int32).reshape(1)
+    shapes = [pltpu.HBM((ROWS, WIDTH), bf16)] * 3
+
+    def finish(turn, *before):
+        return pl.pallas_call(
+            functools.partial(finish_kernel, turn),
+            in_specs=[smem, vmem] + [hbm] * 5 + [vmem] * 6 + [hbm] * len(before),
+            out_specs=[hbm] * 3,
+            out_shape=shapes,
+            input_output_aliases={13 + i: i for i in range(len(before))},
+            scratch_shapes=[
+                whole,
+                whole,
+                whole,
+                pltpu.VMEM(tiles, f32),
+                pltpu.VMEM(tiles, f32),
+                whole,
+                whole,
+                whole,
+                pltpu.SemaphoreType.DMA((BLOCKS, 5)),
+                pltpu.SemaphoreType.DMA((BLOCKS, 3)),
+            ],
+            compiler_params=limit,
+            cost_estimate=pl.CostEstimate(
+                flops=1 << 24, bytes_accessed=10 << 20, transcendentals=0
+            ),
+            name=f"finish{turn}",
+        )(
+            core, late_tab, key_rows, value_rows, upstream, conv, flowing, back,
+            lead_k, lead_v, lead_u, lead_conv, lead_flow, *before,
+        )
+
+    from_first = lax.ppermute(rows, "ch", [(0, 1)])
+    early = finish(1)
+    own, from_first, *early = lax.optimization_barrier((rows, from_first, *early))
+    from_second = lax.ppermute(own, "ch", [(1, 0)])
+    grads_out = finish(0, *early)
+    rows = rows + (from_first + from_second)
     rows = rows.transpose(1, 0, 2).reshape(MODES, count * LANES)
     gain = jnp.sqrt((1.0 + decay_rate) / TOKENS)
     residue_grad = gain * rows / math.sqrt(TOKENS)
-    conv, flowing = in_hbm(conv, flowing)
-    grads_out = pl.pallas_call(
-        finish_kernel,
-        in_specs=[vmem] + [hbm] * 5 + [vmem] * 6,
-        out_specs=[hbm] * 3,
-        out_shape=[pltpu.HBM((ROWS, WIDTH), bf16)] * 3,
-        scratch_shapes=[
-            whole,
-            whole,
-            whole,
-            pltpu.VMEM(tiles, f32),
-            pltpu.VMEM(tiles, f32),
-            whole,
-            whole,
-            whole,
-            pltpu.SemaphoreType.DMA((BLOCKS, 5)),
-            pltpu.SemaphoreType.DMA((BLOCKS, 3)),
-        ],
-        compiler_params=limit,
-        name="finish",
-    )(
-        late_tab, key_rows, value_rows, upstream, conv, flowing, back,
-        lead_k, lead_v, lead_u, lead_conv, lead_flow,
-    )
     return (*grads_out, residue_grad)
 
 

time: 73 us -> 73.6 us (level); the launches traced: 72.7 us -> 72.4 us
  starting transfers between devices: 27.3 us -> 26.3 us
    ppermute x1 -> x2, starting transfers between devices: 3.63 us -> 2.58 us  [the longest x1 1.29 us: local(): from_first = lax.ppermute(rows, 'ch', [(0, 1)])]
    pallas_call x1 -> x2, Pallas kernels: 5.22 us -> 5.81 us  [finish(): pl.pallas_call(functools.partial(finish_kernel, turn), in_specs=[smem, vm...]
  transfers between devices with their start and end apart: 4 -> 5, of which waited for: 2 -> 3; matrix products, arithmetic and copies ran while one was open for 0% -> 0% of each run, Pallas kernels for 26% -> 27%
where the time goes in v6:
time: 73.6 us; the launch traced here: 72.4 us
  starting transfers between devices  26.3 us (36%)
  Pallas kernels  25.9 us (35%)
  waiting for transfers between devices  18.1 us (25%)
  other arithmetic  1.42 us (2%)
  between operations  0.78 us (1%)
    all_to_all x1, starting transfers between devices, local(): arrived = lax.all_to_all(send, ALL, 0, 0, tiled=True)  14.6 us
    pallas_call x2, Pallas kernels, inner(): pl.pallas_call(functools.partial(inner_kernel, reverse), in_specs=[hbm] *...  11 us
    all_to_all x1, waiting for transfers between devices, local(): arrived = lax.all_to_all(send, ALL, 0, 0, tiled=True)  9.71 us
    all_to_all x1, waiting for transfers between devices, local(): back = lax.all_to_all(carries, ALL, 0, 0, tiled=True)  8.13 us
    all_to_all x1, starting transfers between devices, local(): back = lax.all_to_all(carries, ALL, 0, 0, tiled=True)  6.6 us
    pallas_call x2, Pallas kernels, finish(): pl.pallas_call(functools.partial(finish_kernel, turn), in_specs=[smem, vm...  5.81 us
    pallas_call x1, Pallas kernels, local(): pl.pallas_call(summarize_kernel, in_specs=[smem] + [vmem] * 4, out_specs=...  5.22 us
    pallas_call x1, Pallas kernels, local(): pl.pallas_call(prepare_kernel, in_specs=[hbm] * 4, out_specs=[vmem] * 2,...  2.68 us
  transfers between devices with their start and end apart: 5, of which 3 were waited for; matrix products, arithmetic and copies ran while one was open for 0% of the time, Pallas kernels for 27%

profile of v6, /device:TPU:1, one launch (start us, length us, event | category | flops | bytes accessed | tf_op | source)
XLA Modules:
  0.0 72.4 jit_solution(7438809352352661977)
XLA Ops:
  0.6 0.8 %pad_select_fusion.mine_ref = f32[16,256]{1,0:T(8,128)S(1)} fusion(f32[8,256]{1,0:T(8,128)} %param.11, f32[8,256]{1,0:T(8,128)} %param.10, pred[16]{0:T(512)(128)(4,1)S(1)} %iota_compare_fusion), kind=kLoop, calls=%fused_computation.1 | loop fusion | flops 4096 | bytes 32784 | tf_op jit(solution)/shard_map/jit(_where)/select_n | solution.py:445
  1.4 2.5 %collective-permute-start = (f32[16,256]{1,0:T(8,128)S(1)}, f32[16,256]{1,0:T(8,128)S(1)}, u32[]{:S(2)}, u32[]{:S(2)}) collective-permute-start(f32[16,256]{1,0:T(8,128)S(1)} %pad_select_fusion.mine_ref), channel_id=1, source_target_pairs={{0,1},{1,0},{2,3},{3,2},{4,5},{5,4},{6,7},{7,6},{8,9},{9,8},{10,11... | collective-permute-start | bytes 49160 | tf_op jit(solution)/shard_map/ppermute | solution.py:446
  3.9 2.7 %prepare.1 = (f32[4,8,128,128]{3,2,1,0:T(8,128)S(1)}, f32[4,8,128,128]{3,2,1,0:T(8,128)S(1)}) custom-call(bf16[128,4096]{1,0:T(8,128)(2,1)} %q_hbm.1, bf16[128,4096]{1,0:T(8,128)(2,1)} %refs_1_.5, bf16[128,4096]{1,0:T(8,128)(2,1)} %refs_2_.5, bf16[128,4096]{1,0:T(8,128)(2,1)} %refs_3_.3), custom_call_target="tpu_custom_call" | custom-call | flops 4194304 | bytes 12582912 | tf_op jit(solution)/shard_map/prepare/pallas_call | solution.py:461
  6.6 0.0 collective-permute-done.other_ref
  6.6 5.2 %summarize.1 = (f32[128,1,640]{2,1,0:T(1,128)}, f32[4,8,8,8,128]{4,3,2,1,0:T(8,128)}, f32[4,8,8,8,128]{4,3,2,1,0:T(8,128)}, f32[32,128]{1,0:T(8,128)}, f32[32,12...) custom-call(s32[1]{0:T(128)} %bitcast.1.half_ref, f32[16,256]{1,0:T(8,128)S(1)} %pad_select_fusion.mine_ref, ...), custom_call_target="tpu_custom_call" | custom-call | tf_op jit(solution)/shard_map/summarize/pallas_call | solution.py:471
  11.8 14.6 %all-to-all-start = ((f32[128,1,640]{2,1,0:T(1,128)}), f32[128,1,640]{2,1,0:T(1,128)S(1)}, u32[]{:S(2)}, u32[]{:S(2)}) async-start(f32[128,1,640]{2,1,0:T(1,128)} %get-tuple-element.43), calls=%async_computation | async-start | bytes 655360 | tf_op jit(solution)/shard_map/all_to_all | solution.py:494
  26.5 0.0 copy-start
  26.5 5.2 %ahead.1 = (f32[4,8,128,128]{3,2,1,0:T(8,128)}, f32[4,128,128]{2,1,0:T(8,128)S(1)}, bf16[128,512]{1,0:T(8,128)(2,1)S(1)}, bf16[128,512]{1,0:T(8,128)(2,1)S(1)}, ...) custom-call(f32[32,128]{1,0:T(8,128)} %get-tuple-element.38.rates_hbm.rates_ref, ...), custom_call_target="tpu_custom_call" | custom-call | flops 16777216 | bytes 16777216 | tf_op jit(solution)/shard_map/ahead/pallas_call | solution.py:500
  31.7 9.7 %all-to-all-done.x_ref = f32[128,1,640]{2,1,0:T(1,128)S(1)} async-done(((f32[128,1,640]{2,1,0:T(1,128)}), f32[128,1,640]{2,1,0:T(1,128)S(1)}, u32[]{:S(2)}, u32[]{:S(2)}) %all-to-all-start) | async-done | bytes 327712 | tf_op jit(solution)/shard_map/all_to_all | solution.py:494
  41.4 0.0 copy-done
  41.4 1.2 %carry.1 = f32[128,1,640]{2,1,0:T(1,128)} custom-call(s32[1]{0:T(128)} %bitcast.2.where_ref, f32[32,128]{1,0:T(8,128)S(1)} %copy-done, f32[128,1,640]{2,1,0:T(1,128)S(1)} %all-to-all-done.x_ref), custom_call_target="tpu_custom_call" | custom-call | tf_op jit(solution)/shard_map/carry/pallas_call | solution.py:532
  42.6 6.6 %all-to-all-start.1 = ((f32[128,1,640]{2,1,0:T(1,128)}), f32[128,1,640]{2,1,0:T(1,128)S(1)}, u32[]{:S(2)}, u32[]{:S(2)}) async-start(f32[128,1,640]{2,1,0:T(1,128)} %carry.1), calls=%async_computation.1 | async-start | bytes 655360 | tf_op jit(solution)/shard_map/all_to_all | solution.py:541
  49.2 5.8 %behind.1 = (f32[4,8,128,128]{3,2,1,0:T(8,128)}, f32[4,128,128]{2,1,0:T(8,128)S(1)}) custom-call(f32[32,128]{1,0:T(8,128)} %get-tuple-element.38.rates_hbm.rates_ref, f32[32,128]{1,0:T(8,128)} %get-tuple-element.39.residues_hbm, f32[4,8,128,128]{3,2,1,0:T(8,128)} %get-tuple-element.47.xs_hbm, f32[4,8,8,8,128]{4,3,2,1,0:T(8,128)} %get-tuple-element.48.enter_hbm), custom_call_target="tpu_custom_call" | custom-call | flops 16777216 | bytes 16777216 | tf_op jit(solution)/shard_map/behind/pallas_call | solution.py:500
  55.0 8.1 %all-to-all-done.1.refs_6_ = f32[128,1,640]{2,1,0:T(1,128)S(1)} async-done(((f32[128,1,640]{2,1,0:T(1,128)}), f32[128,1,640]{2,1,0:T(1,128)S(1)}, u32[]{:S(2)}, u32[]{:S(2)}) %all-to-all-start.1) | async-done | bytes 327712 | tf_op jit(solution)/shard_map/all_to_all | solution.py:541
  63.2 1.3 %collective-permute-start.1 = (f32[2,8,128]{2,1,0:T(8,128)S(1)}, f32[2,8,128]{2,1,0:T(8,128)S(1)}, u32[]{:S(2)}, u32[]{:S(2)}) collective-permute-start(f32[2,8,128]{2,1,0:T(8,128)S(1)} %dynamic-slice_reduce_fusion), channel_id=1, source_target_pairs={{0,2},{1,3},{4,6},{5,7},{8,10},{9,11},{12,14},{13,15},{16,18},{17,... | collective-permute-start | bytes 24584 | tf_op jit(solution)/shard_map/ppermute | solution.py:580
  64.5 5.2 %finish1.1 = (bf16[128,4096]{1,0:T(8,128)(2,1)}, bf16[128,4096]{1,0:T(8,128)(2,1)}, bf16[128,4096]{1,0:T(8,128)(2,1)}) custom-call(s32[1]{0:T(128)} %bitcast.core_ref, f32[3,32,8,128]{3,2,1,0:T(8,128)S(1)} %get-tuple-element.42.refs_0_, bf16[128,4096]{1,0:T(8,128)(2,1)} %refs_1_.5, bf16[128,4096]{1,0:T(8,128)(2,1)} %refs_2_.5, bf16[128,4096]{1,0:T(8,128)(2,1)} %refs_3_.3, ...), custom_call_target="tpu_custom_call" | custom-call | flops 16777216 | bytes 10485760 | tf_op jit(solution)/shard_map/finish1/pallas_call | solution.py:552
  69.7 0.0 collective-permute-done.1
  69.7 0.0 copy-start.1
  69.7 1.3 %collective-permute-start.2 = (f32[2,8,128]{2,1,0:T(8,128)S(1)}, f32[2,8,128]{2,1,0:T(8,128)S(1)}, u32[]{:S(2)}, u32[]{:S(2)}) collective-permute-start(f32[2,8,128]{2,1,0:T(8,128)S(1)} %dynamic-slice_reduce_fusion), channel_id=1, source_target_pairs={{2,0},{3,1},{6,4},{7,5},{10,8},{11,9},{14,12},{15,13},{18,16},{19,... | collective-permute-start | bytes 24584 | tf_op jit(solution)/shard_map/ppermute | solution.py:583
  71.0 0.6 finish0.1
  71.6 0.2 collective-permute-done.2
  71.8 0.0 copy-done.1
  71.8 0.6 fusion
  (3 shorter events, 0.1 us)
Async XLA Ops:
  1.4 5.2 %collective-permute-start = (f32[16,256]{1,0:T(8,128)S(1)}, f32[16,256]{1,0:T(8,128)S(1)}, u32[]{:S(2)}, u32[]{:S(2)}) collective-permute-start(f32[16,256]{1,0:T(8,128)S(1)} %pad_select_fusion.mine_ref), channel_id=1, source_target_pairs={{0,1},{1,0},{2,3},{3,2},{4,5},{5,4},{6,7},{7,6},{8,9},{9,8},{10,11... | collective-permute-start | bytes 49160 | tf_op jit(solution)/shard_map/ppermute | solution.py:446
  11.8 29.6 %all-to-all-start = ((f32[128,1,640]{2,1,0:T(1,128)}), f32[128,1,640]{2,1,0:T(1,128)S(1)}, u32[]{:S(2)}, u32[]{:S(2)}) async-start(f32[128,1,640]{2,1,0:T(1,128)} %get-tuple-element.43), calls=%async_computation | async-start | bytes 655360 | tf_op jit(solution)/shard_map/all_to_all | solution.py:494
  26.5 14.9 %copy-start = (f32[32,128]{1,0:T(8,128)S(1)}, f32[32,128]{1,0:T(8,128)}, u32[]{:S(2)}) copy-start(f32[32,128]{1,0:T(8,128)} %get-tuple-element.38.rates_hbm.rates_ref) | copy-start | bytes 49156
  42.6 20.5 %all-to-all-start.1 = ((f32[128,1,640]{2,1,0:T(1,128)}), f32[128,1,640]{2,1,0:T(1,128)S(1)}, u32[]{:S(2)}, u32[]{:S(2)}) async-start(f32[128,1,640]{2,1,0:T(1,128)} %carry.1), calls=%async_computation.1 | async-start | bytes 655360 | tf_op jit(solution)/shard_map/all_to_all | solution.py:541
  63.2 6.5 %collective-permute-start.1 = (f32[2,8,128]{2,1,0:T(8,128)S(1)}, f32[2,8,128]{2,1,0:T(8,128)S(1)}, u32[]{:S(2)}, u32[]{:S(2)}) collective-permute-start(f32[2,8,128]{2,1,0:T(8,128)S(1)} %dynamic-slice_reduce_fusion), channel_id=1, source_target_pairs={{0,2},{1,3},{4,6},{5,7},{8,10},{9,11},{12,14},{13,15},{16,18},{17,... | collective-permute-start | bytes 24584 | tf_op jit(solution)/shard_map/ppermute | solution.py:580
  69.7 2.1 %copy-start.1 = (f32[8,256]{1,0:T(8,128)S(1)}, f32[8,256]{1,0:T(8,128)}, u32[]{:S(2)}) copy-start(f32[8,256]{1,0:T(8,128)} %param.10) | copy-start | bytes 24580
  69.7 2.1 %collective-permute-start.2 = (f32[2,8,128]{2,1,0:T(8,128)S(1)}, f32[2,8,128]{2,1,0:T(8,128)S(1)}, u32[]{:S(2)}, u32[]{:S(2)}) collective-permute-start(f32[2,8,128]{2,1,0:T(8,128)S(1)} %dynamic-slice_reduce_fusion), channel_id=1, source_target_pairs={{2,0},{3,1},{6,4},{7,5},{10,8},{11,9},{14,12},{15,13},{18,16},{19,... | collective-permute-start | bytes 24584 | tf_op jit(solution)/shard_map/ppermute | solution.py:583

commit v7 on v6

--- a/solution.py
+++ b/solution.py
@@ -22,6 +22,7 @@
 WIDTH = BLOCKS * FILTERS
 SHARDS = TOKENS // ROWS
 PACKET = 5 * LANES
+HELD = 3
 ALL = ("ctx", "fsdp")
 f32 = jnp.float32
 bf16 = jnp.bfloat16
@@ -340,22 +341,24 @@
     copy.wait()
 
 
-def finish_kernel(turn, core_ref, *refs):
-    @pl.when(core_ref[0] == turn)
-    def _():
-        finish_body(*refs[:12], *refs[-13:])
-
-
-def finish_body(
-    tab, k_hbm, v_hbm, u_hbm, conv_hbm, flow_hbm, in_ref,
-    lead_k, lead_v, lead_u, lead_conv, lead_flow,
-    gq_hbm, gk_hbm, gv_hbm,
-    k_ref, v_ref, u_ref, conv_ref, flow_ref, gq_ref, gk_ref, gv_ref, arrive_sems, sems,
-):
+def finish_kernel(last, core_ref, tab, k_hbm, v_hbm, u_hbm, conv_hbm, flow_hbm, in_ref, *refs):
+    gq_hbm, gk_hbm, gv_hbm, k_ref, v_ref, u_ref, conv_ref, flow_ref = refs[-13:-5]
+    gq_ref, gk_ref, gv_ref, arrive_sems, sems = refs[-5:]
+    second = core_ref[0] == 1
+    if last:
+        low, high = 0, jnp.where(second, HELD, BLOCKS)
+    else:
+        low, high = HELD, jnp.where(second, BLOCKS, HELD)
+
+    def for_blocks(do, first=low):
+        def body(blk, _):
+            do(blk)
+            return 0
+
+        lax.fori_loop(first, high, body, 0)
+
     def arrivals(blk):
-        cols = pl.ds(blk * FILTERS, FILTERS)
-        if not isinstance(blk, int):
-            cols = pl.ds(pl.multiple_of(blk * FILTERS, FILTERS), FILTERS)
+        cols = pl.ds(pl.multiple_of(blk * FILTERS, FILTERS), FILTERS)
         pairs = [
             (a.at[:, blk], b.at[:, blk]) for a, b in ((conv_hbm, conv_ref), (flow_hbm, flow_ref))
         ]
@@ -365,15 +368,19 @@
             pltpu.make_async_copy(a, b, arrive_sems.at[blk, i]) for i, (a, b) in enumerate(pairs)
         ]
 
-    for blk in range(1, BLOCKS):
+    def fetch(blk):
         for copy in arrivals(blk):
             copy.start()
-    lead = pl.ds(0, FILTERS)
-    for a, b in ((lead_k, k_ref), (lead_v, v_ref), (lead_u, u_ref)):
-        b[:, lead] = a[...]
-    for strip in range(STRIPS):
-        conv_ref[strip, 0] = lead_conv[strip]
-        flow_ref[strip, 0] = lead_flow[strip]
+
+    for_blocks(fetch, max(low, 1))
+    if last:
+        lead_k, lead_v, lead_u, lead_conv, lead_flow = refs[:5]
+        lead = pl.ds(0, FILTERS)
+        for a, b in ((lead_k, k_ref), (lead_v, v_ref), (lead_u, u_ref)):
+            b[:, lead] = a[...]
+        for strip in range(STRIPS):
+            conv_ref[strip, 0] = lead_conv[strip]
+            flow_ref[strip, 0] = lead_flow[strip]
 
     def copies(blk):
         cols = pl.ds(pl.multiple_of(blk * FILTERS, FILTERS), FILTERS)
@@ -382,54 +389,55 @@
             for i, (src, dst) in enumerate(((gq_ref, gq_hbm), (gk_ref, gk_hbm), (gv_ref, gv_hbm)))
         ]
 
-    def pair_body(pair, _):
-        for odd in range(2):
-            blk = 2 * pair + odd
-
-            @pl.when(blk > 0)
-            def _():
-                for copy in arrivals(blk):
-                    copy.wait()
-
-            def strip_body(strip, _):
-                base = strip * MODES
-                cols = lanes_of(blk * STRIPS + strip)
-                leap = [tab[0, base + n] for n in range(MODES)]
-                places = [owner(strip, pair, n) for n in range(MODES)]
-                state = [
-                    tab[1, base + n] * in_ref[places[n], :, piece(odd)] for n in range(MODES)
-                ]
-                for i in range(ROWS // 16):
-                    parts = []
-                    for _ in range(2):
-                        parts.append(total(state))
-                        state = [leap[n] * state[n] for n in range(MODES)]
-                    at = pl.ds(16 * i, 16)
-                    conv = conv_ref[strip, blk, at, :] + jnp.concatenate(parts, axis=0)
-                    gq_ref[at, cols] = (u_ref[at, cols].astype(f32) * conv).astype(bf16)
-                state = [
-                    tab[2, base + n] * in_ref[places[n], :, piece(2 + odd)] for n in range(MODES)
-                ]
-                for i in reversed(range(ROWS // 16)):
-                    parts = []
-                    for _ in range(2):
-                        parts.insert(0, total(state))
-                        state = [leap[n] * state[n] for n in range(MODES)]
-                    at = pl.ds(16 * i, 16)
-                    flow = flow_ref[strip, blk, at, :] + jnp.concatenate(parts, axis=0)
-                    gk_ref[at, cols] = (flow * v_ref[at, cols].astype(f32)).astype(bf16)
-                    gv_ref[at, cols] = (flow * k_ref[at, cols].astype(f32)).astype(bf16)
-                return 0
-
-            lax.fori_loop(0, STRIPS, strip_body, 0)
-            for copy in copies(blk):
-                copy.start()
-        return 0
-
-    lax.fori_loop(0, PAIRS, pair_body, 0)
-    for blk in range(BLOCKS):
+    def block(blk):
+        pair, odd = blk // 2, blk % 2
+
+        @pl.when(blk > 0)
+        def _():
+            for copy in arrivals(blk):
+                copy.wait()
+
+        def strip_body(strip, _):
+            base = strip * MODES
+            cols = lanes_of(blk * STRIPS + strip)
+            leap = [tab[0, base + n] for n in range(MODES)]
+            places = [owner(strip, pair, n) for n in range(MODES)]
+            state = [
+                tab[1, base + n] * in_ref[places[n], :, lanes_of(odd)] for n in range(MODES)
+            ]
+            for i in range(ROWS // 16):
+                parts = []
+                for _ in range(2):
+                    parts.append(total(state))
+                    state = [leap[n] * state[n] for n in range(MODES)]
+                at = pl.ds(16 * i, 16)
+                conv = conv_ref[strip, blk, at, :] + jnp.concatenate(parts, axis=0)
+                gq_ref[at, cols] = (u_ref[at, cols].astype(f32) * conv).astype(bf16)
+            state = [
+                tab[2, base + n] * in_ref[places[n], :, lanes_of(2 + odd)] for n in range(MODES)
+            ]
+            for i in reversed(range(ROWS // 16)):
+                parts = []
+                for _ in range(2):
+                    parts.insert(0, total(state))
+                    state = [leap[n] * state[n] for n in range(MODES)]
+                at = pl.ds(16 * i, 16)
+                flow = flow_ref[strip, blk, at, :] + jnp.concatenate(parts, axis=0)
+                gk_ref[at, cols] = (flow * v_ref[at, cols].astype(f32)).astype(bf16)
+                gv_ref[at, cols] = (flow * k_ref[at, cols].astype(f32)).astype(bf16)
+            return 0
+
+        lax.fori_loop(0, STRIPS, strip_body, 0)
+        for copy in copies(blk):
+            copy.start()
+
+    for_blocks(block)
+
+    def drain(blk):
         for copy in copies(blk):
             copy.wait()
+
+    for_blocks(drain)
 
 
 def in_hbm(*arrays):
@@ -548,13 +556,17 @@
     core = lax.axis_index("ch").astype(jnp.int32).reshape(1)
     shapes = [pltpu.HBM((ROWS, WIDTH), bf16)] * 3
 
-    def finish(turn, *before):
+    def finish(last, leads=(), before=()):
+        count_in = 8 + len(leads)
         return pl.pallas_call(
-            functools.partial(finish_kernel, turn),
-            in_specs=[smem, vmem] + [hbm] * 5 + [vmem] * 6 + [hbm] * len(before),
+            functools.partial(finish_kernel, last),
+            in_specs=[smem, vmem]
+            + [hbm] * 5
+            + [vmem] * (1 + len(leads))
+            + [hbm] * len(before),
             out_specs=[hbm] * 3,
             out_shape=shapes,
-            input_output_aliases={13 + i: i for i in range(len(before))},
+            input_output_aliases={count_in + i: i for i in range(len(before))},
             scratch_shapes=[
                 whole,
                 whole,
@@ -571,18 +583,15 @@
             cost_estimate=pl.CostEstimate(
                 flops=1 << 24, bytes_accessed=10 << 20, transcendentals=0
             ),
-            name=f"finish{turn}",
+            name="finish" if last else "begin",
         )(
-            core, late_tab, key_rows, value_rows, upstream, conv, flowing, back,
-            lead_k, lead_v, lead_u, lead_conv, lead_flow, *before,
+            core, late_tab, key_rows, value_rows, upstream, conv, flowing, back, *leads, *before
         )
 
-    from_first = lax.ppermute(rows, "ch", [(0, 1)])
-    early = finish(1)
-    own, from_first, *early = lax.optimization_barrier((rows, from_first, *early))
-    from_second = lax.ppermute(own, "ch", [(1, 0)])
-    grads_out = finish(0, *early)
-    rows = rows + (from_first + from_second)
+    early = finish(False)
+    own, *early = lax.optimization_barrier((rows, *early))
+    rows = rows + lax.ppermute(own, "ch", swap)
+    grads_out = finish(True, (lead_k, lead_v, lead_u, lead_conv, lead_flow), early)
     rows = rows.transpose(1, 0, 2).reshape(MODES, count * LANES)
     gain = jnp.sqrt((1.0 + decay_rate) / TOKENS)
     residue_grad = gain * rows / math.sqrt(TOKENS)

time: 73.6 us -> 72 us (0.978); the launches traced: 72.4 us -> 71.6 us
  starting transfers between devices: 26.3 us -> 23.8 us
  Pallas kernels: 25.9 us -> 27.8 us
    ppermute x2 -> x1, starting transfers between devices: 2.58 us -> 0.09 us  [local(): rows = rows + lax.ppermute(own, 'ch', swap)]
    pallas_call x2, Pallas kernels: 5.81 us -> 7.68 us  [finish(): pl.pallas_call(functools.partial(finish_kernel, last), in_specs=[smem, vm...]
  transfers between devices with their start and end apart: 5 -> 4, of which waited for: 3 -> 2; matrix products, arithmetic and copies ran while one was open for 0% -> 0% of each run, Pallas kernels for 27% -> 24%
where the time goes in v7:
time: 72 us; the launch traced here: 71.6 us
  Pallas kernels  27.8 us (39%)
  starting transfers between devices  23.8 us (33%)
  waiting for transfers between devices  17.7 us (25%)
  other arithmetic  1.42 us (2%)
  between operations  0.78 us (1%)
    all_to_all x1, starting transfers between devices, local(): arrived = lax.all_to_all(send, ALL, 0, 0, tiled=True)  14.6 us
    pallas_call x2, Pallas kernels, inner(): pl.pallas_call(functools.partial(inner_kernel, reverse), in_specs=[hbm] *...  11.1 us
    all_to_all x1, waiting for transfers between devices, local(): arrived = lax.all_to_all(send, ALL, 0, 0, tiled=True)  9.58 us
    all_to_all x1, waiting for transfers between devices, local(): back = lax.all_to_all(carries, ALL, 0, 0, tiled=True)  8.15 us
    pallas_call x2, Pallas kernels, finish(): pl.pallas_call(functools.partial(finish_kernel, last), in_specs=[smem, vm...  7.68 us
    all_to_all x1, starting transfers between devices, local(): back = lax.all_to_all(carries, ALL, 0, 0, tiled=True)  6.6 us
    pallas_call x1, Pallas kernels, local(): pl.pallas_call(summarize_kernel, in_specs=[smem] + [vmem] * 4, out_specs=...  5.22 us
    pallas_call x1, Pallas kernels, local(): pl.pallas_call(prepare_kernel, in_specs=[hbm] * 4, out_specs=[vmem] * 2,...  2.68 us
  transfers between devices with their start and end apart: 4, of which 2 were waited for; matrix products, arithmetic and copies ran while one was open for 0% of the time, Pallas kernels for 24%

profile of v7, /device:TPU:1, one launch (start us, length us, event | category | flops | bytes accessed | tf_op | source)
XLA Modules:
  0.0 71.6 jit_solution(2678224498824342600)
XLA Ops:
  0.6 0.8 %pad_select_fusion.mine_ref = f32[16,256]{1,0:T(8,128)S(1)} fusion(f32[8,256]{1,0:T(8,128)} %param.11, f32[8,256]{1,0:T(8,128)} %param.10, pred[16]{0:T(512)(128)(4,1)S(1)} %iota_compare_fusion), kind=kLoop, calls=%fused_computation.1 | loop fusion | flops 4096 | bytes 32784 | tf_op jit(solution)/shard_map/jit(_where)/select_n | solution.py:453
  1.4 2.5 %collective-permute-start = (f32[16,256]{1,0:T(8,128)S(1)}, f32[16,256]{1,0:T(8,128)S(1)}, u32[]{:S(2)}, u32[]{:S(2)}) collective-permute-start(f32[16,256]{1,0:T(8,128)S(1)} %pad_select_fusion.mine_ref), channel_id=1, source_target_pairs={{0,1},{1,0},{2,3},{3,2},{4,5},{5,4},{6,7},{7,6},{8,9},{9,8},{10,11... | collective-permute-start | bytes 49160 | tf_op jit(solution)/shard_map/ppermute | solution.py:454
  3.9 2.7 %prepare.1 = (f32[4,8,128,128]{3,2,1,0:T(8,128)S(1)}, f32[4,8,128,128]{3,2,1,0:T(8,128)S(1)}) custom-call(bf16[128,4096]{1,0:T(8,128)(2,1)} %q_hbm.1, bf16[128,4096]{1,0:T(8,128)(2,1)} %k_hbm.5, bf16[128,4096]{1,0:T(8,128)(2,1)} %v_hbm.5, bf16[128,4096]{1,0:T(8,128)(2,1)} %u_hbm.5), custom_call_target="tpu_custom_call" | custom-call | flops 4194304 | bytes 12582912 | tf_op jit(solution)/shard_map/prepare/pallas_call | solution.py:469
  6.6 0.0 collective-permute-done.other_ref
  6.6 5.2 %summarize.1 = (f32[128,1,640]{2,1,0:T(1,128)}, f32[4,8,8,8,128]{4,3,2,1,0:T(8,128)}, f32[4,8,8,8,128]{4,3,2,1,0:T(8,128)}, f32[32,128]{1,0:T(8,128)}, f32[32,12...) custom-call(s32[1]{0:T(128)} %bitcast.1.half_ref, f32[16,256]{1,0:T(8,128)S(1)} %pad_select_fusion.mine_ref, ...), custom_call_target="tpu_custom_call" | custom-call | tf_op jit(solution)/shard_map/summarize/pallas_call | solution.py:479
  11.8 14.6 %all-to-all-start = ((f32[128,1,640]{2,1,0:T(1,128)}), f32[128,1,640]{2,1,0:T(1,128)S(1)}, u32[]{:S(2)}, u32[]{:S(2)}) async-start(f32[128,1,640]{2,1,0:T(1,128)} %get-tuple-element.42), calls=%async_computation | async-start | bytes 655360 | tf_op jit(solution)/shard_map/all_to_all | solution.py:502
  26.5 0.0 copy-start
  26.5 5.3 %ahead.1 = (f32[4,8,128,128]{3,2,1,0:T(8,128)}, f32[4,128,128]{2,1,0:T(8,128)S(1)}, bf16[128,512]{1,0:T(8,128)(2,1)S(1)}, bf16[128,512]{1,0:T(8,128)(2,1)S(1)}, ...) custom-call(f32[32,128]{1,0:T(8,128)} %get-tuple-element.37.rates_hbm.rates_ref, ...), custom_call_target="tpu_custom_call" | custom-call | flops 16777216 | bytes 16777216 | tf_op jit(solution)/shard_map/ahead/pallas_call | solution.py:508
  31.8 9.6 %all-to-all-done.x_ref = f32[128,1,640]{2,1,0:T(1,128)S(1)} async-done(((f32[128,1,640]{2,1,0:T(1,128)}), f32[128,1,640]{2,1,0:T(1,128)S(1)}, u32[]{:S(2)}, u32[]{:S(2)}) %all-to-all-start) | async-done | bytes 327712 | tf_op jit(solution)/shard_map/all_to_all | solution.py:502
  41.4 0.0 copy-done
  41.4 1.2 %carry.1 = f32[128,1,640]{2,1,0:T(1,128)} custom-call(s32[1]{0:T(128)} %bitcast.2.where_ref, f32[32,128]{1,0:T(8,128)S(1)} %copy-done, f32[128,1,640]{2,1,0:T(1,128)S(1)} %all-to-all-done.x_ref), custom_call_target="tpu_custom_call" | custom-call | tf_op jit(solution)/shard_map/carry/pallas_call | solution.py:540
  42.6 6.6 %all-to-all-start.1 = ((f32[128,1,640]{2,1,0:T(1,128)}), f32[128,1,640]{2,1,0:T(1,128)S(1)}, u32[]{:S(2)}, u32[]{:S(2)}) async-start(f32[128,1,640]{2,1,0:T(1,128)} %carry.1), calls=%async_computation.1 | async-start | bytes 655360 | tf_op jit(solution)/shard_map/all_to_all | solution.py:549
  49.2 5.7 %behind.1 = (f32[4,8,128,128]{3,2,1,0:T(8,128)}, f32[4,128,128]{2,1,0:T(8,128)S(1)}) custom-call(f32[32,128]{1,0:T(8,128)} %get-tuple-element.37.rates_hbm.rates_ref, f32[32,128]{1,0:T(8,128)} %get-tuple-element.38.residues_hbm, f32[4,8,128,128]{3,2,1,0:T(8,128)} %get-tuple-element.46.xs_hbm, f32[4,8,8,8,128]{4,3,2,1,0:T(8,128)} %get-tuple-element.47.enter_hbm), custom_call_target="tpu_custom_call" | custom-call | flops 16777216 | bytes 16777216 | tf_op jit(solution)/shard_map/behind/pallas_call | solution.py:508
  54.9 8.2 %all-to-all-done.1.in_ref = f32[128,1,640]{2,1,0:T(1,128)S(1)} async-done(((f32[128,1,640]{2,1,0:T(1,128)}), f32[128,1,640]{2,1,0:T(1,128)S(1)}, u32[]{:S(2)}, u32[]{:S(2)}) %all-to-all-start.1) | async-done | bytes 327712 | tf_op jit(solution)/shard_map/all_to_all | solution.py:549
  63.2 4.4 %begin.1 = (bf16[128,4096]{1,0:T(8,128)(2,1)}, bf16[128,4096]{1,0:T(8,128)(2,1)}, bf16[128,4096]{1,0:T(8,128)(2,1)}) custom-call(s32[1]{0:T(128)} %bitcast.core_ref, f32[3,32,8,128]{3,2,1,0:T(8,128)S(1)} %get-tuple-element.41.tab, bf16[128,4096]{1,0:T(8,128)(2,1)} %k_hbm.5, bf16[128,4096]{1,0:T(8,128)(2,1)} %v_hbm.5, bf16[128,4096]{1,0:T(8,128)(2,1)} %u_hbm.5, ...), custom_call_target="tpu_custom_call" | custom-call | flops 16777216 | bytes 10485760 | tf_op jit(solution)/shard_map/begin/pallas_call | solution.py:561
  67.6 0.1 collective-permute-start.1
  67.7 0.0 copy-start.1
  67.7 3.2 %finish.1 = (bf16[128,4096]{1,0:T(8,128)(2,1)}, bf16[128,4096]{1,0:T(8,128)(2,1)}, bf16[128,4096]{1,0:T(8,128)(2,1)}) custom-call(s32[1]{0:T(128)} %bitcast.core_ref, f32[3,32,8,128]{3,2,1,0:T(8,128)S(1)} %get-tuple-element.41.tab, bf16[128,4096]{1,0:T(8,128)(2,1)} %k_hbm.5, ...), custom_call_target="tpu_custom_call", output_to_operand_aliasing={{0}: (13, {}), {1}: (14, {}), {2}: (15, {})} | custom-call | flops 16777216 | bytes 10485760 | tf_op jit(solution)/shard_map/finish/pallas_call | solution.py:561
  71.0 0.0 collective-permute-done.1
  71.0 0.0 copy-done.1
  71.0 0.6 fusion
  (3 shorter events, 0.1 us)
Async XLA Ops:
  1.4 5.2 %collective-permute-start = (f32[16,256]{1,0:T(8,128)S(1)}, f32[16,256]{1,0:T(8,128)S(1)}, u32[]{:S(2)}, u32[]{:S(2)}) collective-permute-start(f32[16,256]{1,0:T(8,128)S(1)} %pad_select_fusion.mine_ref), channel_id=1, source_target_pairs={{0,1},{1,0},{2,3},{3,2},{4,5},{5,4},{6,7},{7,6},{8,9},{9,8},{10,11... | collective-permute-start | bytes 49160 | tf_op jit(solution)/shard_map/ppermute | solution.py:454
  11.8 29.6 %all-to-all-start = ((f32[128,1,640]{2,1,0:T(1,128)}), f32[128,1,640]{2,1,0:T(1,128)S(1)}, u32[]{:S(2)}, u32[]{:S(2)}) async-start(f32[128,1,640]{2,1,0:T(1,128)} %get-tuple-element.42), calls=%async_computation | async-start | bytes 655360 | tf_op jit(solution)/shard_map/all_to_all | solution.py:502
  26.5 14.9 %copy-start = (f32[32,128]{1,0:T(8,128)S(1)}, f32[32,128]{1,0:T(8,128)}, u32[]{:S(2)}) copy-start(f32[32,128]{1,0:T(8,128)} %get-tuple-element.37.rates_hbm.rates_ref) | copy-start | bytes 49156
  42.6 20.5 %all-to-all-start.1 = ((f32[128,1,640]{2,1,0:T(1,128)}), f32[128,1,640]{2,1,0:T(1,128)S(1)}, u32[]{:S(2)}, u32[]{:S(2)}) async-start(f32[128,1,640]{2,1,0:T(1,128)} %carry.1), calls=%async_computation.1 | async-start | bytes 655360 | tf_op jit(solution)/shard_map/all_to_all | solution.py:549
  67.6 3.4 %collective-permute-start.1 = (f32[2,8,128]{2,1,0:T(8,128)S(1)}, f32[2,8,128]{2,1,0:T(8,128)S(1)}, u32[]{:S(2)}, u32[]{:S(2)}) collective-permute-start(f32[2,8,128]{2,1,0:T(8,128)S(1)} %dynamic-slice_reduce_fusion), channel_id=1, source_target_pairs={{0,2},{2,0},{1,3},{3,1},{4,6},{6,4},{5,7},{7,5},{8,10},{10,8},{9,1... | collective-permute-start | bytes 24584 | tf_op jit(solution)/shard_map/ppermute | solution.py:593
  67.7 3.3 %copy-start.1 = (f32[8,256]{1,0:T(8,128)S(1)}, f32[8,256]{1,0:T(8,128)}, u32[]{:S(2)}) copy-start(f32[8,256]{1,0:T(8,128)} %param.10) | copy-start | bytes 24580

commit v8 on v7

--- a/solution.py
+++ b/solution.py
@@ -218,9 +218,10 @@
 
 def inner_kernel(reverse, rates_hbm, residues_hbm, xs_hbm, enter_hbm, *refs):
     if reverse:
-        out_hbm, lead_ref = refs[:2]
+        out_hbm, *lead_refs = refs[:3]
     else:
-        k_hbm, v_hbm, u_hbm, out_hbm, lead_ref, lead_k, lead_v, lead_u, late_tab = refs[:9]
+        rows_hbm, out_hbm, lead_refs, late_tab = refs[:3], refs[3], refs[4:6], refs[6]
+        lead_rows = refs[7:13]
     tab, rates_ref, residues_ref, xs, enter_ref, out_ref, param_sems, sems = refs[-8:]
     params = [
         pltpu.make_async_copy(rates_hbm, rates_ref, param_sems.at[0]),
@@ -239,9 +240,8 @@
     s = sublane()
     leads = []
     if not reverse:
-        pairs = ((k_hbm, lead_k), (v_hbm, lead_v), (u_hbm, lead_u))
-        for i, (a, b) in enumerate(pairs):
-            source = a.at[:, pl.ds(0, FILTERS)]
+        for i, b in enumerate(lead_rows):
+            source = rows_hbm[i % 3].at[:, pl.ds((i // 3) * HELD * FILTERS, FILTERS)]
             leads.append(pltpu.make_async_copy(source, b, param_sems.at[2 + i]))
     for copy in params:
         copy.start()
@@ -293,7 +293,8 @@
 
         lax.fori_loop(0, BLOCKS, body, 0)
         leaving(strip).start()
-        lead_ref[strip] = out_ref[strip, 0]
+        lead_refs[0][strip] = out_ref[strip, 0]
+        lead_refs[1][strip] = out_ref[strip, HELD]
         return 0
 
     lax.fori_loop(0, STRIPS, strip_body, 0)
@@ -372,15 +373,17 @@
         for copy in arrivals(blk):
             copy.start()
 
-    for_blocks(fetch, max(low, 1))
-    if last:
+    for_blocks(fetch, low + 1)
+
+    @pl.when(high > low)
+    def _():
         lead_k, lead_v, lead_u, lead_conv, lead_flow = refs[:5]
-        lead = pl.ds(0, FILTERS)
+        lead = pl.ds(low * FILTERS, FILTERS)
         for a, b in ((lead_k, k_ref), (lead_v, v_ref), (lead_u, u_ref)):
             b[:, lead] = a[...]
         for strip in range(STRIPS):
-            conv_ref[strip, 0] = lead_conv[strip]
-            flow_ref[strip, 0] = lead_flow[strip]
+            conv_ref[strip, low] = lead_conv[strip]
+            flow_ref[strip, low] = lead_flow[strip]
 
     def copies(blk):
         cols = pl.ds(pl.multiple_of(blk * FILTERS, FILTERS), FILTERS)
@@ -392,7 +395,7 @@
     def block(blk):
         pair, odd = blk // 2, blk % 2
 
-        @pl.when(blk > 0)
+        @pl.when(blk > low)
         def _():
             for copy in arrivals(blk):
                 copy.wait()
@@ -508,8 +511,8 @@
         return pl.pallas_call(
             functools.partial(inner_kernel, reverse),
             in_specs=[hbm] * (4 + len(extra)),
-            out_specs=[hbm] + [vmem] * (1 + len(more)),
-            out_shape=[pltpu.HBM(tiles, f32), lead, *more],
+            out_specs=[hbm] + [vmem] * (2 + len(more)),
+            out_shape=[pltpu.HBM(tiles, f32), lead, lead, *more],
             scratch_shapes=[
                 pltpu.VMEM((5 if reverse else 2,) + table, f32),
                 pltpu.VMEM(params, f32),
@@ -517,7 +520,7 @@
                 pltpu.VMEM(tiles, f32),
                 pltpu.VMEM(state, f32),
                 pltpu.VMEM(tiles, f32),
-                pltpu.SemaphoreType.DMA((5,)),
+                pltpu.SemaphoreType.DMA((8,)),
                 pltpu.SemaphoreType.DMA((STRIPS, 3)),
             ],
             compiler_params=limit,
@@ -528,12 +531,12 @@
         )(*in_hbm(rates, residues, xs, enter), *extra)
 
     late = jax.ShapeDtypeStruct((3,) + table, f32)
-    conv, lead_conv, lead_k, lead_v, lead_u, late_tab = inner(
+    conv, lead_conv, held_conv, late_tab, *rows_in = inner(
         product,
         enter_ahead,
         False,
         (key_rows, value_rows, upstream),
-        (lead_rows, lead_rows, lead_rows, late),
+        (late,) + (lead_rows,) * 6,
     )
     arrived, conv = lax.optimization_barrier((arrived, conv))
     place = lax.axis_index(ALL).astype(jnp.int32).reshape(1)
@@ -547,7 +550,7 @@
         name="carry",
     )(place, rates, arrived)
     back = lax.all_to_all(carries, ALL, 0, 0, tiled=True)
-    flowing, lead_flow = inner(gated, enter_behind, True)
+    flowing, lead_flow, held_flow = inner(gated, enter_behind, True)
     back, flowing = lax.optimization_barrier((back, flowing))
     rows = back[:, 0, 4 * LANES :].reshape(STRIPS, PAIRS, MODES, LANES)
     count = STRIPS // 2
@@ -588,10 +591,10 @@
             core, late_tab, key_rows, value_rows, upstream, conv, flowing, back, *leads, *before
         )
 
-    early = finish(False)
+    early = finish(False, (*rows_in[3:], held_conv, held_flow))
     own, *early = lax.optimization_barrier((rows, *early))
     rows = rows + lax.ppermute(own, "ch", swap)
-    grads_out = finish(True, (lead_k, lead_v, lead_u, lead_conv, lead_flow), early)
+    grads_out = finish(True, (*rows_in[:3], lead_conv, lead_flow), early)
     rows = rows.transpose(1, 0, 2).reshape(MODES, count * LANES)
     gain = jnp.sqrt((1.0 + decay_rate) / TOKENS)
     residue_grad = gain * rows / math.sqrt(TOKENS)

time: 72 us -> 71.7 us (level)
  no operation moved by 1% of the time
where the time goes in v8:
time: 71.7 us; the launch traced here: 71.3 us
  Pallas kernels  27.4 us (38%)
  starting transfers between devices  23.9 us (33%)
  waiting for transfers between devices  17.8 us (25%)
  other arithmetic  1.42 us (2%)
  between operations  0.77 us (1%)
    all_to_all x1, starting transfers between devices, local(): arrived = lax.all_to_all(send, ALL, 0, 0, tiled=True)  14.6 us
    pallas_call x2, Pallas kernels, inner(): pl.pallas_call(functools.partial(inner_kernel, reverse), in_specs=[hbm] *...  11 us
    all_to_all x1, waiting for transfers between devices, local(): arrived = lax.all_to_all(send, ALL, 0, 0, tiled=True)  9.66 us
    all_to_all x1, waiting for transfers between devices, local(): back = lax.all_to_all(carries, ALL, 0, 0, tiled=True)  8.11 us
    pallas_call x2, Pallas kernels, finish(): pl.pallas_call(functools.partial(finish_kernel, last), in_specs=[smem, vm...  7.29 us
    all_to_all x1, starting transfers between devices, local(): back = lax.all_to_all(carries, ALL, 0, 0, tiled=True)  6.61 us
    pallas_call x1, Pallas kernels, local(): pl.pallas_call(summarize_kernel, in_specs=[smem] + [vmem] * 4, out_specs=...  5.22 us
    pallas_call x1, Pallas kernels, local(): pl.pallas_call(prepare_kernel, in_specs=[hbm] * 4, out_specs=[vmem] * 2,...  2.68 us
  transfers between devices with their start and end apart: 4, of which 2 were waited for; matrix products, arithmetic and copies ran while one was open for 0% of the time, Pallas kernels for 24%

profile of v8, /device:TPU:1, one launch (start us, length us, event | category | flops | bytes accessed | tf_op | source)
XLA Modules:
  0.0 71.3 jit_solution(14753120563761249800)
XLA Ops:
  0.6 0.8 %pad_select_fusion.mine_ref = f32[16,256]{1,0:T(8,128)S(1)} fusion(f32[8,256]{1,0:T(8,128)} %param.11, f32[8,256]{1,0:T(8,128)} %param.10, pred[16]{0:T(512)(128)(4,1)S(1)} %iota_compare_fusion), kind=kLoop, calls=%fused_computation.1 | loop fusion | flops 4096 | bytes 32784 | tf_op jit(solution)/shard_map/jit(_where)/select_n | solution.py:456
  1.4 2.5 %collective-permute-start = (f32[16,256]{1,0:T(8,128)S(1)}, f32[16,256]{1,0:T(8,128)S(1)}, u32[]{:S(2)}, u32[]{:S(2)}) collective-permute-start(f32[16,256]{1,0:T(8,128)S(1)} %pad_select_fusion.mine_ref), channel_id=1, source_target_pairs={{0,1},{1,0},{2,3},{3,2},{4,5},{5,4},{6,7},{7,6},{8,9},{9,8},{10,11... | collective-permute-start | bytes 49160 | tf_op jit(solution)/shard_map/ppermute | solution.py:457
  3.9 2.7 %prepare.1 = (f32[4,8,128,128]{3,2,1,0:T(8,128)S(1)}, f32[4,8,128,128]{3,2,1,0:T(8,128)S(1)}) custom-call(bf16[128,4096]{1,0:T(8,128)(2,1)} %q_hbm.1, bf16[128,4096]{1,0:T(8,128)(2,1)} %k_hbm.5, bf16[128,4096]{1,0:T(8,128)(2,1)} %v_hbm.5, bf16[128,4096]{1,0:T(8,128)(2,1)} %u_hbm.5), custom_call_target="tpu_custom_call" | custom-call | flops 4194304 | bytes 12582912 | tf_op jit(solution)/shard_map/prepare/pallas_call | solution.py:472
  6.6 0.0 collective-permute-done.other_ref
  6.6 5.2 %summarize.1 = (f32[128,1,640]{2,1,0:T(1,128)}, f32[4,8,8,8,128]{4,3,2,1,0:T(8,128)}, f32[4,8,8,8,128]{4,3,2,1,0:T(8,128)}, f32[32,128]{1,0:T(8,128)}, f32[32,12...) custom-call(s32[1]{0:T(128)} %bitcast.1.half_ref, f32[16,256]{1,0:T(8,128)S(1)} %pad_select_fusion.mine_ref, ...), custom_call_target="tpu_custom_call" | custom-call | tf_op jit(solution)/shard_map/summarize/pallas_call | solution.py:482
  11.8 14.6 %all-to-all-start = ((f32[128,1,640]{2,1,0:T(1,128)}), f32[128,1,640]{2,1,0:T(1,128)S(1)}, u32[]{:S(2)}, u32[]{:S(2)}) async-start(f32[128,1,640]{2,1,0:T(1,128)} %get-tuple-element.47), calls=%async_computation | async-start | bytes 655360 | tf_op jit(solution)/shard_map/all_to_all | solution.py:505
  26.5 0.0 copy-start
  26.5 5.3 %ahead.1 = (f32[4,8,128,128]{3,2,1,0:T(8,128)}, f32[4,128,128]{2,1,0:T(8,128)S(1)}, f32[4,128,128]{2,1,0:T(8,128)S(1)}, f32[3,32,8,128]{3,2,1,0:T(8,128)S(1)}, b...) custom-call(f32[32,128]{1,0:T(8,128)} %get-tuple-element.42.rates_hb, ...), custom_call_target="tpu_custom_call" | custom-call | flops 16777216 | bytes 16777216 | tf_op jit(solution)/shard_map/ahead/pallas_call | solution.py:511
  31.7 9.7 %all-to-all-done.x_ref = f32[128,1,640]{2,1,0:T(1,128)S(1)} async-done(((f32[128,1,640]{2,1,0:T(1,128)}), f32[128,1,640]{2,1,0:T(1,128)S(1)}, u32[]{:S(2)}, u32[]{:S(2)}) %all-to-all-start) | async-done | bytes 327712 | tf_op jit(solution)/shard_map/all_to_all | solution.py:505
  41.4 0.0 copy-done
  41.4 1.2 %carry.1 = f32[128,1,640]{2,1,0:T(1,128)} custom-call(s32[1]{0:T(128)} %bitcast.2.where_ref, f32[32,128]{1,0:T(8,128)S(1)} %copy-done, f32[128,1,640]{2,1,0:T(1,128)S(1)} %all-to-all-done.x_ref), custom_call_target="tpu_custom_call" | custom-call | tf_op jit(solution)/shard_map/carry/pallas_call | solution.py:543
  42.6 6.6 %all-to-all-start.1 = ((f32[128,1,640]{2,1,0:T(1,128)}), f32[128,1,640]{2,1,0:T(1,128)S(1)}, u32[]{:S(2)}, u32[]{:S(2)}) async-start(f32[128,1,640]{2,1,0:T(1,128)} %carry.1), calls=%async_computation.1 | async-start | bytes 655360 | tf_op jit(solution)/shard_map/all_to_all | solution.py:552
  49.2 5.8 %behind.1 = (f32[4,8,128,128]{3,2,1,0:T(8,128)}, f32[4,128,128]{2,1,0:T(8,128)S(1)}, f32[4,128,128]{2,1,0:T(8,128)S(1)}) custom-call(f32[32,128]{1,0:T(8,128)} %get-tuple-element.42.rates_hbm.rates_ref, f32[32,128]{1,0:T(8,128)} %get-tuple-element.43.residues_hbm, f32[4,8,128,128]{3,2,1,0:T(8,128)} %get-tuple-element.51.xs_hbm, ...), custom_call_target="tpu_custom_call" | custom-call | flops 16777216 | bytes 16777216 | tf_op jit(solution)/shard_map/behind/pallas_call | solution.py:511
  55.0 8.1 %all-to-all-done.1.in_ref = f32[128,1,640]{2,1,0:T(1,128)S(1)} async-done(((f32[128,1,640]{2,1,0:T(1,128)}), f32[128,1,640]{2,1,0:T(1,128)S(1)}, u32[]{:S(2)}, u32[]{:S(2)}) %all-to-all-start.1) | async-done | bytes 327712 | tf_op jit(solution)/shard_map/all_to_all | solution.py:552
  63.2 4.0 %begin.1 = (bf16[128,4096]{1,0:T(8,128)(2,1)}, bf16[128,4096]{1,0:T(8,128)(2,1)}, bf16[128,4096]{1,0:T(8,128)(2,1)}) custom-call(s32[1]{0:T(128)} %bitcast.core_ref, f32[3,32,8,128]{3,2,1,0:T(8,128)S(1)} %get-tuple-element.46.tab, bf16[128,4096]{1,0:T(8,128)(2,1)} %k_hbm.5, bf16[128,4096]{1,0:T(8,128)(2,1)} %v_hbm.5, bf16[128,4096]{1,0:T(8,128)(2,1)} %u_hbm.5, ...), custom_call_target="tpu_custom_call" | custom-call | flops 16777216 | bytes 10485760 | tf_op jit(solution)/shard_map/begin/pallas_call | solution.py:564
  67.2 0.2 collective-permute-start.1
  67.4 0.0 copy-start.1
  67.4 3.2 %finish.1 = (bf16[128,4096]{1,0:T(8,128)(2,1)}, bf16[128,4096]{1,0:T(8,128)(2,1)}, bf16[128,4096]{1,0:T(8,128)(2,1)}) custom-call(s32[1]{0:T(128)} %bitcast.core_ref, f32[3,32,8,128]{3,2,1,0:T(8,128)S(1)} %get-tuple-element.46.tab, bf16[128,4096]{1,0:T(8,128)(2,1)} %k_hbm.5, ...), custom_call_target="tpu_custom_call", output_to_operand_aliasing={{0}: (13, {}), {1}: (14, {}), {2}: (15, {})} | custom-call | flops 16777216 | bytes 10485760 | tf_op jit(solution)/shard_map/finish/pallas_call | solution.py:564
  70.6 0.0 collective-permute-done.1
  70.7 0.0 copy-done.1
  70.7 0.6 fusion
  (3 shorter events, 0.1 us)
Async XLA Ops:
  1.4 5.2 %collective-permute-start = (f32[16,256]{1,0:T(8,128)S(1)}, f32[16,256]{1,0:T(8,128)S(1)}, u32[]{:S(2)}, u32[]{:S(2)}) collective-permute-start(f32[16,256]{1,0:T(8,128)S(1)} %pad_select_fusion.mine_ref), channel_id=1, source_target_pairs={{0,1},{1,0},{2,3},{3,2},{4,5},{5,4},{6,7},{7,6},{8,9},{9,8},{10,11... | collective-permute-start | bytes 49160 | tf_op jit(solution)/shard_map/ppermute | solution.py:457
  11.8 29.6 %all-to-all-start = ((f32[128,1,640]{2,1,0:T(1,128)}), f32[128,1,640]{2,1,0:T(1,128)S(1)}, u32[]{:S(2)}, u32[]{:S(2)}) async-start(f32[128,1,640]{2,1,0:T(1,128)} %get-tuple-element.47), calls=%async_computation | async-start | bytes 655360 | tf_op jit(solution)/shard_map/all_to_all | solution.py:505
  26.5 14.9 %copy-start = (f32[32,128]{1,0:T(8,128)S(1)}, f32[32,128]{1,0:T(8,128)}, u32[]{:S(2)}) copy-start(f32[32,128]{1,0:T(8,128)} %get-tuple-element.42.rates_hbm.rates_ref) | copy-start | bytes 49156
  42.6 20.5 %all-to-all-start.1 = ((f32[128,1,640]{2,1,0:T(1,128)}), f32[128,1,640]{2,1,0:T(1,128)S(1)}, u32[]{:S(2)}, u32[]{:S(2)}) async-start(f32[128,1,640]{2,1,0:T(1,128)} %carry.1), calls=%async_computation.1 | async-start | bytes 655360 | tf_op jit(solution)/shard_map/all_to_all | solution.py:552
  67.2 3.4 %collective-permute-start.1 = (f32[2,8,128]{2,1,0:T(8,128)S(1)}, f32[2,8,128]{2,1,0:T(8,128)S(1)}, u32[]{:S(2)}, u32[]{:S(2)}) collective-permute-start(f32[2,8,128]{2,1,0:T(8,128)S(1)} %dynamic-slice_reduce_fusion), channel_id=1, source_target_pairs={{0,2},{2,0},{1,3},{3,1},{4,6},{6,4},{5,7},{7,5},{8,10},{10,8},{9,1... | collective-permute-start | bytes 24584 | tf_op jit(solution)/shard_map/ppermute | solution.py:596
  67.4 3.3 %copy-start.1 = (f32[8,256]{1,0:T(8,128)S(1)}, f32[8,256]{1,0:T(8,128)}, u32[]{:S(2)}) copy-start(f32[8,256]{1,0:T(8,128)} %param.10) | copy-start | bytes 24580

commit v9 on v8

--- a/solution.py
+++ b/solution.py
@@ -101,12 +101,12 @@
 
 
 def summarize_kernel(
-    half_ref, mine_ref, other_ref, ps, gs,
+    mine_ref, other_ref, ps, gs,
     send_hbm, cf_hbm, cb_hbm, rates_hbm, residues_hbm, ps_hbm, gs_hbm,
     tab, lags, joins, send_ref, cf_ref, cb_ref, rates_ref, residues_ref, sems, early_sems,
 ):
     s = sublane()
-    lower = jnp.broadcast_to(half_ref[0], (MODES, LANES)) == 0
+    lower = jnp.broadcast_to(lax.axis_index("fsdp"), (MODES, LANES)) == 0
     for strip in range(STRIPS):
         cols = pl.ds((strip % 2) * LANES, LANES)
         at = pl.ds(strip * MODES, MODES)
@@ -304,8 +304,8 @@
         copy.wait()
 
 
-def carry_kernel(where_ref, rates_ref, x_ref, y_hbm, y_ref, sem):
-    place = where_ref[0]
+def carry_kernel(rates_ref, x_ref, y_hbm, y_ref, sem):
+    place = lax.axis_index("ctx") * 2 + lax.axis_index("fsdp")
     at = (place // (PAIRS * MODES)) * MODES + place % MODES
     log_decay = rates_ref[pl.ds(at, 1), :] / TOKENS
     across = jnp.exp(-log_decay * ROWS)
@@ -342,10 +342,10 @@
     copy.wait()
 
 
-def finish_kernel(last, core_ref, tab, k_hbm, v_hbm, u_hbm, conv_hbm, flow_hbm, in_ref, *refs):
+def finish_kernel(last, tab, k_hbm, v_hbm, u_hbm, conv_hbm, flow_hbm, in_ref, *refs):
     gq_hbm, gk_hbm, gv_hbm, k_ref, v_ref, u_ref, conv_ref, flow_ref = refs[-13:-5]
     gq_ref, gk_ref, gv_ref, arrive_sems, sems = refs[-5:]
-    second = core_ref[0] == 1
+    second = lax.axis_index("ch") == 1
     if last:
         low, high = 0, jnp.where(second, HELD, BLOCKS)
     else:
@@ -456,7 +456,6 @@
     mine = jnp.where(first, lax.pad(decay_rate, zero, below), lax.pad(residue, zero, above))
     other = lax.ppermute(mine, "fsdp", swap)
     vmem = pl.BlockSpec(memory_space=pltpu.VMEM)
-    smem = pl.BlockSpec(memory_space=pltpu.SMEM)
     hbm = pl.BlockSpec(memory_space=pltpu.HBM)
     limit = pltpu.CompilerParams(vmem_limit_bytes=16 << 20)
     packet = (SHARDS, 1, PACKET)
@@ -481,7 +480,7 @@
     )(query_rows, key_rows, value_rows, upstream)
     send, enter_ahead, enter_behind, rates, residues, product, gated = pl.pallas_call(
         summarize_kernel,
-        in_specs=[smem] + [vmem] * 4,
+        in_specs=[vmem] * 4,
         out_specs=[hbm] * 7,
         out_shape=[packets]
         + [pltpu.HBM(state, f32)] * 2
@@ -501,7 +500,7 @@
         ],
         compiler_params=limit,
         name="summarize",
-    )(half.astype(jnp.int32).reshape(1), mine, other, ps, gs)
+    )(mine, other, ps, gs)
     arrived = lax.all_to_all(send, ALL, 0, 0, tiled=True)
 
     lead = jax.ShapeDtypeStruct((STRIPS, ROWS, LANES), f32)
@@ -539,16 +538,15 @@
         (late,) + (lead_rows,) * 6,
     )
     arrived, conv = lax.optimization_barrier((arrived, conv))
-    place = lax.axis_index(ALL).astype(jnp.int32).reshape(1)
     carries = pl.pallas_call(
         carry_kernel,
-        in_specs=[smem] + [vmem] * 2,
+        in_specs=[vmem] * 2,
         out_specs=hbm,
         out_shape=packets,
         scratch_shapes=[pltpu.VMEM(packet, f32), pltpu.SemaphoreType.DMA],
         compiler_params=limit,
         name="carry",
-    )(place, rates, arrived)
+    )(rates, arrived)
     back = lax.all_to_all(carries, ALL, 0, 0, tiled=True)
     flowing, lead_flow, held_flow = inner(gated, enter_behind, True)
     back, flowing = lax.optimization_barrier((back, flowing))
@@ -556,14 +554,13 @@
     count = STRIPS // 2
     rows = lax.dynamic_slice_in_dim(rows, half * count, count, 0).sum(axis=1)
     conv, flowing = in_hbm(conv, flowing)
-    core = lax.axis_index("ch").astype(jnp.int32).reshape(1)
     shapes = [pltpu.HBM((ROWS, WIDTH), bf16)] * 3
 
     def finish(last, leads=(), before=()):
-        count_in = 8 + len(leads)
+        count_in = 7 + len(leads)
         return pl.pallas_call(
             functools.partial(finish_kernel, last),
-            in_specs=[smem, vmem]
+            in_specs=[vmem]
             + [hbm] * 5
             + [vmem] * (1 + len(leads))
             + [hbm] * len(before),
@@ -588,7 +585,7 @@
             ),
             name="finish" if last else "begin",
         )(
-            core, late_tab, key_rows, value_rows, upstream, conv, flowing, back, *leads, *before
+            late_tab, key_rows, value_rows, upstream, conv, flowing, back, *leads, *before
         )
 
     early = finish(False, (*rows_in[3:], held_conv, held_flow))

time: 71.7 us -> 71.7 us (level)
  no operation moved by 1% of the time
where the time goes in v9:
time: 71.7 us; the launch traced here: 71.3 us
  Pallas kernels  27.4 us (38%)
  starting transfers between devices  23.9 us (33%)
  waiting for transfers between devices  17.8 us (25%)
  other arithmetic  1.42 us (2%)
  between operations  0.76 us (1%)
    all_to_all x1, starting transfers between devices, local(): arrived = lax.all_to_all(send, ALL, 0, 0, tiled=True)  14.6 us
    pallas_call x2, Pallas kernels, inner(): pl.pallas_call(functools.partial(inner_kernel, reverse), in_specs=[hbm] *...  11 us
    all_to_all x1, waiting for transfers between devices, local(): arrived = lax.all_to_all(send, ALL, 0, 0, tiled=True)  9.68 us
    all_to_all x1, waiting for transfers between devices, local(): back = lax.all_to_all(carries, ALL, 0, 0, tiled=True)  8.11 us
    pallas_call x2, Pallas kernels, finish(): pl.pallas_call(functools.partial(finish_kernel, last), in_specs=[vmem] +...  7.29 us
    all_to_all x1, starting transfers between devices, local(): back = lax.all_to_all(carries, ALL, 0, 0, tiled=True)  6.59 us
    pallas_call x1, Pallas kernels, local(): pl.pallas_call(summarize_kernel, in_specs=[vmem] * 4, out_specs=[hbm] * 7...  5.23 us
    pallas_call x1, Pallas kernels, local(): pl.pallas_call(prepare_kernel, in_specs=[hbm] * 4, out_specs=[vmem] * 2,...  2.68 us
  transfers between devices with their start and end apart: 4, of which 2 were waited for; matrix products, arithmetic and copies ran while one was open for 0% of the time, Pallas kernels for 24%

profile of v9, /device:TPU:1, one launch (start us, length us, event | category | flops | bytes accessed | tf_op | source)
XLA Modules:
  0.0 71.3 jit_solution(1522245333887177195)
XLA Ops:
  0.6 0.8 %pad_select_fusion.mine_ref = f32[16,256]{1,0:T(8,128)S(1)} fusion(f32[8,256]{1,0:T(8,128)} %param.11, f32[8,256]{1,0:T(8,128)} %param.10, pred[16]{0:T(512)(128)(4,1)S(1)} %iota_compare_fusion), kind=kLoop, calls=%fused_computation.1 | loop fusion | flops 4096 | bytes 32784 | tf_op jit(solution)/shard_map/jit(_where)/select_n | solution.py:456
  1.4 2.5 %collective-permute-start = (f32[16,256]{1,0:T(8,128)S(1)}, f32[16,256]{1,0:T(8,128)S(1)}, u32[]{:S(2)}, u32[]{:S(2)}) collective-permute-start(f32[16,256]{1,0:T(8,128)S(1)} %pad_select_fusion.mine_ref), channel_id=1, source_target_pairs={{0,1},{1,0},{2,3},{3,2},{4,5},{5,4},{6,7},{7,6},{8,9},{9,8},{10,11... | collective-permute-start | bytes 49160 | tf_op jit(solution)/shard_map/ppermute | solution.py:457
  3.9 2.7 %prepare.1 = (f32[4,8,128,128]{3,2,1,0:T(8,128)S(1)}, f32[4,8,128,128]{3,2,1,0:T(8,128)S(1)}) custom-call(bf16[128,4096]{1,0:T(8,128)(2,1)} %q_hbm.1, bf16[128,4096]{1,0:T(8,128)(2,1)} %k_hbm.5, bf16[128,4096]{1,0:T(8,128)(2,1)} %v_hbm.5, bf16[128,4096]{1,0:T(8,128)(2,1)} %u_hbm.5), custom_call_target="tpu_custom_call" | custom-call | flops 4194304 | bytes 12582912 | tf_op jit(solution)/shard_map/prepare/pallas_call | solution.py:471
  6.6 0.0 collective-permute-done.other_ref
  6.6 5.2 %summarize.1 = (f32[128,1,640]{2,1,0:T(1,128)}, f32[4,8,8,8,128]{4,3,2,1,0:T(8,128)}, f32[4,8,8,8,128]{4,3,2,1,0:T(8,128)}, f32[32,128]{1,0:T(8,128)}, f32[32,12...) custom-call(f32[16,256]{1,0:T(8,128)S(1)} %pad_select_fusion.mine_ref, ...), custom_call_target="tpu_custom_call" | custom-call | tf_op jit(solution)/shard_map/summarize/pallas_call | solution.py:481
  11.8 14.6 %all-to-all-start = ((f32[128,1,640]{2,1,0:T(1,128)}), f32[128,1,640]{2,1,0:T(1,128)S(1)}, u32[]{:S(2)}, u32[]{:S(2)}) async-start(f32[128,1,640]{2,1,0:T(1,128)} %get-tuple-element.47), calls=%async_computation | async-start | bytes 655360 | tf_op jit(solution)/shard_map/all_to_all | solution.py:504
  26.5 0.0 copy-start
  26.5 5.3 %ahead.1 = (f32[4,8,128,128]{3,2,1,0:T(8,128)}, f32[4,128,128]{2,1,0:T(8,128)S(1)}, f32[4,128,128]{2,1,0:T(8,128)S(1)}, f32[3,32,8,128]{3,2,1,0:T(8,128)S(1)}, b...) custom-call(f32[32,128]{1,0:T(8,128)} %get-tuple-element.42.rates_hb, ...), custom_call_target="tpu_custom_call" | custom-call | flops 16777216 | bytes 16777216 | tf_op jit(solution)/shard_map/ahead/pallas_call | solution.py:510
  31.7 9.7 %all-to-all-done.x_ref = f32[128,1,640]{2,1,0:T(1,128)S(1)} async-done(((f32[128,1,640]{2,1,0:T(1,128)}), f32[128,1,640]{2,1,0:T(1,128)S(1)}, u32[]{:S(2)}, u32[]{:S(2)}) %all-to-all-start) | async-done | bytes 327712 | tf_op jit(solution)/shard_map/all_to_all | solution.py:504
  41.4 0.0 copy-done
  41.4 1.2 %carry.1 = f32[128,1,640]{2,1,0:T(1,128)} custom-call(f32[32,128]{1,0:T(8,128)S(1)} %copy-done, f32[128,1,640]{2,1,0:T(1,128)S(1)} %all-to-all-done.x_ref), custom_call_target="tpu_custom_call" | custom-call | tf_op jit(solution)/shard_map/carry/pallas_call | solution.py:541
  42.6 6.6 %all-to-all-start.1 = ((f32[128,1,640]{2,1,0:T(1,128)}), f32[128,1,640]{2,1,0:T(1,128)S(1)}, u32[]{:S(2)}, u32[]{:S(2)}) async-start(f32[128,1,640]{2,1,0:T(1,128)} %carry.1), calls=%async_computation.1 | async-start | bytes 655360 | tf_op jit(solution)/shard_map/all_to_all | solution.py:550
  49.2 5.8 %behind.1 = (f32[4,8,128,128]{3,2,1,0:T(8,128)}, f32[4,128,128]{2,1,0:T(8,128)S(1)}, f32[4,128,128]{2,1,0:T(8,128)S(1)}) custom-call(f32[32,128]{1,0:T(8,128)} %get-tuple-element.42.rates_hbm.rates_ref, f32[32,128]{1,0:T(8,128)} %get-tuple-element.43.residues_hbm, f32[4,8,128,128]{3,2,1,0:T(8,128)} %get-tuple-element.51.xs_hbm, ...), custom_call_target="tpu_custom_call" | custom-call | flops 16777216 | bytes 16777216 | tf_op jit(solution)/shard_map/behind/pallas_call | solution.py:510
  55.0 8.1 %all-to-all-done.1.in_ref = f32[128,1,640]{2,1,0:T(1,128)S(1)} async-done(((f32[128,1,640]{2,1,0:T(1,128)}), f32[128,1,640]{2,1,0:T(1,128)S(1)}, u32[]{:S(2)}, u32[]{:S(2)}) %all-to-all-start.1) | async-done | bytes 327712 | tf_op jit(solution)/shard_map/all_to_all | solution.py:550
  63.2 4.1 %begin.1 = (bf16[128,4096]{1,0:T(8,128)(2,1)}, bf16[128,4096]{1,0:T(8,128)(2,1)}, bf16[128,4096]{1,0:T(8,128)(2,1)}) custom-call(f32[3,32,8,128]{3,2,1,0:T(8,128)S(1)} %get-tuple-element.46.tab, bf16[128,4096]{1,0:T(8,128)(2,1)} %k_hbm.5, bf16[128,4096]{1,0:T(8,128)(2,1)} %v_hbm.5, bf16[128,4096]{1,0:T(8,128)(2,1)} %u_hbm.5, ...), custom_call_target="tpu_custom_call" | custom-call | flops 16777216 | bytes 10485760 | tf_op jit(solution)/shard_map/begin/pallas_call | solution.py:561
  67.2 0.2 collective-permute-start.1
  67.4 0.0 copy-start.1
  67.4 3.2 %finish.1 = (bf16[128,4096]{1,0:T(8,128)(2,1)}, bf16[128,4096]{1,0:T(8,128)(2,1)}, bf16[128,4096]{1,0:T(8,128)(2,1)}) custom-call(f32[3,32,8,128]{3,2,1,0:T(8,128)S(1)} %get-tuple-element.46.tab, bf16[128,4096]{1,0:T(8,128)(2,1)} %k_hbm.5, bf16[128,4096]{1,0:T(8,128)(2,1)} %v_hbm.5, ...), custom_call_target="tpu_custom_call", output_to_operand_aliasing={{0}: (12, {}), {1}: (13, {}), {2}: (14, {})} | custom-call | flops 16777216 | bytes 10485760 | tf_op jit(solution)/shard_map/finish/pallas_call | solution.py:561
  70.7 0.0 collective-permute-done.1
  70.7 0.0 copy-done.1
  70.7 0.6 fusion
  (3 shorter events, 0.1 us)
Async XLA Ops:
  1.4 5.2 %collective-permute-start = (f32[16,256]{1,0:T(8,128)S(1)}, f32[16,256]{1,0:T(8,128)S(1)}, u32[]{:S(2)}, u32[]{:S(2)}) collective-permute-start(f32[16,256]{1,0:T(8,128)S(1)} %pad_select_fusion.mine_ref), channel_id=1, source_target_pairs={{0,1},{1,0},{2,3},{3,2},{4,5},{5,4},{6,7},{7,6},{8,9},{9,8},{10,11... | collective-permute-start | bytes 49160 | tf_op jit(solution)/shard_map/ppermute | solution.py:457
  11.8 29.6 %all-to-all-start = ((f32[128,1,640]{2,1,0:T(1,128)}), f32[128,1,640]{2,1,0:T(1,128)S(1)}, u32[]{:S(2)}, u32[]{:S(2)}) async-start(f32[128,1,640]{2,1,0:T(1,128)} %get-tuple-element.47), calls=%async_computation | async-start | bytes 655360 | tf_op jit(solution)/shard_map/all_to_all | solution.py:504
  26.5 15.0 %copy-start = (f32[32,128]{1,0:T(8,128)S(1)}, f32[32,128]{1,0:T(8,128)}, u32[]{:S(2)}) copy-start(f32[32,128]{1,0:T(8,128)} %get-tuple-element.42.rates_hbm.rates_ref) | copy-start | bytes 49156
  42.6 20.5 %all-to-all-start.1 = ((f32[128,1,640]{2,1,0:T(1,128)}), f32[128,1,640]{2,1,0:T(1,128)S(1)}, u32[]{:S(2)}, u32[]{:S(2)}) async-start(f32[128,1,640]{2,1,0:T(1,128)} %carry.1), calls=%async_computation.1 | async-start | bytes 655360 | tf_op jit(solution)/shard_map/all_to_all | solution.py:550
  67.2 3.4 %collective-permute-start.1 = (f32[2,8,128]{2,1,0:T(8,128)S(1)}, f32[2,8,128]{2,1,0:T(8,128)S(1)}, u32[]{:S(2)}, u32[]{:S(2)}) collective-permute-start(f32[2,8,128]{2,1,0:T(8,128)S(1)} %dynamic-slice_reduce_fusion), channel_id=1, source_target_pairs={{0,2},{2,0},{1,3},{3,1},{4,6},{6,4},{5,7},{7,5},{8,10},{10,8},{9,1... | collective-permute-start | bytes 24584 | tf_op jit(solution)/shard_map/ppermute | solution.py:593
  67.4 3.3 %copy-start.1 = (f32[8,256]{1,0:T(8,128)S(1)}, f32[8,256]{1,0:T(8,128)}, u32[]{:S(2)}) copy-start(f32[8,256]{1,0:T(8,128)} %param.10) | copy-start | bytes 24580

commit v10 on v8

--- a/solution.py
+++ b/solution.py
@@ -22,7 +22,7 @@
 WIDTH = BLOCKS * FILTERS
 SHARDS = TOKENS // ROWS
 PACKET = 5 * LANES
-HELD = 3
+HELD = 4
 ALL = ("ctx", "fsdp")
 f32 = jnp.float32
 bf16 = jnp.bfloat16

time: 71.7 us -> 72 us (level)
  no operation moved by 1% of the time
where the time goes in v10:
time: 72 us; the launch traced here: 71.7 us
  Pallas kernels  27.4 us (38%)
  starting transfers between devices  24.3 us (34%)
  waiting for transfers between devices  17.8 us (25%)
  other arithmetic  1.42 us (2%)
  between operations  0.77 us (1%)
    all_to_all x1, starting transfers between devices, local(): arrived = lax.all_to_all(send, ALL, 0, 0, tiled=True)  14.6 us
    pallas_call x2, Pallas kernels, inner(): pl.pallas_call(functools.partial(inner_kernel, reverse), in_specs=[hbm] *...  11 us
    all_to_all x1, waiting for transfers between devices, local(): arrived = lax.all_to_all(send, ALL, 0, 0, tiled=True)  9.66 us
    all_to_all x1, waiting for transfers between devices, local(): back = lax.all_to_all(carries, ALL, 0, 0, tiled=True)  8.11 us
    pallas_call x2, Pallas kernels, finish(): pl.pallas_call(functools.partial(finish_kernel, last), in_specs=[smem, vm...  7.3 us
    all_to_all x1, starting transfers between devices, local(): back = lax.all_to_all(carries, ALL, 0, 0, tiled=True)  6.61 us
    pallas_call x1, Pallas kernels, local(): pl.pallas_call(summarize_kernel, in_specs=[smem] + [vmem] * 4, out_specs=...  5.22 us
    pallas_call x1, Pallas kernels, local(): pl.pallas_call(prepare_kernel, in_specs=[hbm] * 4, out_specs=[vmem] * 2,...  2.68 us
  transfers between devices with their start and end apart: 4, of which 2 were waited for; matrix products, arithmetic and copies ran while one was open for 0% of the time, Pallas kernels for 24%

profile of v10, /device:TPU:1, one launch (start us, length us, event | category | flops | bytes accessed | tf_op | source)
XLA Modules:
  0.0 71.7 jit_solution(10501778789927003155)
XLA Ops:
  0.6 0.8 %pad_select_fusion.mine_ref = f32[16,256]{1,0:T(8,128)S(1)} fusion(f32[8,256]{1,0:T(8,128)} %param.11, f32[8,256]{1,0:T(8,128)} %param.10, pred[16]{0:T(512)(128)(4,1)S(1)} %iota_compare_fusion), kind=kLoop, calls=%fused_computation.1 | loop fusion | flops 4096 | bytes 32784 | tf_op jit(solution)/shard_map/jit(_where)/select_n | solution.py:456
  1.4 2.5 %collective-permute-start = (f32[16,256]{1,0:T(8,128)S(1)}, f32[16,256]{1,0:T(8,128)S(1)}, u32[]{:S(2)}, u32[]{:S(2)}) collective-permute-start(f32[16,256]{1,0:T(8,128)S(1)} %pad_select_fusion.mine_ref), channel_id=1, source_target_pairs={{0,1},{1,0},{2,3},{3,2},{4,5},{5,4},{6,7},{7,6},{8,9},{9,8},{10,11... | collective-permute-start | bytes 49160 | tf_op jit(solution)/shard_map/ppermute | solution.py:457
  3.9 2.7 %prepare.1 = (f32[4,8,128,128]{3,2,1,0:T(8,128)S(1)}, f32[4,8,128,128]{3,2,1,0:T(8,128)S(1)}) custom-call(bf16[128,4096]{1,0:T(8,128)(2,1)} %q_hbm.1, bf16[128,4096]{1,0:T(8,128)(2,1)} %k_hbm.5, bf16[128,4096]{1,0:T(8,128)(2,1)} %v_hbm.5, bf16[128,4096]{1,0:T(8,128)(2,1)} %u_hbm.5), custom_call_target="tpu_custom_call" | custom-call | flops 4194304 | bytes 12582912 | tf_op jit(solution)/shard_map/prepare/pallas_call | solution.py:472
  6.6 0.0 collective-permute-done.other_ref
  6.6 5.2 %summarize.1 = (f32[128,1,640]{2,1,0:T(1,128)}, f32[4,8,8,8,128]{4,3,2,1,0:T(8,128)}, f32[4,8,8,8,128]{4,3,2,1,0:T(8,128)}, f32[32,128]{1,0:T(8,128)}, f32[32,12...) custom-call(s32[1]{0:T(128)} %bitcast.1.half_ref, f32[16,256]{1,0:T(8,128)S(1)} %pad_select_fusion.mine_ref, ...), custom_call_target="tpu_custom_call" | custom-call | tf_op jit(solution)/shard_map/summarize/pallas_call | solution.py:482
  11.8 14.6 %all-to-all-start = ((f32[128,1,640]{2,1,0:T(1,128)}), f32[128,1,640]{2,1,0:T(1,128)S(1)}, u32[]{:S(2)}, u32[]{:S(2)}) async-start(f32[128,1,640]{2,1,0:T(1,128)} %get-tuple-element.47), calls=%async_computation | async-start | bytes 655360 | tf_op jit(solution)/shard_map/all_to_all | solution.py:505
  26.5 0.0 copy-start
  26.5 5.3 %ahead.1 = (f32[4,8,128,128]{3,2,1,0:T(8,128)}, f32[4,128,128]{2,1,0:T(8,128)S(1)}, f32[4,128,128]{2,1,0:T(8,128)S(1)}, f32[3,32,8,128]{3,2,1,0:T(8,128)S(1)}, b...) custom-call(f32[32,128]{1,0:T(8,128)} %get-tuple-element.42.rates_hb, ...), custom_call_target="tpu_custom_call" | custom-call | flops 16777216 | bytes 16777216 | tf_op jit(solution)/shard_map/ahead/pallas_call | solution.py:511
  31.7 9.7 %all-to-all-done.x_ref = f32[128,1,640]{2,1,0:T(1,128)S(1)} async-done(((f32[128,1,640]{2,1,0:T(1,128)}), f32[128,1,640]{2,1,0:T(1,128)S(1)}, u32[]{:S(2)}, u32[]{:S(2)}) %all-to-all-start) | async-done | bytes 327712 | tf_op jit(solution)/shard_map/all_to_all | solution.py:505
  41.4 0.0 copy-done
  41.4 1.2 %carry.1 = f32[128,1,640]{2,1,0:T(1,128)} custom-call(s32[1]{0:T(128)} %bitcast.2.where_ref, f32[32,128]{1,0:T(8,128)S(1)} %copy-done, f32[128,1,640]{2,1,0:T(1,128)S(1)} %all-to-all-done.x_ref), custom_call_target="tpu_custom_call" | custom-call | tf_op jit(solution)/shard_map/carry/pallas_call | solution.py:543
  42.6 6.6 %all-to-all-start.1 = ((f32[128,1,640]{2,1,0:T(1,128)}), f32[128,1,640]{2,1,0:T(1,128)S(1)}, u32[]{:S(2)}, u32[]{:S(2)}) async-start(f32[128,1,640]{2,1,0:T(1,128)} %carry.1), calls=%async_computation.1 | async-start | bytes 655360 | tf_op jit(solution)/shard_map/all_to_all | solution.py:552
  49.2 5.8 %behind.1 = (f32[4,8,128,128]{3,2,1,0:T(8,128)}, f32[4,128,128]{2,1,0:T(8,128)S(1)}, f32[4,128,128]{2,1,0:T(8,128)S(1)}) custom-call(f32[32,128]{1,0:T(8,128)} %get-tuple-element.42.rates_hbm.rates_ref, f32[32,128]{1,0:T(8,128)} %get-tuple-element.43.residues_hbm, f32[4,8,128,128]{3,2,1,0:T(8,128)} %get-tuple-element.51.xs_hbm, ...), custom_call_target="tpu_custom_call" | custom-call | flops 16777216 | bytes 16777216 | tf_op jit(solution)/shard_map/behind/pallas_call | solution.py:511
  55.0 8.1 %all-to-all-done.1.in_ref = f32[128,1,640]{2,1,0:T(1,128)S(1)} async-done(((f32[128,1,640]{2,1,0:T(1,128)}), f32[128,1,640]{2,1,0:T(1,128)S(1)}, u32[]{:S(2)}, u32[]{:S(2)}) %all-to-all-start.1) | async-done | bytes 327712 | tf_op jit(solution)/shard_map/all_to_all | solution.py:552
  63.2 3.7 %begin.1 = (bf16[128,4096]{1,0:T(8,128)(2,1)}, bf16[128,4096]{1,0:T(8,128)(2,1)}, bf16[128,4096]{1,0:T(8,128)(2,1)}) custom-call(s32[1]{0:T(128)} %bitcast.core_ref, f32[3,32,8,128]{3,2,1,0:T(8,128)S(1)} %get-tuple-element.46.tab, bf16[128,4096]{1,0:T(8,128)(2,1)} %k_hbm.5, bf16[128,4096]{1,0:T(8,128)(2,1)} %v_hbm.5, bf16[128,4096]{1,0:T(8,128)(2,1)} %u_hbm.5, ...), custom_call_target="tpu_custom_call" | custom-call | flops 16777216 | bytes 10485760 | tf_op jit(solution)/shard_map/begin/pallas_call | solution.py:564
  66.8 0.6 collective-permute-start.1
  67.4 0.0 copy-start.1
  67.4 3.6 %finish.1 = (bf16[128,4096]{1,0:T(8,128)(2,1)}, bf16[128,4096]{1,0:T(8,128)(2,1)}, bf16[128,4096]{1,0:T(8,128)(2,1)}) custom-call(s32[1]{0:T(128)} %bitcast.core_ref, f32[3,32,8,128]{3,2,1,0:T(8,128)S(1)} %get-tuple-element.46.tab, bf16[128,4096]{1,0:T(8,128)(2,1)} %k_hbm.5, ...), custom_call_target="tpu_custom_call", output_to_operand_aliasing={{0}: (13, {}), {1}: (14, {}), {2}: (15, {})} | custom-call | flops 16777216 | bytes 10485760 | tf_op jit(solution)/shard_map/finish/pallas_call | solution.py:564
  71.1 0.0 collective-permute-done.1
  71.1 0.0 copy-done.1
  71.1 0.6 fusion
  (3 shorter events, 0.1 us)
Async XLA Ops:
  1.4 5.2 %collective-permute-start = (f32[16,256]{1,0:T(8,128)S(1)}, f32[16,256]{1,0:T(8,128)S(1)}, u32[]{:S(2)}, u32[]{:S(2)}) collective-permute-start(f32[16,256]{1,0:T(8,128)S(1)} %pad_select_fusion.mine_ref), channel_id=1, source_target_pairs={{0,1},{1,0},{2,3},{3,2},{4,5},{5,4},{6,7},{7,6},{8,9},{9,8},{10,11... | collective-permute-start | bytes 49160 | tf_op jit(solution)/shard_map/ppermute | solution.py:457
  11.8 29.6 %all-to-all-start = ((f32[128,1,640]{2,1,0:T(1,128)}), f32[128,1,640]{2,1,0:T(1,128)S(1)}, u32[]{:S(2)}, u32[]{:S(2)}) async-start(f32[128,1,640]{2,1,0:T(1,128)} %get-tuple-element.47), calls=%async_computation | async-start | bytes 655360 | tf_op jit(solution)/shard_map/all_to_all | solution.py:505
  26.5 14.9 %copy-start = (f32[32,128]{1,0:T(8,128)S(1)}, f32[32,128]{1,0:T(8,128)}, u32[]{:S(2)}) copy-start(f32[32,128]{1,0:T(8,128)} %get-tuple-element.42.rates_hbm.rates_ref) | copy-start | bytes 49156
  42.6 20.5 %all-to-all-start.1 = ((f32[128,1,640]{2,1,0:T(1,128)}), f32[128,1,640]{2,1,0:T(1,128)S(1)}, u32[]{:S(2)}, u32[]{:S(2)}) async-start(f32[128,1,640]{2,1,0:T(1,128)} %carry.1), calls=%async_computation.1 | async-start | bytes 655360 | tf_op jit(solution)/shard_map/all_to_all | solution.py:552
  66.8 4.2 %collective-permute-start.1 = (f32[2,8,128]{2,1,0:T(8,128)S(1)}, f32[2,8,128]{2,1,0:T(8,128)S(1)}, u32[]{:S(2)}, u32[]{:S(2)}) collective-permute-start(f32[2,8,128]{2,1,0:T(8,128)S(1)} %dynamic-slice_reduce_fusion), channel_id=1, source_target_pairs={{0,2},{2,0},{1,3},{3,1},{4,6},{6,4},{5,7},{7,5},{8,10},{10,8},{9,1... | collective-permute-start | bytes 24584 | tf_op jit(solution)/shard_map/ppermute | solution.py:596
  67.4 3.7 %copy-start.1 = (f32[8,256]{1,0:T(8,128)S(1)}, f32[8,256]{1,0:T(8,128)}, u32[]{:S(2)}) copy-start(f32[8,256]{1,0:T(8,128)} %param.10) | copy-start | bytes 24580
